TPU v7x, 128 devices: a whole 4x4x4 slice. The times are simulated.
128 devices in a mesh: shard: 8 (over y_lo, z), ctx: 8 (over y_hi, x), tp: 2 (over core).
Axes of the slice: x: 4, y: 4 (y_hi: 2, y_lo: 2; y = y_hi * 2 + y_lo), z: 4, core: 2. Of those that a mesh axis runs over, the one named last changes fastest.
Arguments:
- tokens: bfloat16 [8, 2048, 2048], P('shard', 'ctx'), may hold values from -6 to 6
- cotangent: bfloat16 [8, 2048, 2048], P('shard', 'ctx'), may hold values from -6 to 6
- seq_ids: int32 [8, 2048], P('shard'), may hold values from 0 to 1, as said below
- block_ids: int32 [8, 2048], P('shard'), may hold values from 0 to 7, as said below
- keep_layer: int32 [8], P('shard'), may hold values from 0 to 1, as said below
- gain_attn: float32 [2048], replicated, may hold values from 0.25 to 1.75
- gain_ffn: float32 [2048], replicated, may hold values from 0.25 to 1.75
- w_query: float32 [2048, 2048], P('shard', 'tp'), may hold values from -0.125 to 0.125
- w_key: float32 [2048, 512], P('shard', 'tp'), may hold values from -0.125 to 0.125
- w_value: float32 [2048, 512], P('shard', 'tp'), may hold values from -0.125 to 0.125
- w_out: float32 [2048, 2048], P('shard', 'tp'), may hold values from -0.75 to 0.75
- w_gate: float32 [2048, 5632], P('shard', 'tp'), may hold values from -0.125 to 0.125
- w_up: float32 [2048, 5632], P('shard', 'tp'), may hold values from -0.125 to 0.125
- w_down: float32 [2048, 5632], P('shard', 'tp'), may hold values from -0.078125 to 0.078125
Outputs:
- output: bfloat16 [8, 2048, 2048], P('shard', 'ctx')
- input_grad: bfloat16 [8, 2048, 2048], P('shard', 'ctx')
- grad_gain_attn: float32 [2048], P('shard')
- grad_gain_ffn: float32 [2048], P('shard')
- grad_query: float32 [2048, 2048], P('shard', 'tp')
- grad_key: float32 [2048, 512], P('shard', 'tp')
- grad_value: float32 [2048, 512], P('shard', 'tp')
- grad_out: float32 [2048, 2048], P('shard', 'tp')
- grad_gate: float32 [2048, 5632], P('shard', 'tp')
- grad_up: float32 [2048, 5632], P('shard', 'tp')
- grad_down: float32 [2048, 5632], P('shard', 'tp')
Inputs may be any that keep to these rules, and one draw needn't show every extreme that they name: `seq_ids`: each sample holds exactly two documents: id 0 on a leading run of fewer than min(256, 256) positions, id 1 on the rest. Blocks of 256 positions are counted from each document's start: block_ids[p] = (p - start of p's document) // 256. `keep_layer`: at least one sample runs the layer and at least one skips it.
All inputs are finite; a program needn't handle non-finite values.
Results may differ from a plain program's by a relative error of at most 0.02.
Values may be sent and summed in bfloat16 or wider, within the bound.
No kernel may reach another device: no remote copies, remote signals or barrier semaphores. Data moves between devices by JAX's collectives and lax.ppermute only.
A program may use at most 256 MiB of HBM per device.

v0:
```python
import jax
import jax.numpy as jnp
from jax import lax
from jax.sharding import PartitionSpec as P

HD = 128


EPS = 1e-05
NEG = -1e30


def to_half(value):
    return value.astype(jnp.bfloat16)


def contract_rows(left, right):
    return lax.dot_general(
        left, right, (((0,), (0,)), ((), ())), preferred_element_type=jnp.float32
    )


def contract_cols(left, right):
    return lax.dot_general(
        left, right, (((1,), (1,)), ((), ())), preferred_element_type=jnp.float32
    )


def rope_tables(positions):
    freqs = 10000.0 ** (-(jnp.arange(HD // 2).astype(jnp.float32) * 2.0 / HD))
    angle = positions[:, None] * freqs[None, :]
    cosine = jnp.concatenate([jnp.cos(angle), jnp.cos(angle)], axis=-1)
    sine = jnp.concatenate([jnp.sin(angle), jnp.sin(angle)], axis=-1)
    return (cosine, sine)


def rotate(value, cosine, sine):
    half = value.shape[-1] // 2
    turned = jnp.concatenate([-value[..., half:], value[..., :half]], axis=-1)
    return value * cosine[:, None, :] + turned * sine[:, None, :]


def unrotate(grad, cosine, sine):
    half = grad.shape[-1] // 2
    scaled = grad * sine[:, None, :]
    return grad * cosine[:, None, :] + jnp.concatenate(
        [scaled[..., half:], -scaled[..., :half]], axis=-1
    )


def norm_backward(value, inv_root, gain, grad_norm):
    scaled = gain * grad_norm
    grad_value = inv_root * scaled - value * inv_root**3 * jnp.mean(
        scaled * value, axis=-1, keepdims=True
    )
    grad_gain = jnp.sum(grad_norm * value * inv_root, axis=0)
    return (grad_value, grad_gain)


def per_device(
    tokens,
    cotangent,
    seq_ids,
    block_ids,
    keep_layer,
    gain_attn,
    gain_ffn,
    w_query,
    w_key,
    w_value,
    w_out,
    w_gate,
    w_up,
    w_down,
):
    tok_count = tokens.shape[1]
    q_start = lax.axis_index("ctx") * tok_count
    seg_all = seq_ids[0]
    blk_all = block_ids[0]
    seg_query = lax.dynamic_slice_in_dim(seg_all, q_start, tok_count)
    blk_query = lax.dynamic_slice_in_dim(blk_all, q_start, tok_count)
    keep_flag = keep_layer[0].astype(jnp.float32)
    heads_local = w_query.shape[1] // HD
    kv_local = w_key.shape[1] // HD
    group_size = heads_local // kv_local
    score_scale = HD ** (-0.5)
    cosine, sine = rope_tables((q_start + jnp.arange(tok_count)).astype(jnp.float32))
    full_query, full_key, full_value, full_out, full_gate, full_up, full_down = (
        lax.all_gather(to_half(w_query), "shard", axis=0, tiled=True),
        lax.all_gather(to_half(w_key), "shard", axis=0, tiled=True),
        lax.all_gather(to_half(w_value), "shard", axis=0, tiled=True),
        lax.all_gather(to_half(w_out), "shard", axis=0, tiled=True),
        lax.all_gather(to_half(w_gate), "shard", axis=0, tiled=True),
        lax.all_gather(to_half(w_up), "shard", axis=0, tiled=True),
        lax.all_gather(to_half(w_down), "shard", axis=0, tiled=True),
    )
    xval = tokens[0].astype(jnp.float32)
    root_attn = lax.rsqrt(jnp.mean(xval * xval, axis=-1, keepdims=True) + EPS)
    normed_attn = to_half(xval * root_attn * gain_attn)
    query_pre = jnp.dot(normed_attn, full_query, preferred_element_type=jnp.float32)
    key_pre = jnp.dot(normed_attn, full_key, preferred_element_type=jnp.float32)
    values = to_half(jnp.dot(normed_attn, full_value, preferred_element_type=jnp.float32))
    query = to_half(rotate(query_pre.reshape(tok_count, heads_local, HD), cosine, sine))
    query_g = query.reshape(tok_count, kv_local, group_size, HD).transpose(1, 2, 0, 3)
    keys = to_half(rotate(key_pre.reshape(tok_count, kv_local, HD), cosine, sine)).reshape(
        tok_count, kv_local * HD
    )

    def visible():
        allowed = (seg_query[:, None] == seg_all[None, :]) & (
            blk_all[None, :] <= blk_query[:, None]
        )
        return allowed[None, None]

    def piece_scores(key_piece):
        count = key_piece.shape[0]
        keys3 = key_piece.reshape(count, kv_local, HD)
        raw = (
            jnp.einsum("grtd,ngd->grtn", query_g, keys3, preferred_element_type=jnp.float32)
            * score_scale
        )
        allowed = visible()
        return (jnp.where(allowed, raw, NEG), allowed, keys3)

    run_max = jnp.full((kv_local, group_size, tok_count), NEG, jnp.float32)
    key_piece = lax.all_gather(keys, "ctx", axis=0, tiled=True)
    value_piece = lax.all_gather(values, "ctx", axis=0, tiled=True)
    count = key_piece.shape[0]
    safe, allowed, keys3 = piece_scores(key_piece)
    new_max = jnp.maximum(run_max, jnp.max(safe, axis=-1))
    weights = jnp.where(allowed, jnp.exp(safe - new_max[..., None]), 0.0)
    values3 = value_piece.reshape(count, kv_local, HD)
    added = jnp.einsum(
        "grtn,ngd->grtd", to_half(weights), values3, preferred_element_type=jnp.float32
    )
    run_total = jnp.sum(weights, axis=-1)
    heads_f = added / run_total[..., None]
    log_total = new_max + jnp.log(run_total)
    heads = to_half(heads_f.transpose(2, 0, 1, 3).reshape(tok_count, heads_local * HD))
    attn_branch = lax.psum(contract_cols(heads, full_out).astype(jnp.bfloat16), "tp").astype(
        jnp.float32
    )
    middle = xval + keep_flag * attn_branch
    root_ffn = lax.rsqrt(jnp.mean(middle * middle, axis=-1, keepdims=True) + EPS)
    normed_ffn = to_half(middle * root_ffn * gain_ffn)
    gate = jnp.dot(normed_ffn, full_gate, preferred_element_type=jnp.float32)
    up_val = jnp.dot(normed_ffn, full_up, preferred_element_type=jnp.float32)
    sig_gate = jax.nn.sigmoid(gate)
    silu_gate = gate * sig_gate
    hidden = to_half(silu_gate * up_val)
    ffn_branch = lax.psum(contract_cols(hidden, full_down).astype(jnp.bfloat16), "tp").astype(
        jnp.float32
    )
    output = to_half(middle + keep_flag * ffn_branch)
    back_query, back_key, back_value, back_out = (full_query, full_key, full_value, full_out)
    back_gate, back_up, back_down = (full_gate, full_up, full_down)
    grad_top = cotangent[0].astype(jnp.float32)
    d_ffn = to_half(keep_flag * grad_top)
    d_hidden = jnp.dot(d_ffn, back_down, preferred_element_type=jnp.float32)
    d_gate = to_half(d_hidden * up_val * sig_gate * (1.0 + gate * (1.0 - sig_gate)))
    d_up = to_half(d_hidden * silu_gate)
    d_normed_ffn = lax.psum(
        (contract_cols(d_gate, back_gate) + contract_cols(d_up, back_up)).astype(jnp.bfloat16), "tp"
    ).astype(jnp.float32)
    mid_part, gain_ffn_local = norm_backward(middle, root_ffn, gain_ffn, d_normed_ffn)
    d_middle = grad_top + mid_part
    d_attn = to_half(keep_flag * d_middle)
    d_heads = to_half(jnp.dot(d_attn, back_out, preferred_element_type=jnp.float32))
    d_heads_g = d_heads.reshape(tok_count, kv_local, group_size, HD).transpose(1, 2, 0, 3)
    row_delta = jnp.sum(d_heads_g.astype(jnp.float32) * heads_f, axis=-1)
    key_piece = lax.all_gather(keys, "ctx", axis=0, tiled=True)
    value_piece = lax.all_gather(values, "ctx", axis=0, tiled=True)
    count = key_piece.shape[0]
    safe, allowed, keys3 = piece_scores(key_piece)
    probs = jnp.where(allowed, jnp.exp(safe - log_total[..., None]), 0.0)
    values3 = value_piece.reshape(count, kv_local, HD)
    d_probs = jnp.einsum("grtd,ngd->grtn", d_heads_g, values3, preferred_element_type=jnp.float32)
    d_scores = to_half(score_scale * probs * (d_probs - row_delta[..., None]))
    grad_q = jnp.einsum("grtn,ngd->grtd", d_scores, keys3, preferred_element_type=jnp.float32)
    key_part = jnp.einsum("grtn,grtd->ngd", d_scores, query_g, preferred_element_type=jnp.float32)
    value_part = jnp.einsum(
        "grtn,grtd->ngd", to_half(probs), d_heads_g, preferred_element_type=jnp.float32
    )
    rows = jnp.concatenate(
        [key_part.reshape(count, kv_local * HD), value_part.reshape(count, kv_local * HD)], axis=1
    )
    grad_kv = lax.psum_scatter(
        rows.astype(jnp.bfloat16), "ctx", scatter_dimension=0, tiled=True
    ).astype(jnp.float32)
    d_key = to_half(
        unrotate(grad_kv[:, : kv_local * HD].reshape(tok_count, kv_local, HD), cosine, sine)
    ).reshape(tok_count, kv_local * HD)
    d_values = to_half(grad_kv[:, kv_local * HD :])
    d_query = to_half(
        unrotate(grad_q.transpose(2, 0, 1, 3).reshape(tok_count, heads_local, HD), cosine, sine)
    ).reshape(tok_count, heads_local * HD)
    d_normed_attn = lax.psum(
        (
            contract_cols(d_query, back_query)
            + contract_cols(d_key, back_key)
            + contract_cols(d_values, back_value)
        ).astype(jnp.bfloat16),
        "tp",
    ).astype(jnp.float32)
    input_part, gain_attn_local = norm_backward(xval, root_attn, gain_attn, d_normed_attn)
    input_grad = to_half(d_middle + input_part)
    grad_query_local = contract_rows(normed_attn, d_query)
    grad_key_local = contract_rows(normed_attn, d_key)
    grad_value_local = contract_rows(normed_attn, d_values)
    grad_out_local = contract_rows(d_attn, heads)
    grad_gate_local = contract_rows(normed_ffn, d_gate)
    grad_up_local = contract_rows(normed_ffn, d_up)
    grad_down_local = contract_rows(d_ffn, hidden)
    own_ga, own_gf, own_q, own_k, own_v, own_o, own_g, own_u, own_d = (
        lax.psum_scatter(gain_attn_local, ("shard", "ctx"), scatter_dimension=0, tiled=True),
        lax.psum_scatter(gain_ffn_local, ("shard", "ctx"), scatter_dimension=0, tiled=True),
        lax.psum_scatter(grad_query_local, ("shard", "ctx"), scatter_dimension=0, tiled=True),
        lax.psum_scatter(grad_key_local, ("shard", "ctx"), scatter_dimension=0, tiled=True),
        lax.psum_scatter(grad_value_local, ("shard", "ctx"), scatter_dimension=0, tiled=True),
        lax.psum_scatter(grad_out_local, ("shard", "ctx"), scatter_dimension=0, tiled=True),
        lax.psum_scatter(grad_gate_local, ("shard", "ctx"), scatter_dimension=0, tiled=True),
        lax.psum_scatter(grad_up_local, ("shard", "ctx"), scatter_dimension=0, tiled=True),
        lax.psum_scatter(grad_down_local, ("shard", "ctx"), scatter_dimension=0, tiled=True),
    )
    sum_ga, sum_gf, sum_q, sum_k, sum_v, sum_o, sum_g, sum_u, sum_d = (
        lax.all_gather(own_ga.astype(jnp.bfloat16), "ctx", axis=0, tiled=True).astype(own_ga.dtype),
        lax.all_gather(own_gf.astype(jnp.bfloat16), "ctx", axis=0, tiled=True).astype(own_gf.dtype),
        lax.all_gather(own_q.astype(jnp.bfloat16), "ctx", axis=0, tiled=True).astype(own_q.dtype),
        lax.all_gather(own_k.astype(jnp.bfloat16), "ctx", axis=0, tiled=True).astype(own_k.dtype),
        lax.all_gather(own_v.astype(jnp.bfloat16), "ctx", axis=0, tiled=True).astype(own_v.dtype),
        lax.all_gather(own_o.astype(jnp.bfloat16), "ctx", axis=0, tiled=True).astype(own_o.dtype),
        lax.all_gather(own_g.astype(jnp.bfloat16), "ctx", axis=0, tiled=True).astype(own_g.dtype),
        lax.all_gather(own_u.astype(jnp.bfloat16), "ctx", axis=0, tiled=True).astype(own_u.dtype),
        lax.all_gather(own_d.astype(jnp.bfloat16), "ctx", axis=0, tiled=True).astype(own_d.dtype),
    )
    return (
        output[None],
        input_grad[None],
        sum_ga,
        sum_gf,
        sum_q,
        sum_k,
        sum_v,
        sum_o,
        sum_g,
        sum_u,
        sum_d,
    )


def solution(mesh):
    placed = (
        P("shard", "ctx", None),
        P("shard", "ctx", None),
        P("shard", None),
        P("shard", None),
        P("shard"),
        P(),
        P(),
        P("shard", "tp"),
        P("shard", "tp"),
        P("shard", "tp"),
        P("shard", "tp"),
        P("shard", "tp"),
        P("shard", "tp"),
        P("shard", "tp"),
    )
    return jax.shard_map(
        per_device,
        mesh=mesh,
        in_specs=placed,
        out_specs=(
            P("shard", "ctx", None),
            P("shard", "ctx", None),
            P("shard"),
            P("shard"),
            P("shard", "tp"),
            P("shard", "tp"),
            P("shard", "tp"),
            P("shard", "tp"),
            P("shard", "tp"),
            P("shard", "tp"),
            P("shard", "tp"),
        ),
        check_vma=False,
    )
```

profile of v0, /device:TPU:97, one launch (start us, length us, event | category | flops | bytes accessed | tf_op | source)
XLA Modules:
  0.0 3692.0 jit_solution(15048867028550153105)
XLA Ops:
  12.9 30.6 all-gather.19.cloned.1.call-done
  43.4 2.4 convolution_convert_fusion.3
  47.2 36.6 all-gather.15.cloned.1.call-done
  83.9 2.3 copy.42
  90.4 49.2 %all-gather.21.cloned.1.call-done = bf16[2048,256]{1,0:T(8,128)(2,1)} async-done(((bf16[256,256]{1,0:T(8,128)(2,1)}), bf16[2048,256]{1,0:T(8,128)(2,1)}) %all-gather.21.cloned.1.call-update) | async-done | bytes 1048592 | tf_op jit(solution)/shard_map/all_gather | solution.py:127
  139.6 2.1 reshape.261
  141.7 49.5 %all-gather.13.cloned.1.call-done = bf16[2048,1024]{1,0:T(8,128)(2,1)} async-done(((bf16[256,1024]{1,0:T(8,128)(2,1)}), bf16[2048,1024]{1,0:T(8,128)(2,1)}) %all-gather.13.cloned.1.call-update) | async-done | bytes 4194320 | tf_op jit(solution)/shard_map/all_gather | solution.py:89
  191.2 6.5 copy.41
  197.6 3.5 fusion.57
  201.6 40.7 %all-gather.17.cloned.1.call-done = bf16[2048,256]{0,1:T(8,128)(2,1)} async-done(((bf16[256,256]{0,1:T(8,128)(2,1)}), bf16[2048,256]{0,1:T(8,128)(2,1)}) %all-gather.17.cloned.1.call-update) | async-done | bytes 1048592 | tf_op jit(solution)/shard_map/all_gather | solution.py:126
  242.3 4.3 fusion.3
  246.7 5.3 fusion
  252.6 5.6 fusion.54
  258.1 36.2 all-gather.23.cloned.1.call-done
  294.3 4.5 convolution_convert_fusion.1
  298.9 3.1 convert_element_type.245
  302.0 3.1 convert_element_type.246
  305.1 3.1 convert_element_type.248
  309.2 17.2 all-reduce.11.cloned.1.call-done
  328.7 119.8 %all-gather.25.cloned.1.call-done = bf16[2048,2816]{1,0:T(8,128)(2,1)} async-done(((bf16[256,2816]{1,0:T(8,128)(2,1)}), bf16[2048,2816]{1,0:T(8,128)(2,1)}) %all-gather.25.cloned.1.call-update) | async-done | bytes 11534352 | tf_op jit(solution)/shard_map/all_gather | solution.py:93
  448.5 9.0 fusion.89
  457.5 113.6 %all-gather.27.cloned.1.call-done = bf16[2048,2816]{1,0:T(8,128)(2,1)} async-done(((bf16[256,2816]{1,0:T(8,128)(2,1)}), bf16[2048,2816]{1,0:T(8,128)(2,1)}) %all-gather.27.cloned.1.call-update) | async-done | bytes 11534352 | tf_op jit(solution)/shard_map/all_gather | solution.py:94
  571.1 9.3 fusion.90
  580.4 113.1 %all-gather.29.cloned.1.call-done = bf16[2048,2816]{1,0:T(8,128)(2,1)} async-done(((bf16[256,2816]{1,0:T(8,128)(2,1)}), bf16[2048,2816]{1,0:T(8,128)(2,1)}) %all-gather.29.cloned.1.call-update) | async-done | bytes 11534352 | tf_op jit(solution)/shard_map/all_gather | solution.py:95
  693.6 10.3 multiply_convert_fusion.1
  703.9 7.1 fusion.91
  711.0 8.4 fusion.20
  720.0 26.6 all-reduce.13.cloned.1.call-done
  746.6 2.1 fusion.35
  748.7 4.7 convolution_convert_fusion.2
  753.5 2.0 copy.46
  757.1 10.9 fusion.21
  768.1 11.0 multiply_convert_fusion
  784.1 12.7 fusion.94
  796.9 12.9 fusion.95
  809.8 11.2 fusion.63
  821.1 9.1 convolution_convert_fusion
  830.2 6.4 fusion.92
  839.9 2.6 fusion.93
  842.5 16.5 reduce-scatter.9.cloned.1.call-done
  860.3 2.2 convolution_add_fusion.1
  866.7 2.8 fusion.71
  869.6 5.7 fusion.59
  875.7 6.9 fusion.67
  882.7 305.9 %reduce-scatter.19.cloned.1.call-done = f32[32,2816]{1,0:T(8,128)} async-done(((f32[2048,2816]{1,0:T(8,128)}), f32[32,2816]{1,0:T(8,128)}) %reduce-scatter.19.cloned.1.call-update) | async-done | bytes 360464 | tf_op jit(solution)/shard_map/reduce_scatter | solution.py:221
  1190.3 399.6 %reduce-scatter.21.cloned.1.call-done = f32[32,2816]{1,0:T(8,128)} async-done(((f32[2048,2816]{1,0:T(8,128)}), f32[32,2816]{1,0:T(8,128)}) %reduce-scatter.21.cloned.1.call-update) | async-done | bytes 360464 | tf_op jit(solution)/shard_map/reduce_scatter | solution.py:222
  1591.7 398.8 %reduce-scatter.23.cloned.1.call-done = f32[32,2816]{1,0:T(8,128)} async-done(((f32[2048,2816]{1,0:T(8,128)}), f32[32,2816]{1,0:T(8,128)}) %reduce-scatter.23.cloned.1.call-update) | async-done | bytes 360464 | tf_op jit(solution)/shard_map/reduce_scatter | solution.py:223
  1994.7 98.5 %all-reduce.15.cloned.1.call-done = (bf16[256,2048]{1,0:T(8,128)(2,1)}, bf16[256,2048]{1,0:T(8,128)(2,1)}) async-done(((bf16[256,2048]{1,0:T(8,128)(2,1)}, bf16[256,2048]{1,0:T(8,128)(2,1)}), (bf16[256,2048]{1,0:T(8,128)(2,1)}, bf16[256,2048]{1,0:T(8,128)(2,1)})) %all-reduce.15.cloned.1.call-update) | async-done | bytes 2097168 | tf_op jit(solution)/shard_map/psum | solution.py:151
  2095.1 267.8 %all-reduce.4 = (bf16[2048]{0:T(1024)(128)(2,1)S(1)}, bf16[2048]{0:T(1024)(128)(2,1)S(1)}) all-reduce(f32[2048]{0:T(1024)S(1)} %get-tuple-element.13, f32[2048]{0:T(1024)S(1)} %get-tuple-element.11), channel_id=3, replica_groups=mesh['shard'=8,'ctx'=8,'tp'=2] {'shard','ctx'}, use_global_device_ids=true, to_apply=%region_13.14.clone | all-reduce | flops 4096 | bytes 24576
  2363.5 16.7 all-reduce.5
  2381.3 4.5 fusion.47
  2386.5 28.2 all_gather.68
  2415.5 304.2 %reduce-scatter.15.cloned.1.call-done = f32[32,256]{1,0:T(8,128)} async-done(((f32[2048,256]{1,0:T(8,128)}), f32[32,256]{1,0:T(8,128)}) %reduce-scatter.15.cloned.1.call-update) | async-done | bytes 32784 | tf_op jit(solution)/shard_map/reduce_scatter | solution.py:219
  2720.4 27.9 all_gather.69
  2749.1 339.4 %reduce-scatter.11.cloned.1.call-done = f32[32,1024]{1,0:T(8,128)} async-done(((f32[2048,1024]{1,0:T(8,128)}), f32[32,1024]{1,0:T(8,128)}) %reduce-scatter.11.cloned.1.call-update) | async-done | bytes 131088 | tf_op jit(solution)/shard_map/reduce_scatter | solution.py:217
  3089.4 29.8 all_gather.67
  3120.3 333.0 %reduce-scatter.17.cloned.1.call-done = f32[32,1024]{1,0:T(8,128)} async-done(((f32[2048,1024]{1,0:T(8,128)}), f32[32,1024]{1,0:T(8,128)}) %reduce-scatter.17.cloned.1.call-update) | async-done | bytes 131088 | tf_op jit(solution)/shard_map/reduce_scatter | solution.py:220
  3454.2 30.0 all_gather.70
  3485.3 93.8 %all-gather.31.cloned.1.call-done = bf16[256,2816]{1,0:T(8,128)(2,1)} async-done(((bf16[32,2816]{1,0:T(8,128)(2,1)}), bf16[256,2816]{1,0:T(8,128)(2,1)}) %all-gather.31.cloned.1.call-update) | async-done | bytes 1441808 | tf_op jit(solution)/shard_map/all_gather | solution.py:232
  3579.1 3.1 convert_element_type.284
  3582.2 48.3 %all-gather.33.cloned.1.call-done = bf16[256,2816]{1,0:T(8,128)(2,1)} async-done(((bf16[32,2816]{1,0:T(8,128)(2,1)}), bf16[256,2816]{1,0:T(8,128)(2,1)}) %all-gather.33.cloned.1.call-update) | async-done | bytes 1441808 | tf_op jit(solution)/shard_map/all_gather | solution.py:233
  3630.5 3.1 convert_element_type.286
  3633.6 48.3 %all-gather.35.cloned.1.call-done = bf16[256,2816]{1,0:T(8,128)(2,1)} async-done(((bf16[32,2816]{1,0:T(8,128)(2,1)}), bf16[256,2816]{1,0:T(8,128)(2,1)}) %all-gather.35.cloned.1.call-update) | async-done | bytes 1441808 | tf_op jit(solution)/shard_map/all_gather | solution.py:234
  3681.9 3.1 convert_element_type.288
  (184 shorter events, 48.1 us)
Async XLA Ops:
  7.2 36.3 copy-start
  7.2 36.3 copy-start.28
  7.2 36.2 all-gather.19.cloned.1.call-start
  9.0 74.9 %all-gather.15.cloned.1.call-start = ((), (), s32[]{:S(2)}) async-start(), calls=%async_computation.9 | async-start | bytes 1179648 | tf_op jit(solution)/shard_map/all_gather | solution.py:90
  10.7 35.2 copy-start.22
  10.7 128.9 %all-gather.21.cloned.1.call-start = ((), (), s32[]{:S(2)}) async-start(), calls=%async_computation.12 | async-start | bytes 1179648 | tf_op jit(solution)/shard_map/all_gather | solution.py:127
  12.9 184.8 %copy-start.31 = (f32[256]{0:T(256)}, f32[256]{0:T(256)S(1)}, u32[]{:S(2)}) copy-start(f32[256]{0:T(256)S(1)} %get-tuple-element.39) | copy-start | bytes 3076
  45.8 145.3 %all-gather.13.cloned.1.call-start = ((), (), s32[]{:S(2)}) async-start(), calls=%async_computation.8 | async-start | bytes 4718592 | tf_op jit(solution)/shard_map/all_gather | solution.py:89
  46.8 195.5 %all-gather.17.cloned.1.call-start = ((), (), s32[]{:S(2)}) async-start(), calls=%async_computation.10 | async-start | bytes 1179648 | tf_op jit(solution)/shard_map/all_gather | solution.py:126
  47.2 154.1 %copy-start.16 = (f32[256,128]{0,1:T(8,128)}, f32[256,128]{0,1:T(8,128)S(1)}, u32[]{:S(2)}) copy-start(f32[256,128]{0,1:T(8,128)S(1)} %pad_maximum_fusion.4) | copy-start | bytes 393220
  47.2 154.1 %copy-start.11 = (f32[256,128]{0,1:T(8,128)}, f32[256,128]{0,1:T(8,128)S(1)}, u32[]{:S(2)}) copy-start(f32[256,128]{0,1:T(8,128)S(1)} %pad_maximum_fusion.3) | copy-start | bytes 393220
  86.2 2.7 copy-start.23
  88.0 1.8 copy-start.33
  88.0 1.8 copy-start.34
  88.8 205.5 %all-gather.23.cloned.1.call-start = ((), (), s32[]{:S(2)}) async-start(), calls=%async_computation.13 | async-start | bytes 4718592 | tf_op jit(solution)/shard_map/all_gather | solution.py:92
  89.8 236.6 %all-reduce.11.cloned.1.call-start = ((), (), s32[]{:S(2)}) async-start(), calls=%async_computation.14 | async-start | bytes 2097152 | tf_op jit(solution)/shard_map/psum | solution.py:140
  90.4 161.6 %copy-start.9 = (pred[256,2048]{1,0:T(8,128)(4,1)}, pred[256,2048]{1,0:T(8,128)(4,1)S(1)}, u32[]{:S(2)}) copy-start(pred[256,2048]{1,0:T(8,128)(4,1)S(1)} %compare_and_fusion) | copy-start | bytes 1572868
  201.5 45.1 %copy-start.6 = (bf16[256,8,128]{0,2,1:T(8,128)(2,1)}, bf16[256,8,128]{0,2,1:T(8,128)(2,1)S(1)}, u32[]{:S(2)}) copy-start(bf16[256,8,128]{0,2,1:T(8,128)(2,1)S(1)} %fusion.49) | copy-start | bytes 1572868
  246.6 5.9 copy-start.1
  246.7 5.9 copy-start.24
  258.1 40.7 %copy-start.27 = (bf16[256,2,4,128]{0,3,2,1:T(8,128)(2,1)}, bf16[256,2,4,128]{0,3,2,1:T(8,128)(2,1)S(1)}, u32[]{:S(2)}) copy-start(bf16[256,2,4,128]{0,3,2,1:T(8,128)(2,1)S(1)} %get-tuple-element.44) | copy-start | bytes 1572868
  298.8 149.7 %all-gather.25.cloned.1.call-start = ((), (), s32[]{:S(2)}) async-start(), calls=%async_computation.15 | async-start | bytes 12976128 | tf_op jit(solution)/shard_map/all_gather | solution.py:93
  302.0 269.2 %all-gather.27.cloned.1.call-start = ((), (), s32[]{:S(2)}) async-start(), calls=%async_computation.16 | async-start | bytes 12976128 | tf_op jit(solution)/shard_map/all_gather | solution.py:94
  305.1 388.5 %all-gather.29.cloned.1.call-start = ((), (), s32[]{:S(2)}) async-start(), calls=%async_computation.17 | async-start | bytes 12976128 | tf_op jit(solution)/shard_map/all_gather | solution.py:95
  308.2 20.0 copy-start.30
  308.2 438.4 %all-reduce.13.cloned.1.call-start = ((), (), s32[]{:S(2)}) async-start(), calls=%async_computation.18 | async-start | bytes 2097152 | tf_op jit(solution)/shard_map/psum | solution.py:162
  326.4 1.8 copy-start.3
  328.7 119.8 %copy-start.5 = (bf16[256,2048]{1,0:T(8,128)(2,1)}, bf16[256,2048]{1,0:T(8,128)(2,1)S(1)}, u32[]{:S(2)}) copy-start(bf16[256,2048]{1,0:T(8,128)(2,1)S(1)} %multiply_convert_fusion.5) | copy-start | bytes 3145732
  457.5 236.1 %copy-start.4 = (bf16[1,256,2048]{2,1,0:T(8,128)(2,1)S(1)}, bf16[1,256,2048]{2,1,0:T(8,128)(2,1)}, u32[]{:S(2)}) copy-start(bf16[1,256,2048]{2,1,0:T(8,128)(2,1)} %param.15) | copy-start | bytes 3145732
  703.9 7.1 copy-start.20
  703.9 7.1 copy-start.19
  719.4 139.5 %reduce-scatter.9.cloned.1.call-start = ((), (), s32[]{:S(2)}) async-start(), calls=%async_computation.19 | async-start | bytes 2359296 | tf_op jit(solution)/shard_map/reduce_scatter | solution.py:187
  746.6 2.1 copy-start.8
  757.0 11.0 copy-start.10
  757.1 11.0 copy-start.18
  757.1 11.0 copy-start.25
  768.0 11.1 copy-start.7
  779.1 3.3 copy-start.2
  784.0 404.6 %reduce-scatter.19.cloned.1.call-start = ((), (), s32[]{:S(2)}) async-start(), calls=%async_computation.24 | async-start | bytes 23429120 | tf_op jit(solution)/shard_map/reduce_scatter | solution.py:221
  796.8 793.1 %reduce-scatter.21.cloned.1.call-start = ((), (), s32[]{:S(2)}) async-start(), calls=%async_computation.26 | async-start | bytes 23429120 | tf_op jit(solution)/shard_map/reduce_scatter | solution.py:222
  809.8 1180.7 %reduce-scatter.23.cloned.1.call-start = ((), (), s32[]{:S(2)}) async-start(), calls=%async_computation.28 | async-start | bytes 23429120 | tf_op jit(solution)/shard_map/reduce_scatter | solution.py:223
  821.0 1272.2 %all-reduce.15.cloned.1.call-start = ((), (), s32[]{:S(2)}) async-start(), calls=%async_computation.30 | async-start | bytes 4194304 | tf_op jit(solution)/shard_map/psum | solution.py:151
  821.1 9.1 copy-start.13
  830.2 6.4 copy-start.17
  836.6 0.9 copy-start.12
  837.5 2.4 copy-start.14
  859.0 1.1 copy-start.21
  859.0 1.4 copy-start.15
  860.3 2.2 copy-start.26
  864.0 0.7 copy-start.29
  864.0 0.7 copy-start.32
  864.0 1521.7 %reduce-scatter.13.cloned.1.call-start = ((), (), s32[]{:S(2)}) async-start(), calls=%async_computation.21 | async-start | bytes 2129920 | tf_op jit(solution)/shard_map/reduce_scatter | solution.py:218
  866.7 1853.0 %reduce-scatter.15.cloned.1.call-start = ((), (), s32[]{:S(2)}) async-start(), calls=%async_computation.22 | async-start | bytes 2129920 | tf_op jit(solution)/shard_map/reduce_scatter | solution.py:219
  869.6 2218.9 %reduce-scatter.11.cloned.1.call-start = ((), (), s32[]{:S(2)}) async-start(), calls=%async_computation.20 | async-start | bytes 8519680 | tf_op jit(solution)/shard_map/reduce_scatter | solution.py:217
  875.4 2577.9 %reduce-scatter.17.cloned.1.call-start = ((), (), s32[]{:S(2)}) async-start(), calls=%async_computation.23 | async-start | bytes 8519680 | tf_op jit(solution)/shard_map/reduce_scatter | solution.py:220
  882.7 1109.5 %copy-start.37 = (u32[128]{0:T(128)S(1)}, u32[128]{0:T(128)}, u32[]{:S(2)}) copy-start(u32[128]{0:T(128)} %constant.59) | copy-start | bytes 1540
  882.7 1110.7 %copy-start.36 = (u32[128]{0:T(128)S(1)}, u32[128]{0:T(128)}, u32[]{:S(2)}) copy-start(u32[128]{0:T(128)} %constant.47) | copy-start | bytes 1540
  882.7 1498.6 %copy-start.35 = (f32[256]{0:T(256)S(1)}, f32[256]{0:T(256)}, u32[]{:S(2)}) copy-start(f32[256]{0:T(256)} %get-tuple-element.38) | copy-start | bytes 3076
  882.7 2696.4 %all-gather.31.cloned.1.call-start = ((), (), s32[]{:S(2)}) async-start(), calls=%async_computation.25 | async-start | bytes 1622016 | tf_op jit(solution)/shard_map/all_gather | solution.py:232
  1190.3 2440.2 %all-gather.33.cloned.1.call-start = ((), (), s32[]{:S(2)}) async-start(), calls=%async_computation.27 | async-start | bytes 1622016 | tf_op jit(solution)/shard_map/all_gather | solution.py:233
  1591.6 2090.3 %all-gather.35.cloned.1.call-start = ((), (), s32[]{:S(2)}) async-start(), calls=%async_computation.29 | async-start | bytes 1622016 | tf_op jit(solution)/shard_map/all_gather | solution.py:234
Sparse Core Ops, SparseCore 0:
  10.3 33.1 all-gather.18
  45.7 38.1 all-gather.14
  86.8 52.7 all-gather.20
  141.6 49.4 all-gather.12
  193.8 48.4 all-gather.16
  244.4 49.9 all-gather.22
  298.9 27.4 all-reduce.10
  328.7 119.7 all-gather.24
  450.8 120.2 all-gather.26
  573.3 120.2 all-gather.28
  719.6 27.0 all-reduce.12
  784.1 74.7 reduce-scatter.8
  861.5 327.0 reduce-scatter.18
  1191.0 398.8 reduce-scatter.20
  1592.3 398.0 reduce-scatter.22
  1993.5 99.6 all-reduce.14
  2096.0 274.9 reduce-scatter.12
  2373.9 345.7 reduce-scatter.14
  2722.0 366.3 reduce-scatter.10
  3090.7 362.5 reduce-scatter.16
  3456.2 122.8 all-gather.30
  3581.4 49.0 all-gather.32
  3632.8 49.0 all-gather.34
where the time goes:
time: 3700 us; the launch traced here: 3690 us
  waiting for transfers between devices  3020 us (82%)
  blocking collectives  401 us (11%)
  matrix products  170 us (5%)
  other arithmetic  62.4 us (2%)
    reduce_scatter x1, waiting for transfers between devices, per_device(): lax.psum_scatter(grad_up_local, ('shard', 'ctx'), scatter_dimension=0, ti...  400 us
    reduce_scatter x1, waiting for transfers between devices, per_device(): lax.psum_scatter(grad_down_local, ('shard', 'ctx'), scatter_dimension=0,...  399 us
    reduce_scatter x1, waiting for transfers between devices, per_device(): lax.psum_scatter(grad_query_local, ('shard', 'ctx'), scatter_dimension=0,...  339 us
    reduce_scatter x1, waiting for transfers between devices, per_device(): lax.psum_scatter(grad_out_local, ('shard', 'ctx'), scatter_dimension=0, t...  333 us
    reduce_scatter x1, waiting for transfers between devices, per_device(): lax.psum_scatter(grad_gate_local, ('shard', 'ctx'), scatter_dimension=0,...  306 us
    reduce_scatter x1, waiting for transfers between devices, per_device(): lax.psum_scatter(grad_value_local, ('shard', 'ctx'), scatter_dimension=0,...  304 us
    unnamed x2, blocking collectives  285 us
    all_gather x1, waiting for transfers between devices, per_device(): lax.all_gather(to_half(w_gate), 'shard', axis=0, tiled=True)  120 us
  transfers between devices with their start and end apart: 23, of which 22 were waited for; matrix products, arithmetic and copies ran while one was open for 5% of the time, Pallas kernels for 0%

commit v1 on v0

v1 whole, which is shorter than its diff:
```python
import jax
import jax.numpy as jnp
from jax import lax
from jax.sharding import Mesh, PartitionSpec as P

HD = 128
EPS = 1e-05
NEG = -1e30
F32 = jnp.float32
BF16 = jnp.bfloat16
SHARD = ("yl", "z")
SWAP = ((0, 1), (1, 0))


def half(value):
    return value.astype(BF16)


def mm(left, right):
    return jnp.dot(left, right, preferred_element_type=F32)


def mm_nt(left, right):
    return lax.dot_general(left, right, (((1,), (1,)), ((), ())), preferred_element_type=F32)


def mm_tn(left, right):
    return lax.dot_general(left, right, (((0,), (0,)), ((), ())), preferred_element_type=F32)


def swap_cores(value):
    return lax.ppermute(value, "tp", SWAP)


def shift_x(value, hop):
    return lax.ppermute(value, "x", [(i, (i + hop) % 4) for i in range(4)])


def gather_x(value):
    return [value] + [shift_x(value, -hop) for hop in (1, 2, 3)]


def scatter_x(chunks):
    moved = [shift_x(half(chunks[hop]), hop) for hop in (2, 1, 3)]
    return chunks[0] + moved[0].astype(F32) + moved[1].astype(F32) + moved[2].astype(F32)


def absolute(chunks, x_at):
    stacked = jnp.stack(chunks + chunks[:3])
    return lax.dynamic_slice_in_dim(stacked, (4 - x_at) % 4, 4, axis=0)


def rotate(value, cosine, sine):
    turned = jnp.concatenate([-value[..., HD // 2 :], value[..., : HD // 2]], axis=-1)
    return value * cosine + turned * sine


def unrotate(grad, cosine, sine):
    scaled = grad * sine
    return grad * cosine + jnp.concatenate(
        [scaled[..., HD // 2 :], -scaled[..., : HD // 2]], axis=-1
    )


def norm_root(value):
    return lax.rsqrt(jnp.mean(value * value, axis=-1, keepdims=True) + EPS)


def norm_backward(value, root, gain, grad):
    scaled = gain * grad
    grad_value = root * scaled - value * root**3 * jnp.mean(
        scaled * value, axis=-1, keepdims=True
    )
    return grad_value, jnp.sum(grad * value * root, axis=0)


def per_device(
    tokens, cotangent, seq_ids, block_ids, keep_layer, gain_attn, gain_ffn,
    w_query, w_key, w_value, w_out, w_gate, w_up, w_down,
):
    core, x_at, y_at = lax.axis_index("tp"), lax.axis_index("x"), lax.axis_index("yh")
    first = core == 0
    rows = tokens.shape[1] // 2
    width = tokens.shape[2]
    keep = keep_layer[0].astype(F32)
    scale = HD ** (-0.5)

    side = x_at // 2
    at = x_at % 2
    wq = half(lax.dynamic_slice_in_dim(w_query, at * 512, 512, axis=1))
    wk = half(lax.dynamic_slice_in_dim(w_key, at * HD, HD, axis=1))
    wv = half(lax.dynamic_slice_in_dim(w_value, at * HD, HD, axis=1))
    wo = half(lax.dynamic_slice_in_dim(w_out, at * 512, 512, axis=1))
    pack0 = jnp.concatenate([wq[:, :256], wk, wo[:, :256]], axis=1)
    pack1 = jnp.concatenate([wq[:, 256:], wv, wo[:, 256:]], axis=1)
    lent = lax.ppermute(
        jnp.where(first, pack1, pack0),
        ("x", "tp"),
        [(2 * i + i // 2, 2 * i + 1 - i // 2) for i in range(4)],
    )
    pack = jnp.where(core == side, jnp.where(first, pack0, pack1), lent)
    pack = lax.all_gather(pack, SHARD, axis=0, tiled=True)
    pack_other = swap_cores(pack)
    att0 = jnp.where(first, pack, pack_other)
    att1 = jnp.where(first, pack_other, pack)
    full_qkv = jnp.concatenate([att0[:, :384], att1[:, :384]], axis=1)
    full_out = jnp.concatenate([att0[:, 384:], att1[:, 384:]], axis=1)

    units = w_gate.shape[1] // 4

    def hidden_units(weight):
        own = half(lax.dynamic_slice_in_dim(weight, x_at * units, units, axis=1))
        own = lax.all_gather(own, SHARD, axis=0, tiled=True)
        return own, swap_cores(own)

    xval = lax.dynamic_slice_in_dim(tokens[0], core * rows, rows, axis=0).astype(F32)
    grad_top = lax.dynamic_slice_in_dim(cotangent[0], core * rows, rows, axis=0).astype(F32)
    root_attn = norm_root(xval)
    normed_attn = jnp.concatenate(gather_x(half(xval * root_attn * gain_attn)), axis=0)
    count = normed_attn.shape[0]

    def of_positions(line, y_index, core_index):
        grid = line.reshape(2, 4, 2, rows)
        picked = lax.dynamic_index_in_dim(grid, y_index, 0, keepdims=False)
        picked = lax.dynamic_index_in_dim(picked, core_index, 1, keepdims=False)
        double = jnp.concatenate([picked, picked], axis=0)
        return lax.dynamic_slice_in_dim(double, x_at, 4, axis=0).reshape(-1)

    corners = ((y_at, core), (y_at, 1 - core), (1 - y_at, core), (1 - y_at, 1 - core))
    seg_query = of_positions(seq_ids[0], y_at, core)
    blk_query = of_positions(block_ids[0], y_at, core)
    seg_keys = jnp.concatenate([of_positions(seq_ids[0], *corner) for corner in corners])
    blk_keys = jnp.concatenate([of_positions(block_ids[0], *corner) for corner in corners])
    allowed = (seg_query[:, None] == seg_keys[None, :]) & (blk_keys[None, :] <= blk_query[:, None])
    position = of_positions(jnp.arange(seq_ids.shape[1], dtype=jnp.int32), y_at, core)
    freqs = 10000.0 ** (-(jnp.arange(HD // 2).astype(F32) * 2.0 / HD))
    angle = position.astype(F32)[:, None] * freqs[None, :]
    cosine = jnp.concatenate([jnp.cos(angle), jnp.cos(angle)], axis=-1)
    sine = jnp.concatenate([jnp.sin(angle), jnp.sin(angle)], axis=-1)

    qkv = mm(normed_attn, full_qkv)
    starts = (0, 128, 384, 512)
    query = jnp.stack([half(rotate(qkv[:, s : s + HD], cosine, sine)) for s in starts])
    keys_values = jnp.concatenate(
        [half(rotate(qkv[:, 256:384], cosine, sine)), half(qkv[:, 640:])], axis=1
    )

    def across_y(value):
        return lax.ppermute(value, "yh", SWAP)

    two_kv = jnp.concatenate([keys_values, across_y(keys_values)], axis=0)
    other_kv = swap_cores(two_kv)
    all_kv = jnp.concatenate(
        [two_kv[:count], other_kv[:count], two_kv[count:], other_kv[count:]], axis=0
    )
    all_keys, all_values = all_kv[:, :HD], all_kv[:, HD:]

    raw = jnp.einsum("htd,nd->htn", query, all_keys, preferred_element_type=F32) * scale
    safe = jnp.where(allowed[None], raw, NEG)
    top = jnp.max(safe, axis=-1, keepdims=True)
    weights = jnp.where(allowed[None], jnp.exp(safe - top), 0.0)
    total = jnp.sum(weights, axis=-1, keepdims=True)
    added = jnp.einsum("htn,nd->htd", half(weights), all_values, preferred_element_type=F32)
    heads_f = added / total
    log_total = top + jnp.log(total)
    heads = half(heads_f.transpose(1, 0, 2).reshape(count, 4 * HD))

    def chunked(value):
        return [value[j * rows : (j + 1) * rows] for j in range(4)]

    attn_branch = scatter_x(chunked(mm_nt(heads, full_out)))
    middle = xval + keep * attn_branch
    root_ffn = norm_root(middle)
    normed_ffn = jnp.concatenate(gather_x(half(middle * root_ffn * gain_ffn)), axis=0)

    full_gate, full_up, full_down = hidden_units(w_gate), hidden_units(w_up), hidden_units(w_down)
    d_ffn = jnp.concatenate(gather_x(half(keep * grad_top)), axis=0)
    branch = 0.0
    d_normed = 0.0
    grads_gate, grads_up, grads_down = [], [], []
    for wg, wu, wd in zip(full_gate, full_up, full_down, strict=True):
        gate = mm(normed_ffn, wg)
        up = mm(normed_ffn, wu)
        sig = jax.nn.sigmoid(gate)
        silu = gate * sig
        hidden = half(silu * up)
        branch = branch + mm_nt(hidden, wd)
        d_hidden = mm(d_ffn, wd)
        d_gate = half(d_hidden * up * sig * (1.0 + gate * (1.0 - sig)))
        d_up = half(d_hidden * silu)
        d_normed = d_normed + mm_nt(d_gate, wg) + mm_nt(d_up, wu)
        grads_gate.append(mm_tn(normed_ffn, d_gate))
        grads_up.append(mm_tn(normed_ffn, d_up))
        grads_down.append(mm_tn(d_ffn, hidden))
    d_normed_ffn = scatter_x(chunked(d_normed))
    ffn_branch = scatter_x(chunked(branch))

    def both_cores(value):
        other = swap_cores(value)
        return jnp.concatenate(
            [jnp.where(first, value, other), jnp.where(first, other, value)], axis=0
        )

    output = both_cores(half(middle + keep * ffn_branch))

    def reduce_columns(mine, theirs):
        value = half(mine + swap_cores(half(theirs)).astype(F32))
        value = lax.psum_scatter(value, SHARD, scatter_dimension=0, tiled=True)
        value = half(value.astype(F32) + across_y(value).astype(F32))
        return absolute(gather_x(value), x_at)

    def units_of(value):
        return jnp.concatenate([value[i] for i in range(4)], axis=1).astype(F32)

    grad_down = units_of(reduce_columns(*grads_down))
    grad_gate = units_of(reduce_columns(*grads_gate))
    grad_up = units_of(reduce_columns(*grads_up))

    mid_part, gain_ffn_local = norm_backward(middle, root_ffn, gain_ffn, d_normed_ffn)
    d_middle = grad_top + mid_part
    d_attn = jnp.concatenate(gather_x(half(keep * d_middle)), axis=0)

    d_heads = half(mm(d_attn, full_out))
    d_heads_g = d_heads.reshape(count, 4, HD).transpose(1, 0, 2)
    row_delta = jnp.sum(d_heads_g.astype(F32) * heads_f, axis=-1, keepdims=True)
    raw = jnp.einsum("htd,nd->htn", query, all_keys, preferred_element_type=F32) * scale
    probs = jnp.where(allowed[None], jnp.exp(raw - log_total), 0.0)
    d_probs = jnp.einsum("htd,nd->htn", d_heads_g, all_values, preferred_element_type=F32)
    d_scores = half(scale * probs * (d_probs - row_delta))
    grad_q = jnp.einsum("htn,nd->htd", d_scores, all_keys, preferred_element_type=F32)
    key_part = jnp.einsum("htn,htd->nd", d_scores, query, preferred_element_type=F32)
    value_part = jnp.einsum("htn,htd->nd", half(probs), d_heads_g, preferred_element_type=F32)
    kv_part = jnp.concatenate([key_part, value_part], axis=1)
    kv_mine = jnp.concatenate([kv_part[:count], kv_part[2 * count : 3 * count]], axis=0)
    kv_theirs = jnp.concatenate([kv_part[count : 2 * count], kv_part[3 * count :]], axis=0)
    kv_two = kv_mine + swap_cores(half(kv_theirs)).astype(F32)
    grad_kv = kv_two[:count] + across_y(half(kv_two[count:])).astype(F32)
    d_q = [half(unrotate(grad_q[h], cosine, sine)) for h in range(4)]
    d_key = half(unrotate(grad_kv[:, :HD], cosine, sine))
    d_qkv = jnp.concatenate([d_q[0], d_q[1], d_key, d_q[2], d_q[3], half(grad_kv[:, HD:])], axis=1)
    d_normed_attn = scatter_x(chunked(mm_nt(d_qkv, full_qkv)))
    grad_qkv = mm_tn(normed_attn, d_qkv)
    grad_o = mm_tn(d_attn, heads)
    grads0 = jnp.concatenate([grad_qkv[:, :384], grad_o[:, :256]], axis=1)
    grads1 = jnp.concatenate([grad_qkv[:, 384:], grad_o[:, 256:]], axis=1)
    packs = reduce_columns(jnp.where(first, grads0, grads1), jnp.where(first, grads1, grads0))
    mine = lax.dynamic_slice_in_dim(packs, 2 * core, 2, axis=0)
    theirs = swap_cores(lax.dynamic_slice_in_dim(packs, 2 - 2 * core, 2, axis=0))
    out0 = jnp.where(first, mine, theirs).astype(F32)
    out1 = jnp.where(first, theirs, mine).astype(F32)
    grad_query = jnp.concatenate(
        [out0[0, :, :256], out1[0, :, :256], out0[1, :, :256], out1[1, :, :256]], axis=1
    )
    grad_key = jnp.concatenate([out0[0, :, 256:384], out0[1, :, 256:384]], axis=1)
    grad_value = jnp.concatenate([out1[0, :, 256:384], out1[1, :, 256:384]], axis=1)
    grad_out = jnp.concatenate(
        [out0[0, :, 384:], out1[0, :, 384:], out0[1, :, 384:], out1[1, :, 384:]], axis=1
    )

    input_part, gain_attn_local = norm_backward(xval, root_attn, gain_attn, d_normed_attn)
    input_grad = both_cores(half(d_middle + input_part))
    gains = lax.psum(
        jnp.stack([gain_attn_local, gain_ffn_local]), ("yl", "z", "yh", "x", "tp")
    )
    owned = width // 8
    gains = lax.dynamic_slice_in_dim(
        gains, (lax.axis_index("yl") * 4 + lax.axis_index("z")) * owned, owned, axis=1
    )
    return (
        output[None], input_grad[None], gains[0], gains[1],
        grad_query, grad_key, grad_value, grad_out, grad_gate, grad_up, grad_down,
    )


def solution(mesh):
    fine = Mesh(mesh.devices.reshape(2, 4, 2, 4, 2), ("yl", "z", "yh", "x", "tp"))
    shard, ctx = ("yl", "z"), ("yh", "x")
    acts, weight = P(shard, ctx, None), P(shard, "tp")
    return jax.shard_map(
        per_device,
        mesh=fine,
        in_specs=(acts, acts, P(shard, None), P(shard, None), P(shard), P(), P()) + (weight,) * 7,
        out_specs=(acts, acts, P(shard), P(shard)) + (weight,) * 7,
        check_vma=False,
    )
```

time: 3700 us -> 734 us (0.20)
  waiting for transfers between devices: 3020 us -> 290 us
  blocking collectives: 401 us -> 70.8 us
  starting transfers between devices: 1.93 us -> 107 us
  matrix products: 170 us -> 114 us
  local copies, waits for them, and re-layouts: 20.1 us -> 63.3 us
    reduce_scatter x8 -> x4, waiting for transfers between devices: 2100 us -> 0.03 us  [reduce_columns(): value = lax.psum_scatter(value, SHARD, scatter_dimension=0, tiled=True)]
    all_gather x12 -> x4, waiting for transfers between devices: 780 us -> 110 us  [the longest x3 68.3 us: hidden_units(): own = lax.all_gather(own, SHARD, axis=0, tiled=True)]
    unnamed x2 -> x0, blocking collectives: 285 us -> none
    ppermute x0 -> x56, waiting for transfers between devices: none -> 180 us  [the longest x36 140 us: shift_x(): return lax.ppermute(value, 'x', [(i, (i + hop) % 4) for i in range(4)])]
    psum x3 -> x0, waiting for transfers between devices: 142 us -> none  [the longest x1 98.5 us: per_device(): lax.psum(contract_cols(hidden, full_down).astype(jnp.bfloat16), 'tp')]
    all_gather x4 -> x0, blocking collectives: 116 us -> none  [the longest x1 30 us: per_device(): lax.all_gather(own_o.astype(jnp.bfloat16), 'ctx', axis=0, tiled=True)]
    ppermute x0 -> x56, starting transfers between devices: none -> 106 us  [the longest x13 47.3 us: swap_cores(): return lax.ppermute(value, 'tp', SWAP)]
    psum x0 -> x1, blocking collectives: none -> 70.8 us  [per_device(): lax.psum(jnp.stack([gain_attn_local, gain_ffn_local]), ('yl', 'z', 'yh',...]
  transfers between devices with their start and end apart: 23 -> 64, of which waited for: 22 -> 31; matrix products, arithmetic and copies ran while one was open for 5% -> 26% of each run, Pallas kernels for 0% -> 0%
where the time goes in v1:
time: 734 us; the launch traced here: 719 us
  waiting for transfers between devices  290 us (40%)
  matrix products  114 us (16%)
  starting transfers between devices  107 us (15%)
  blocking collectives  70.8 us (10%)
  local copies, waits for them, and re-layouts  63.3 us (9%)
  other arithmetic  58.3 us (8%)
  between operations  17 us (2%)
    ppermute x36, waiting for transfers between devices, shift_x(): return lax.ppermute(value, 'x', [(i, (i + hop) % 4) for i in range(4)])  140 us
    psum x1, blocking collectives, per_device(): lax.psum(jnp.stack([gain_attn_local, gain_ffn_local]), ('yl', 'z', 'yh',...  70.8 us
    all_gather x3, waiting for transfers between devices, hidden_units(): own = lax.all_gather(own, SHARD, axis=0, tiled=True)  68.3 us
    ppermute x13, starting transfers between devices, swap_cores(): return lax.ppermute(value, 'tp', SWAP)  47.3 us
    ppermute x36, starting transfers between devices, shift_x(): return lax.ppermute(value, 'x', [(i, (i + hop) % 4) for i in range(4)])  43.2 us
    all_gather x1, waiting for transfers between devices, per_device(): pack = lax.all_gather(pack, SHARD, axis=0, tiled=True)  41.6 us
    unnamed x222, local copies, waits for them, and re-layouts  37.6 us
    ppermute x6, waiting for transfers between devices, across_y(): return lax.ppermute(value, 'yh', SWAP)  37.4 us
  transfers between devices with their start and end apart: 64, of which 31 were waited for; matrix products, arithmetic and copies ran while one was open for 26% of the time, Pallas kernels for 0%

profile of v1, /device:TPU:97, one launch (start us, length us, event | category | flops | bytes accessed | tf_op | source)
XLA Modules:
  0.0 719.4 jit_solution(15446372410941713195)
XLA Ops:
  17.1 2.5 collective-permute-done.3
  25.9 41.6 %all-gather.5.cloned.1.call-done = bf16[2048,640]{0,1:T(8,128)(2,1)} async-done(((bf16[256,640]{0,1:T(8,128)(2,1)}), bf16[2048,640]{0,1:T(8,128)(2,1)}) %all-gather.5.cloned.1.call-update) | async-done | bytes 2621456 | tf_op jit(solution)/shard_map/all_gather | solution.py:102
  67.5 5.3 collective-permute-start.4
  88.9 12.2 %collective-permute-done.1 = bf16[128,2048]{1,0:T(8,128)(2,1)} collective-permute-done((bf16[128,2048]{1,0:T(8,128)(2,1)}, bf16[128,2048]{1,0:T(8,128)(2,1)}, u32[]{:S(2)}, u32[]{:S(2)}) %collective-permute-start.1) | collective-permute-done | bytes 524320 | tf_op jit(solution)/shard_map/ppermute | solution.py:36
  101.0 3.4 fusion.14
  109.0 11.7 %collective-permute-done.5 = bf16[512,256]{1,0:T(8,128)(2,1)S(1)} collective-permute-done((bf16[512,256]{1,0:T(8,128)(2,1)S(1)}, bf16[512,256]{1,0:T(8,128)(2,1)S(1)}, u32[]{:S(2)}, u32[]{:S(2)}) %collective-permute-start.5) | collective-permute-done | bytes 262176 | tf_op jit(solution)/shard_map/ppermute | solution.py:149
  125.7 4.5 collective-permute-start.15
  130.2 49.6 %all-gather.9.cloned.1.call-done = bf16[2048,704]{0,1:T(8,128)(2,1)} async-done(((bf16[256,704]{0,1:T(8,128)(2,1)}), bf16[2048,704]{0,1:T(8,128)(2,1)}) %all-gather.9.cloned.1.call-update) | async-done | bytes 2883600 | tf_op jit(solution)/shard_map/all_gather | solution.py:113
  179.8 5.5 collective-permute-start.14
  192.6 3.6 select_reduce_fusion
  196.2 5.0 fusion.1
  202.0 5.8 fusion.43
  207.8 3.3 fusion.129
  214.7 18.6 %all-gather.7.cloned.1.call-done = bf16[2048,704]{0,1:T(8,128)(2,1)} async-done(((bf16[256,704]{0,1:T(8,128)(2,1)}), bf16[2048,704]{0,1:T(8,128)(2,1)}) %all-gather.7.cloned.1.call-update) | async-done | bytes 2883600 | tf_op jit(solution)/shard_map/all_gather | solution.py:113
  233.3 4.6 collective-permute-start.13
  237.9 2.7 collective-permute-start.7
  242.5 10.9 %collective-permute-done.7 = bf16[128,2048]{1,0:T(8,128)(2,1)} collective-permute-done((bf16[128,2048]{1,0:T(8,128)(2,1)}, bf16[128,2048]{1,0:T(8,128)(2,1)}, u32[]{:S(2)}, u32[]{:S(2)}) %collective-permute-start.7) | collective-permute-done | bytes 524320 | tf_op jit(solution)/shard_map/ppermute | solution.py:36
  253.4 2.7 collective-permute-start.21
  258.2 7.0 collective-permute-done.22
  265.8 9.9 %collective-permute-done.21 = bf16[128,2048]{1,0:T(8,128)(2,1)S(1)} collective-permute-done((bf16[128,2048]{1,0:T(8,128)(2,1)}, bf16[128,2048]{1,0:T(8,128)(2,1)S(1)}, u32[]{:S(2)}, u32[]{:S(2)}) %collective-permute-start.21) | collective-permute-done | bytes 524320 | tf_op jit(solution)/shard_map/ppermute | solution.py:36
  275.7 4.0 collective-permute-done.20
  283.2 3.8 fusion.104
  287.1 2.5 collective-permute-done.12
  289.6 11.6 %collective-permute-done.11 = bf16[128,2048]{1,0:T(8,128)(2,1)S(1)} collective-permute-done((bf16[128,2048]{1,0:T(8,128)(2,1)S(1)}, bf16[128,2048]{1,0:T(8,128)(2,1)S(1)}, u32[]{:S(2)}, u32[]{:S(2)}) %collective-permute-start.11) | collective-permute-done | bytes 524320 | tf_op jit(solution)/shard_map/ppermute | solution.py:36
  301.2 4.7 collective-permute-done.10
  305.9 3.7 fusion.106
  309.6 4.2 multiply_convert_fusion.2
  313.8 3.2 convolution_convert_fusion.2
  318.6 3.7 fusion.135
  325.9 3.5 multiply_convert_fusion.3
  333.1 4.1 fusion.112
  337.4 2.9 collective-permute-start.25
  343.4 5.8 fusion.130
  351.7 11.0 %collective-permute-done.25 = bf16[128,2048]{1,0:T(8,128)(2,1)S(1)} collective-permute-done((bf16[128,2048]{1,0:T(8,128)(2,1)S(1)}, bf16[128,2048]{1,0:T(8,128)(2,1)S(1)}, u32[]{:S(2)}, u32[]{:S(2)}) %collective-permute-start.25) | collective-permute-done | bytes 524320 | tf_op jit(solution)/shard_map/ppermute | solution.py:36
  362.7 3.2 collective-permute-done.24
  368.8 4.3 add_convert_fusion.2
  373.3 12.0 %collective-permute-done.18 = bf16[128,2048]{1,0:T(8,128)(2,1)S(1)} collective-permute-done((bf16[128,2048]{1,0:T(8,128)(2,1)}, bf16[128,2048]{1,0:T(8,128)(2,1)S(1)}, u32[]{:S(2)}, u32[]{:S(2)}) %collective-permute-start.18) | collective-permute-done | bytes 524320 | tf_op jit(solution)/shard_map/ppermute | solution.py:36
  385.3 4.6 collective-permute-done.16
  390.0 4.2 multiply_convert_fusion.7
  398.7 2.6 collective-permute-start.46
  401.3 4.5 convolution_convert_fusion
  407.3 14.1 %collective-permute-start.19 = (bf16[128,2048]{1,0:T(8,128)(2,1)}, bf16[128,2048]{1,0:T(8,128)(2,1)}, u32[]{:S(2)}, u32[]{:S(2)}) collective-permute-start(bf16[128,2048]{1,0:T(8,128)(2,1)} %get-tuple-element.127), channel_id=1, source_target_pairs={{0,1},{1,0},{2,3},{3,2},{4,5},{5,4},{6,7},{7,6},{8,9},{9,8},{10,11... | collective-permute-start | bytes 1572872 | tf_op jit(solution)/shard_map/ppermute | solution.py:32
  423.4 12.5 %multiply_convert_fusion = bf16[4,512,2048]{2,1,0:T(8,128)(2,1)} fusion(f32[4,512,2048]{2,1,0:T(8,128)} %copy-done.5, f32[4,512]{1,0:T(4,128)S(1)} %get-tuple-element.171, f32[4,512]{1,0:T(4,128)S(1)} %log_add_fusion, pred[512,2048]{1,0:T(8,128)(4,1)S(1)} %copy-done.13, bf16[4,512,128]{1,2,0:T(8,128)(2,1)S(1)} %bitcast.246, bf16[2048,256]{1,0:T(8,128)(2,1)S(1)} %copy-done.31), kind=kOutput, calls=%fused_computation | convolution fusion | flops 1103101952 | bytes 27279360 | tf_op jit(solution)/shard_map/htd,nd->htn/dot_general | solution.py:228
  435.9 5.8 convolution_bitcast_fusion
  441.7 8.1 %fusion.9 = f32[2048,128]{1,0:T(8,128)S(1)} fusion(bf16[4,512,128]{1,2,0:T(8,128)(2,1)S(1)} %bitcast.247, f32[4,512,2048]{2,1,0:T(8,128)} %copy-done.5, f32[4,512]{1,0:T(4,128)S(1)} %log_add_fusion, pred[512,2048]{1,0:T(8,128)(4,1)S(1)} %copy-done.13), kind=kOutput, calls=%fused_computation.33 | convolution fusion | flops 1090519040 | bytes 19406848 | tf_op jit(solution)/shard_map/htn,htd->nd/dot_general | solution.py:232
  451.8 3.0 add_convert_fusion.1
  460.5 2.7 collective-permute-start.30
  465.6 9.1 %collective-permute-done.30 = bf16[512,256]{1,0:T(8,128)(2,1)S(1)} collective-permute-done((bf16[512,256]{1,0:T(8,128)(2,1)S(1)}, bf16[512,256]{1,0:T(8,128)(2,1)S(1)}, u32[]{:S(2)}, u32[]{:S(2)}) %collective-permute-start.30) | collective-permute-done | bytes 262176 | tf_op jit(solution)/shard_map/ppermute | solution.py:149
  477.8 5.5 add_convert_fusion
  485.0 3.2 fusion.131
  491.1 3.4 fusion.48
  503.7 9.0 %collective-permute-done.31 = bf16[128,2048]{1,0:T(8,128)(2,1)S(1)} collective-permute-done((bf16[128,2048]{1,0:T(8,128)(2,1)S(1)}, bf16[128,2048]{1,0:T(8,128)(2,1)S(1)}, u32[]{:S(2)}, u32[]{:S(2)}) %collective-permute-start.31) | collective-permute-done | bytes 524320 | tf_op jit(solution)/shard_map/ppermute | solution.py:36
  514.8 3.7 collective-permute-start.34
  519.5 70.8 %psum.7 = f32[2,2048]{1,0:T(2,128)S(1)} all-reduce(f32[2,2048]{1,0:T(2,128)S(1)} %pad_maximum_fusion.34), channel_id=1, replica_groups=mesh['yl'=2,'z'=4,'yh'=2,'x'=4,'tp'=2] {'yl','z','yh','x','tp'}, use_global_device_ids=true, to_apply=%region_9.10 | all-reduce | flops 4096 | bytes 32768 | tf_op jit(solution)/shard_map/psum | solution.py:262
  595.3 5.7 add_convert_fusion.3
  608.6 4.0 collective-permute-done.47
  614.9 12.5 %collective-permute-done.52 = bf16[256,704]{0,1:T(8,128)(2,1)S(1)} collective-permute-done((bf16[256,704]{0,1:T(8,128)(2,1)}, bf16[256,704]{0,1:T(8,128)(2,1)S(1)}, u32[]{:S(2)}, u32[]{:S(2)}) %collective-permute-start.52) | collective-permute-done | bytes 360480 | tf_op jit(solution)/shard_map/ppermute | solution.py:149
  636.5 12.3 %collective-permute-done.50 = bf16[256,704]{0,1:T(8,128)(2,1)S(1)} collective-permute-done((bf16[256,704]{0,1:T(8,128)(2,1)S(1)}, bf16[256,704]{0,1:T(8,128)(2,1)S(1)}, u32[]{:S(2)}, u32[]{:S(2)}) %collective-permute-start.50) | collective-permute-done | bytes 360480 | tf_op jit(solution)/shard_map/ppermute | solution.py:36
  652.6 4.3 collective-permute-start.36
  657.7 4.3 collective-permute-done.55
  671.8 2.8 collective-permute-done.38
  674.6 9.7 %collective-permute-done.39 = bf16[256,640]{0,1:T(8,128)(2,1)S(1)} collective-permute-done((bf16[256,640]{0,1:T(8,128)(2,1)S(1)}, bf16[256,640]{0,1:T(8,128)(2,1)S(1)}, u32[]{:S(2)}, u32[]{:S(2)}) %collective-permute-start.39) | collective-permute-done | bytes 327712 | tf_op jit(solution)/shard_map/ppermute | solution.py:36
  690.6 3.4 copy.68
  709.6 2.5 copy.66
  (446 shorter events, 175.4 us)
Async XLA Ops:
  7.2 60.3 %all-gather.5.cloned.1.call-start = ((), (), s32[]{:S(2)}) async-start(), calls=%async_computation.4 | async-start | bytes 2949120 | tf_op jit(solution)/shard_map/all_gather | solution.py:102
  15.8 3.9 collective-permute-start.3
  21.5 104.2 %all-gather.11.cloned.1.call-start = ((), (), s32[]{:S(2)}) async-start(), calls=%async_computation.7 | async-start | bytes 3244032 | tf_op jit(solution)/shard_map/all_gather | solution.py:113
  22.7 157.0 %all-gather.9.cloned.1.call-start = ((), (), s32[]{:S(2)}) async-start(), calls=%async_computation.6 | async-start | bytes 3244032 | tf_op jit(solution)/shard_map/all_gather | solution.py:113
  25.1 208.2 %all-gather.7.cloned.1.call-start = ((), (), s32[]{:S(2)}) async-start(), calls=%async_computation.5 | async-start | bytes 3244032 | tf_op jit(solution)/shard_map/all_gather | solution.py:113
  67.5 14.8 %collective-permute-start.4 = (bf16[2048,640]{0,1:T(8,128)(2,1)}, bf16[2048,640]{0,1:T(8,128)(2,1)}, u32[]{:S(2)}, u32[]{:S(2)}) collective-permute-start(bf16[2048,640]{0,1:T(8,128)(2,1)} %all-gather.5.cloned.1.call-done), channel_id=1, source_target_pairs={{0,1},{1,0},{2,3},{3,2},{4,5},{5,4},{6,7},{7,6},{8,9},{9,8},{10,11... | collective-permute-start | bytes 7864328 | tf_op jit(solution)/shard_map/ppermute | solution.py:32
  73.8 15.1 %collective-permute-start.2 = (bf16[128,2048]{1,0:T(8,128)(2,1)}, bf16[128,2048]{1,0:T(8,128)(2,1)}, u32[]{:S(2)}, u32[]{:S(2)}) collective-permute-start(bf16[128,2048]{1,0:T(8,128)(2,1)} %fusion.23), channel_id=1, source_target_pairs={{0,2},{2,4},{4,6},{6,0},{1,3},{3,5},{5,7},{7,1},{8,10},{10,12},{12... | collective-permute-start | bytes 1572872 | tf_op jit(solution)/shard_map/ppermute | solution.py:36
  75.0 26.0 %collective-permute-start.1 = (bf16[128,2048]{1,0:T(8,128)(2,1)}, bf16[128,2048]{1,0:T(8,128)(2,1)}, u32[]{:S(2)}, u32[]{:S(2)}) collective-permute-start(bf16[128,2048]{1,0:T(8,128)(2,1)} %fusion.23), channel_id=1, source_target_pairs={{0,4},{2,6},{4,0},{6,2},{1,5},{3,7},{5,1},{7,3},{8,12},{10,14},{12... | collective-permute-start | bytes 1572872 | tf_op jit(solution)/shard_map/ppermute | solution.py:36
  77.4 23.6 %collective-permute-start = (bf16[128,2048]{1,0:T(8,128)(2,1)}, bf16[128,2048]{1,0:T(8,128)(2,1)}, u32[]{:S(2)}, u32[]{:S(2)}) collective-permute-start(bf16[128,2048]{1,0:T(8,128)(2,1)} %fusion.23), channel_id=1, source_target_pairs={{0,6},{2,0},{4,2},{6,4},{1,7},{3,1},{5,3},{7,5},{8,14},{10,8},{12,... | collective-permute-start | bytes 1572872 | tf_op jit(solution)/shard_map/ppermute | solution.py:36
  80.8 512.3 %reduce-scatter.7.cloned.1.call-start = ((), (), s32[]{:S(2)}) async-start(), calls=%async_computation.9 | async-start | bytes 3244032 | tf_op jit(solution)/shard_map/reduce_scatter | solution.py:208
  106.4 14.3 %collective-permute-start.5 = (bf16[512,256]{1,0:T(8,128)(2,1)S(1)}, bf16[512,256]{1,0:T(8,128)(2,1)S(1)}, u32[]{:S(2)}, u32[]{:S(2)}) collective-permute-start(bf16[512,256]{1,0:T(8,128)(2,1)S(1)} %pad_maximum_fusion.29), channel_id=1, source_target_pairs={{0,8},{8,0},{1,9},{9,1},{2,10},{10,2},{3,11},{11,3},{4,12},{12,4},... | collective-permute-start | bytes 786440 | tf_op jit(solution)/shard_map/ppermute | solution.py:149
  121.6 69.8 %collective-permute-start.6 = (bf16[1024,256]{1,0:T(8,128)(2,1)}, bf16[1024,256]{1,0:T(8,128)(2,1)}, u32[]{:S(2)}, u32[]{:S(2)}) collective-permute-start(bf16[1024,256]{1,0:T(8,128)(2,1)} %pad_maximum_fusion.19), channel_id=1, source_target_pairs={{0,1},{1,0},{2,3},{3,2},{4,5},{5,4},{6,7},{7,6},{8,9},{9,8},{10,11... | collective-permute-start | bytes 1572872 | tf_op jit(solution)/shard_map/ppermute | solution.py:32
  125.7 155.8 %collective-permute-start.15 = (bf16[2048,704]{0,1:T(8,128)(2,1)}, bf16[2048,704]{0,1:T(8,128)(2,1)}, u32[]{:S(2)}, u32[]{:S(2)}) collective-permute-start(bf16[2048,704]{0,1:T(8,128)(2,1)} %all-gather.11.cloned.1.call-done), channel_id=1, source_target_pairs={{0,1},{1,0},{2,3},{3,2},{4,5},{5,4},{6,7},{7,6},{8,9},{9,8},{10,11... | collective-permute-start | bytes 8650760 | tf_op jit(solution)/shard_map/ppermute | solution.py:32
  179.8 107.3 %collective-permute-start.14 = (bf16[2048,704]{0,1:T(8,128)(2,1)}, bf16[2048,704]{0,1:T(8,128)(2,1)}, u32[]{:S(2)}, u32[]{:S(2)}) collective-permute-start(bf16[2048,704]{0,1:T(8,128)(2,1)} %all-gather.9.cloned.1.call-done), channel_id=1, source_target_pairs={{0,1},{1,0},{2,3},{3,2},{4,5},{5,4},{6,7},{7,6},{8,9},{9,8},{10,11... | collective-permute-start | bytes 8650760 | tf_op jit(solution)/shard_map/ppermute | solution.py:32
  212.3 25.7 %collective-permute-start.9 = (bf16[128,2048]{1,0:T(8,128)(2,1)}, bf16[128,2048]{1,0:T(8,128)(2,1)S(1)}, u32[]{:S(2)}, u32[]{:S(2)}) collective-permute-start(bf16[128,2048]{1,0:T(8,128)(2,1)} %get-tuple-element.91), channel_id=1, source_target_pairs={{0,6},{2,0},{4,2},{6,4},{1,7},{3,1},{5,3},{7,5},{8,14},{10,8},{12,... | collective-permute-start | bytes 1572872 | tf_op jit(solution)/shard_map/ppermute | solution.py:36
  214.7 27.5 %collective-permute-start.8 = (bf16[128,2048]{1,0:T(8,128)(2,1)}, bf16[128,2048]{1,0:T(8,128)(2,1)}, u32[]{:S(2)}, u32[]{:S(2)}) collective-permute-start(bf16[128,2048]{1,0:T(8,128)(2,1)} %get-tuple-element.92), channel_id=1, source_target_pairs={{0,2},{2,4},{4,6},{6,0},{1,3},{3,5},{5,7},{7,1},{8,10},{10,12},{12... | collective-permute-start | bytes 1572872 | tf_op jit(solution)/shard_map/ppermute | solution.py:36
  233.3 76.3 %collective-permute-start.13 = (bf16[2048,704]{0,1:T(8,128)(2,1)}, bf16[2048,704]{0,1:T(8,128)(2,1)}, u32[]{:S(2)}, u32[]{:S(2)}) collective-permute-start(bf16[2048,704]{0,1:T(8,128)(2,1)} %all-gather.7.cloned.1.call-done), channel_id=1, source_target_pairs={{0,1},{1,0},{2,3},{3,2},{4,5},{5,4},{6,7},{7,6},{8,9},{9,8},{10,11... | collective-permute-start | bytes 8650760 | tf_op jit(solution)/shard_map/ppermute | solution.py:32
  237.9 15.4 %collective-permute-start.7 = (bf16[128,2048]{1,0:T(8,128)(2,1)}, bf16[128,2048]{1,0:T(8,128)(2,1)}, u32[]{:S(2)}, u32[]{:S(2)}) collective-permute-start(bf16[128,2048]{1,0:T(8,128)(2,1)} %get-tuple-element.90), channel_id=1, source_target_pairs={{0,4},{2,6},{4,0},{6,2},{1,5},{3,7},{5,1},{7,3},{8,12},{10,14},{12... | collective-permute-start | bytes 1572872 | tf_op jit(solution)/shard_map/ppermute | solution.py:36
  242.2 22.9 %collective-permute-start.22 = (bf16[128,2048]{1,0:T(8,128)(2,1)}, bf16[128,2048]{1,0:T(8,128)(2,1)}, u32[]{:S(2)}, u32[]{:S(2)}) collective-permute-start(bf16[128,2048]{1,0:T(8,128)(2,1)} %fusion.20), channel_id=1, source_target_pairs={{0,2},{2,4},{4,6},{6,0},{1,3},{3,5},{5,7},{7,1},{8,10},{10,12},{12... | collective-permute-start | bytes 1572872 | tf_op jit(solution)/shard_map/ppermute | solution.py:36
  253.4 22.4 %collective-permute-start.21 = (bf16[128,2048]{1,0:T(8,128)(2,1)}, bf16[128,2048]{1,0:T(8,128)(2,1)S(1)}, u32[]{:S(2)}, u32[]{:S(2)}) collective-permute-start(bf16[128,2048]{1,0:T(8,128)(2,1)} %fusion.20), channel_id=1, source_target_pairs={{0,4},{2,6},{4,0},{6,2},{1,5},{3,7},{5,1},{7,3},{8,12},{10,14},{12... | collective-permute-start | bytes 1572872 | tf_op jit(solution)/shard_map/ppermute | solution.py:36
  265.1 14.5 %collective-permute-start.20 = (bf16[128,2048]{1,0:T(8,128)(2,1)}, bf16[128,2048]{1,0:T(8,128)(2,1)S(1)}, u32[]{:S(2)}, u32[]{:S(2)}) collective-permute-start(bf16[128,2048]{1,0:T(8,128)(2,1)} %fusion.20), channel_id=1, source_target_pairs={{0,6},{2,0},{4,2},{6,4},{1,7},{3,1},{5,3},{7,5},{8,14},{10,8},{12,... | collective-permute-start | bytes 1572872 | tf_op jit(solution)/shard_map/ppermute | solution.py:36
  275.7 13.9 %collective-permute-start.12 = (bf16[128,2048]{1,0:T(8,128)(2,1)S(1)}, bf16[128,2048]{1,0:T(8,128)(2,1)S(1)}, u32[]{:S(2)}, u32[]{:S(2)}) collective-permute-start(bf16[128,2048]{1,0:T(8,128)(2,1)S(1)} %multiply_convert_fusion.8), channel_id=1, source_target_pairs={{0,2},{2,4},{4,6},{6,0},{1,3},{3,5},{5,7},{7,1},{8,10},{10,12},{12... | collective-permute-start | bytes 1572872 | tf_op jit(solution)/shard_map/ppermute | solution.py:36
  279.7 21.5 %collective-permute-start.11 = (bf16[128,2048]{1,0:T(8,128)(2,1)S(1)}, bf16[128,2048]{1,0:T(8,128)(2,1)S(1)}, u32[]{:S(2)}, u32[]{:S(2)}) collective-permute-start(bf16[128,2048]{1,0:T(8,128)(2,1)S(1)} %multiply_convert_fusion.8), channel_id=1, source_target_pairs={{0,4},{2,6},{4,0},{6,2},{1,5},{3,7},{5,1},{7,3},{8,12},{10,14},{12... | collective-permute-start | bytes 1572872 | tf_op jit(solution)/shard_map/ppermute | solution.py:36
  281.5 24.4 %collective-permute-start.10 = (bf16[128,2048]{1,0:T(8,128)(2,1)S(1)}, bf16[128,2048]{1,0:T(8,128)(2,1)S(1)}, u32[]{:S(2)}, u32[]{:S(2)}) collective-permute-start(bf16[128,2048]{1,0:T(8,128)(2,1)S(1)} %multiply_convert_fusion.8), channel_id=1, source_target_pairs={{0,6},{2,0},{4,2},{6,4},{1,7},{3,1},{5,3},{7,5},{8,14},{10,8},{12,... | collective-permute-start | bytes 1572872 | tf_op jit(solution)/shard_map/ppermute | solution.py:36
  317.1 51.7 %collective-permute-start.41 = (bf16[2048,704]{0,1:T(8,128)(2,1)}, bf16[2048,704]{0,1:T(8,128)(2,1)}, u32[]{:S(2)}, u32[]{:S(2)}) collective-permute-start(bf16[2048,704]{0,1:T(8,128)(2,1)} %convolution_convert_fusion.2), channel_id=1, source_target_pairs={{0,1},{1,0},{2,3},{3,2},{4,5},{5,4},{6,7},{7,6},{8,9},{9,8},{10,11... | collective-permute-start | bytes 8650760 | tf_op jit(solution)/shard_map/ppermute | solution.py:32
  337.4 25.4 %collective-permute-start.25 = (bf16[128,2048]{1,0:T(8,128)(2,1)S(1)}, bf16[128,2048]{1,0:T(8,128)(2,1)S(1)}, u32[]{:S(2)}, u32[]{:S(2)}) collective-permute-start(bf16[128,2048]{1,0:T(8,128)(2,1)S(1)} %get-tuple-element.85), channel_id=1, source_target_pairs={{0,6},{2,0},{4,2},{6,4},{1,7},{3,1},{5,3},{7,5},{8,14},{10,8},{12,... | collective-permute-start | bytes 1572872 | tf_op jit(solution)/shard_map/ppermute | solution.py:36
  340.2 25.7 %collective-permute-start.24 = (bf16[128,2048]{1,0:T(8,128)(2,1)S(1)}, bf16[128,2048]{1,0:T(8,128)(2,1)S(1)}, u32[]{:S(2)}, u32[]{:S(2)}) collective-permute-start(bf16[128,2048]{1,0:T(8,128)(2,1)S(1)} %get-tuple-element.86), channel_id=1, source_target_pairs={{0,2},{2,4},{4,6},{6,0},{1,3},{3,5},{5,7},{7,1},{8,10},{10,12},{12... | collective-permute-start | bytes 1572872 | tf_op jit(solution)/shard_map/ppermute | solution.py:36
  340.2 27.3 %collective-permute-start.23 = (bf16[128,2048]{1,0:T(8,128)(2,1)S(1)}, bf16[128,2048]{1,0:T(8,128)(2,1)S(1)}, u32[]{:S(2)}, u32[]{:S(2)}) collective-permute-start(bf16[128,2048]{1,0:T(8,128)(2,1)S(1)} %get-tuple-element.84), channel_id=1, source_target_pairs={{0,4},{2,6},{4,0},{6,2},{1,5},{3,7},{5,1},{7,3},{8,12},{10,14},{12... | collective-permute-start | bytes 1572872 | tf_op jit(solution)/shard_map/ppermute | solution.py:36
  350.3 35.0 %collective-permute-start.18 = (bf16[128,2048]{1,0:T(8,128)(2,1)}, bf16[128,2048]{1,0:T(8,128)(2,1)S(1)}, u32[]{:S(2)}, u32[]{:S(2)}) collective-permute-start(bf16[128,2048]{1,0:T(8,128)(2,1)} %get-tuple-element.88), channel_id=1, source_target_pairs={{0,6},{2,0},{4,2},{6,4},{1,7},{3,1},{5,3},{7,5},{8,14},{10,8},{12,... | collective-permute-start | bytes 1572872 | tf_op jit(solution)/shard_map/ppermute | solution.py:36
  362.7 22.6 %collective-permute-start.17 = (bf16[128,2048]{1,0:T(8,128)(2,1)}, bf16[128,2048]{1,0:T(8,128)(2,1)}, u32[]{:S(2)}, u32[]{:S(2)}) collective-permute-start(bf16[128,2048]{1,0:T(8,128)(2,1)} %get-tuple-element.89), channel_id=1, source_target_pairs={{0,2},{2,4},{4,6},{6,0},{1,3},{3,5},{5,7},{7,1},{8,10},{10,12},{12... | collective-permute-start | bytes 1572872 | tf_op jit(solution)/shard_map/ppermute | solution.py:36
  365.9 24.0 %collective-permute-start.16 = (bf16[128,2048]{1,0:T(8,128)(2,1)}, bf16[128,2048]{1,0:T(8,128)(2,1)}, u32[]{:S(2)}, u32[]{:S(2)}) collective-permute-start(bf16[128,2048]{1,0:T(8,128)(2,1)} %get-tuple-element.87), channel_id=1, source_target_pairs={{0,4},{2,6},{4,0},{6,2},{1,5},{3,7},{5,1},{7,3},{8,12},{10,14},{12... | collective-permute-start | bytes 1572872 | tf_op jit(solution)/shard_map/ppermute | solution.py:36
  373.2 228.0 %reduce-scatter.9.cloned.1.call-start = ((), (), s32[]{:S(2)}) async-start(), calls=%async_computation.10 | async-start | bytes 3244032 | tf_op jit(solution)/shard_map/reduce_scatter | solution.py:208
  394.2 13.1 %collective-permute-start.28 = (bf16[128,2048]{1,0:T(8,128)(2,1)S(1)}, bf16[128,2048]{1,0:T(8,128)(2,1)S(1)}, u32[]{:S(2)}, u32[]{:S(2)}) collective-permute-start(bf16[128,2048]{1,0:T(8,128)(2,1)S(1)} %get-tuple-element.46), channel_id=1, source_target_pairs={{0,2},{2,4},{4,6},{6,0},{1,3},{3,5},{5,7},{7,1},{8,10},{10,12},{12... | collective-permute-start | bytes 1572872 | tf_op jit(solution)/shard_map/ppermute | solution.py:36
  394.3 27.2 %collective-permute-start.27 = (bf16[128,2048]{1,0:T(8,128)(2,1)S(1)}, bf16[128,2048]{1,0:T(8,128)(2,1)S(1)}, u32[]{:S(2)}, u32[]{:S(2)}) collective-permute-start(bf16[128,2048]{1,0:T(8,128)(2,1)S(1)} %get-tuple-element.46), channel_id=1, source_target_pairs={{0,4},{2,6},{4,0},{6,2},{1,5},{3,7},{5,1},{7,3},{8,12},{10,14},{12... | collective-permute-start | bytes 1572872 | tf_op jit(solution)/shard_map/ppermute | solution.py:36
  395.2 26.2 %collective-permute-start.26 = (bf16[128,2048]{1,0:T(8,128)(2,1)S(1)}, bf16[128,2048]{1,0:T(8,128)(2,1)S(1)}, u32[]{:S(2)}, u32[]{:S(2)}) collective-permute-start(bf16[128,2048]{1,0:T(8,128)(2,1)S(1)} %get-tuple-element.46), channel_id=1, source_target_pairs={{0,6},{2,0},{4,2},{6,4},{1,7},{3,1},{5,3},{7,5},{8,14},{10,8},{12,... | collective-permute-start | bytes 1572872 | tf_op jit(solution)/shard_map/ppermute | solution.py:36
  398.7 52.3 %collective-permute-start.46 = (bf16[2048,704]{0,1:T(8,128)(2,1)S(1)}, bf16[2048,704]{0,1:T(8,128)(2,1)S(1)}, u32[]{:S(2)}, u32[]{:S(2)}) collective-permute-start(bf16[2048,704]{0,1:T(8,128)(2,1)S(1)} %convolution_convert_fusion.1), channel_id=1, source_target_pairs={{0,1},{1,0},{2,3},{3,2},{4,5},{5,4},{6,7},{7,6},{8,9},{9,8},{10,11... | collective-permute-start | bytes 8650760 | tf_op jit(solution)/shard_map/ppermute | solution.py:32
  405.8 71.9 %collective-permute-start.51 = (bf16[2048,704]{0,1:T(8,128)(2,1)}, bf16[2048,704]{0,1:T(8,128)(2,1)}, u32[]{:S(2)}, u32[]{:S(2)}) collective-permute-start(bf16[2048,704]{0,1:T(8,128)(2,1)} %convolution_convert_fusion), channel_id=1, source_target_pairs={{0,1},{1,0},{2,3},{3,2},{4,5},{5,4},{6,7},{7,6},{8,9},{9,8},{10,11... | collective-permute-start | bytes 8650760 | tf_op jit(solution)/shard_map/ppermute | solution.py:32
  407.3 94.4 %collective-permute-start.19 = (bf16[128,2048]{1,0:T(8,128)(2,1)}, bf16[128,2048]{1,0:T(8,128)(2,1)}, u32[]{:S(2)}, u32[]{:S(2)}) collective-permute-start(bf16[128,2048]{1,0:T(8,128)(2,1)} %get-tuple-element.127), channel_id=1, source_target_pairs={{0,1},{1,0},{2,3},{3,2},{4,5},{5,4},{6,7},{7,6},{8,9},{9,8},{10,11... | collective-permute-start | bytes 1572872 | tf_op jit(solution)/shard_map/ppermute | solution.py:32
  454.8 148.5 %reduce-scatter.11.cloned.1.call-start = ((), (), s32[]{:S(2)}) async-start(), calls=%async_computation.11 | async-start | bytes 3244032 | tf_op jit(solution)/shard_map/reduce_scatter | solution.py:208
  456.2 4.2 collective-permute-start.29
  460.5 14.1 %collective-permute-start.30 = (bf16[512,256]{1,0:T(8,128)(2,1)S(1)}, bf16[512,256]{1,0:T(8,128)(2,1)S(1)}, u32[]{:S(2)}, u32[]{:S(2)}) collective-permute-start(bf16[512,256]{1,0:T(8,128)(2,1)S(1)} %slice.636), channel_id=1, source_target_pairs={{0,8},{8,0},{1,9},{9,1},{2,10},{10,2},{3,11},{11,3},{4,12},{12,4},... | collective-permute-start | bytes 786440 | tf_op jit(solution)/shard_map/ppermute | solution.py:149
  483.3 169.3 %reduce-scatter.5.cloned.1.call-start = ((), (), s32[]{:S(2)}) async-start(), calls=%async_computation.8 | async-start | bytes 2949120 | tf_op jit(solution)/shard_map/reduce_scatter | solution.py:208
  488.3 14.7 %collective-permute-start.33 = (bf16[128,2048]{1,0:T(8,128)(2,1)S(1)}, bf16[128,2048]{1,0:T(8,128)(2,1)S(1)}, u32[]{:S(2)}, u32[]{:S(2)}) collective-permute-start(bf16[128,2048]{1,0:T(8,128)(2,1)S(1)} %get-tuple-element.80), channel_id=1, source_target_pairs={{0,6},{2,0},{4,2},{6,4},{1,7},{3,1},{5,3},{7,5},{8,14},{10,8},{12,... | collective-permute-start | bytes 1572872 | tf_op jit(solution)/shard_map/ppermute | solution.py:36
  489.6 14.1 %collective-permute-start.32 = (bf16[128,2048]{1,0:T(8,128)(2,1)S(1)}, bf16[128,2048]{1,0:T(8,128)(2,1)S(1)}, u32[]{:S(2)}, u32[]{:S(2)}) collective-permute-start(bf16[128,2048]{1,0:T(8,128)(2,1)S(1)} %get-tuple-element.81), channel_id=1, source_target_pairs={{0,2},{2,4},{4,6},{6,0},{1,3},{3,5},{5,7},{7,1},{8,10},{10,12},{12... | collective-permute-start | bytes 1572872 | tf_op jit(solution)/shard_map/ppermute | solution.py:36
  489.8 22.9 %collective-permute-start.31 = (bf16[128,2048]{1,0:T(8,128)(2,1)S(1)}, bf16[128,2048]{1,0:T(8,128)(2,1)S(1)}, u32[]{:S(2)}, u32[]{:S(2)}) collective-permute-start(bf16[128,2048]{1,0:T(8,128)(2,1)S(1)} %get-tuple-element.79), channel_id=1, source_target_pairs={{0,4},{2,6},{4,0},{6,2},{1,5},{3,7},{5,1},{7,3},{8,12},{10,14},{12... | collective-permute-start | bytes 1572872 | tf_op jit(solution)/shard_map/ppermute | solution.py:36
  499.9 95.5 %collective-permute-start.35 = (bf16[2048,640]{0,1:T(8,128)(2,1)}, bf16[2048,640]{0,1:T(8,128)(2,1)}, u32[]{:S(2)}, u32[]{:S(2)}) collective-permute-start(bf16[2048,640]{0,1:T(8,128)(2,1)} %select_convert_fusion), channel_id=1, source_target_pairs={{0,1},{1,0},{2,3},{3,2},{4,5},{5,4},{6,7},{7,6},{8,9},{9,8},{10,11... | collective-permute-start | bytes 7864328 | tf_op jit(solution)/shard_map/ppermute | solution.py:32
  514.8 76.1 %collective-permute-start.34 = (bf16[128,2048]{1,0:T(8,128)(2,1)}, bf16[128,2048]{1,0:T(8,128)(2,1)}, u32[]{:S(2)}, u32[]{:S(2)}) collective-permute-start(bf16[128,2048]{1,0:T(8,128)(2,1)} %fusion.27), channel_id=1, source_target_pairs={{0,1},{1,0},{2,3},{3,2},{4,5},{5,4},{6,7},{7,6},{8,9},{9,8},{10,11... | collective-permute-start | bytes 1572872 | tf_op jit(solution)/shard_map/ppermute | solution.py:32
  593.2 12.1 %collective-permute-start.42 = (bf16[256,704]{0,1:T(8,128)(2,1)}, bf16[256,704]{0,1:T(8,128)(2,1)S(1)}, u32[]{:S(2)}, u32[]{:S(2)}) collective-permute-start(bf16[256,704]{0,1:T(8,128)(2,1)} %reduce-scatter.7.cloned.1.call-done), channel_id=1, source_target_pairs={{0,8},{8,0},{1,9},{9,1},{2,10},{10,2},{3,11},{11,3},{4,12},{12,4},... | collective-permute-start | bytes 1081352 | tf_op jit(solution)/shard_map/ppermute | solution.py:149
  601.2 11.4 %collective-permute-start.47 = (bf16[256,704]{0,1:T(8,128)(2,1)}, bf16[256,704]{0,1:T(8,128)(2,1)S(1)}, u32[]{:S(2)}, u32[]{:S(2)}) collective-permute-start(bf16[256,704]{0,1:T(8,128)(2,1)} %reduce-scatter.9.cloned.1.call-done), channel_id=1, source_target_pairs={{0,8},{8,0},{1,9},{9,1},{2,10},{10,2},{3,11},{11,3},{4,12},{12,4},... | collective-permute-start | bytes 1081352 | tf_op jit(solution)/shard_map/ppermute | solution.py:149
  603.3 24.1 %collective-permute-start.52 = (bf16[256,704]{0,1:T(8,128)(2,1)}, bf16[256,704]{0,1:T(8,128)(2,1)S(1)}, u32[]{:S(2)}, u32[]{:S(2)}) collective-permute-start(bf16[256,704]{0,1:T(8,128)(2,1)} %reduce-scatter.11.cloned.1.call-done), channel_id=1, source_target_pairs={{0,8},{8,0},{1,9},{9,1},{2,10},{10,2},{3,11},{11,3},{4,12},{12,4},... | collective-permute-start | bytes 1081352 | tf_op jit(solution)/shard_map/ppermute | solution.py:149
  605.4 24.2 %collective-permute-start.43 = (bf16[256,704]{0,1:T(8,128)(2,1)S(1)}, bf16[256,704]{0,1:T(8,128)(2,1)S(1)}, u32[]{:S(2)}, u32[]{:S(2)}) collective-permute-start(bf16[256,704]{0,1:T(8,128)(2,1)S(1)} %get-tuple-element.42), channel_id=1, source_target_pairs={{0,6},{2,0},{4,2},{6,4},{1,7},{3,1},{5,3},{7,5},{8,14},{10,8},{12,... | collective-permute-start | bytes 1081352 | tf_op jit(solution)/shard_map/ppermute | solution.py:36
  606.6 24.0 %collective-permute-start.44 = (bf16[256,704]{0,1:T(8,128)(2,1)S(1)}, bf16[256,704]{0,1:T(8,128)(2,1)S(1)}, u32[]{:S(2)}, u32[]{:S(2)}) collective-permute-start(bf16[256,704]{0,1:T(8,128)(2,1)S(1)} %get-tuple-element.42), channel_id=1, source_target_pairs={{0,4},{2,6},{4,0},{6,2},{1,5},{3,7},{5,1},{7,3},{8,12},{10,14},{12... | collective-permute-start | bytes 1081352 | tf_op jit(solution)/shard_map/ppermute | solution.py:36
  608.6 23.8 %collective-permute-start.45 = (bf16[256,704]{0,1:T(8,128)(2,1)S(1)}, bf16[256,704]{0,1:T(8,128)(2,1)S(1)}, u32[]{:S(2)}, u32[]{:S(2)}) collective-permute-start(bf16[256,704]{0,1:T(8,128)(2,1)S(1)} %get-tuple-element.42), channel_id=1, source_target_pairs={{0,2},{2,4},{4,6},{6,0},{1,3},{3,5},{5,7},{7,1},{8,10},{10,12},{12... | collective-permute-start | bytes 1081352 | tf_op jit(solution)/shard_map/ppermute | solution.py:36
  612.7 20.5 %collective-permute-start.48 = (bf16[256,704]{0,1:T(8,128)(2,1)S(1)}, bf16[256,704]{0,1:T(8,128)(2,1)S(1)}, u32[]{:S(2)}, u32[]{:S(2)}) collective-permute-start(bf16[256,704]{0,1:T(8,128)(2,1)S(1)} %get-tuple-element.40), channel_id=1, source_target_pairs={{0,6},{2,0},{4,2},{6,4},{1,7},{3,1},{5,3},{7,5},{8,14},{10,8},{12,... | collective-permute-start | bytes 1081352 | tf_op jit(solution)/shard_map/ppermute | solution.py:36
  627.5 9.0 %collective-permute-start.49 = (bf16[256,704]{0,1:T(8,128)(2,1)S(1)}, bf16[256,704]{0,1:T(8,128)(2,1)S(1)}, u32[]{:S(2)}, u32[]{:S(2)}) collective-permute-start(bf16[256,704]{0,1:T(8,128)(2,1)S(1)} %get-tuple-element.40), channel_id=1, source_target_pairs={{0,4},{2,6},{4,0},{6,2},{1,5},{3,7},{5,1},{7,3},{8,12},{10,14},{12... | collective-permute-start | bytes 1081352 | tf_op jit(solution)/shard_map/ppermute | solution.py:36
  629.5 19.2 %collective-permute-start.50 = (bf16[256,704]{0,1:T(8,128)(2,1)S(1)}, bf16[256,704]{0,1:T(8,128)(2,1)S(1)}, u32[]{:S(2)}, u32[]{:S(2)}) collective-permute-start(bf16[256,704]{0,1:T(8,128)(2,1)S(1)} %get-tuple-element.40), channel_id=1, source_target_pairs={{0,2},{2,4},{4,6},{6,0},{1,3},{3,5},{5,7},{7,1},{8,10},{10,12},{12... | collective-permute-start | bytes 1081352 | tf_op jit(solution)/shard_map/ppermute | solution.py:36
  630.6 20.5 %collective-permute-start.53 = (bf16[256,704]{0,1:T(8,128)(2,1)}, bf16[256,704]{0,1:T(8,128)(2,1)S(1)}, u32[]{:S(2)}, u32[]{:S(2)}) collective-permute-start(bf16[256,704]{0,1:T(8,128)(2,1)} %get-tuple-element.38), channel_id=1, source_target_pairs={{0,6},{2,0},{4,2},{6,4},{1,7},{3,1},{5,3},{7,5},{8,14},{10,8},{12,... | collective-permute-start | bytes 1081352 | tf_op jit(solution)/shard_map/ppermute | solution.py:36
  632.4 24.5 %collective-permute-start.54 = (bf16[256,704]{0,1:T(8,128)(2,1)}, bf16[256,704]{0,1:T(8,128)(2,1)S(1)}, u32[]{:S(2)}, u32[]{:S(2)}) collective-permute-start(bf16[256,704]{0,1:T(8,128)(2,1)} %get-tuple-element.38), channel_id=1, source_target_pairs={{0,4},{2,6},{4,0},{6,2},{1,5},{3,7},{5,1},{7,3},{8,12},{10,14},{12... | collective-permute-start | bytes 1081352 | tf_op jit(solution)/shard_map/ppermute | solution.py:36
  633.2 28.7 %collective-permute-start.55 = (bf16[256,704]{0,1:T(8,128)(2,1)}, bf16[256,704]{0,1:T(8,128)(2,1)}, u32[]{:S(2)}, u32[]{:S(2)}) collective-permute-start(bf16[256,704]{0,1:T(8,128)(2,1)} %get-tuple-element.38), channel_id=1, source_target_pairs={{0,2},{2,4},{4,6},{6,0},{1,3},{3,5},{5,7},{7,1},{8,10},{10,12},{12... | collective-permute-start | bytes 1081352 | tf_op jit(solution)/shard_map/ppermute | solution.py:36
  652.6 11.1 %collective-permute-start.36 = (bf16[256,640]{0,1:T(8,128)(2,1)}, bf16[256,640]{0,1:T(8,128)(2,1)S(1)}, u32[]{:S(2)}, u32[]{:S(2)}) collective-permute-start(bf16[256,640]{0,1:T(8,128)(2,1)} %reduce-scatter.5.cloned.1.call-done), channel_id=1, source_target_pairs={{0,8},{8,0},{1,9},{9,1},{2,10},{10,2},{3,11},{11,3},{4,12},{12,4},... | collective-permute-start | bytes 983048 | tf_op jit(solution)/shard_map/ppermute | solution.py:149
  664.8 7.0 collective-permute-start.37
  666.6 7.9 %collective-permute-start.38 = (bf16[256,640]{0,1:T(8,128)(2,1)S(1)}, bf16[256,640]{0,1:T(8,128)(2,1)S(1)}, u32[]{:S(2)}, u32[]{:S(2)}) collective-permute-start(bf16[256,640]{0,1:T(8,128)(2,1)S(1)} %get-tuple-element.44), channel_id=1, source_target_pairs={{0,4},{2,6},{4,0},{6,2},{1,5},{3,7},{5,1},{7,3},{8,12},{10,14},{12... | collective-permute-start | bytes 983048 | tf_op jit(solution)/shard_map/ppermute | solution.py:36
  669.1 15.2 %collective-permute-start.39 = (bf16[256,640]{0,1:T(8,128)(2,1)S(1)}, bf16[256,640]{0,1:T(8,128)(2,1)S(1)}, u32[]{:S(2)}, u32[]{:S(2)}) collective-permute-start(bf16[256,640]{0,1:T(8,128)(2,1)S(1)} %get-tuple-element.44), channel_id=1, source_target_pairs={{0,2},{2,4},{4,6},{6,0},{1,3},{3,5},{5,7},{7,1},{8,10},{10,12},{12... | collective-permute-start | bytes 983048 | tf_op jit(solution)/shard_map/ppermute | solution.py:36
  686.7 11.2 %collective-permute-start.40 = (bf16[2,256,640]{1,2,0:T(8,128)(2,1)}, bf16[2,256,640]{1,2,0:T(8,128)(2,1)}, u32[]{:S(2)}, u32[]{:S(2)}) collective-permute-start(bf16[2,256,640]{1,2,0:T(8,128)(2,1)} %constant_dynamic-slice_fusion.1), channel_id=1, source_target_pairs={{0,1},{1,0},{2,3},{3,2},{4,5},{5,4},{6,7},{7,6},{8,9},{9,8},{10,11... | collective-permute-start | bytes 1966088 | tf_op jit(solution)/shard_map/ppermute | solution.py:32
  (94 other events, 1301.2 us)
Sparse Core Ops, SparseCore 0:
  21.6 45.7 all-gather.4
  69.6 56.0 all-gather.10
  127.9 51.8 all-gather.8
  181.8 51.5 all-gather.6
  373.3 39.7 reduce-scatter.6
  454.9 44.4 reduce-scatter.8
  502.4 43.1 reduce-scatter.10
  601.2 46.5 reduce-scatter.4

commit v2 on v1

v2 whole, which is shorter than its diff:
```python
import functools

import jax
import jax.numpy as jnp
from jax import lax
from jax.experimental import pallas as pl
from jax.experimental.pallas import tpu as pltpu
from jax.sharding import Mesh, PartitionSpec as P

HD = 128
EPS = 1e-05
NEG = -1e30
F32 = jnp.float32
BF16 = jnp.bfloat16
SHARD = ("yl", "z")
SCALE = HD ** (-0.5)
LOG2E = 1.4426950408889634
VMEM = 48 * 2**20
SWAP = ((0, 1), (1, 0))


def half(value):
    return value.astype(BF16)


def mm(left, right):
    return jnp.dot(left, right, preferred_element_type=F32)


def mm_nt(left, right):
    return lax.dot_general(left, right, (((1,), (1,)), ((), ())), preferred_element_type=F32)


def mm_tn(left, right):
    return lax.dot_general(left, right, (((0,), (0,)), ((), ())), preferred_element_type=F32)


def swap_cores(value):
    return lax.ppermute(value, "tp", SWAP)


def across_y(value):
    return lax.ppermute(value, "yh", SWAP)


def after(value, *others):
    zero = sum((other[:1, :1] * 0).astype(value.dtype) for other in others)
    tile = value[:16, :HD] + zero
    return lax.dynamic_update_slice(value, tile, (0, 0))


def shift_x(value, hop):
    return lax.ppermute(value, "x", [(i, (i + hop) % 4) for i in range(4)])


def gather_x(value):
    moved = {hop: shift_x(value, -hop) for hop in (2, 1, 3)}
    return [value, moved[1], moved[2], moved[3]]


def scatter_x(chunks):
    moved = [shift_x(half(chunks[hop]), hop) for hop in (2, 1, 3)]
    return chunks[0] + moved[0].astype(F32) + moved[1].astype(F32) + moved[2].astype(F32)


def absolute(chunks, x_at):
    return [lax.select_n((i - x_at) % 4, *chunks) for i in range(4)]


def gather_shard(value):
    spread = jnp.broadcast_to(value[None], (8, *value.shape))
    return lax.all_to_all(spread, SHARD, 0, 0).reshape(-1, value.shape[1])


def rotate(value, cosine, sine):
    turned = jnp.concatenate([-value[..., HD // 2 :], value[..., : HD // 2]], axis=-1)
    return value * cosine + turned * sine


def unrotate(grad, cosine, sine):
    scaled = grad * sine
    return grad * cosine + jnp.concatenate(
        [scaled[..., HD // 2 :], -scaled[..., : HD // 2]], axis=-1
    )


def norm_root(value):
    return lax.rsqrt(jnp.mean(value * value, axis=-1, keepdims=True) + EPS)


def norm_backward(value, root, gain, grad):
    scaled = gain * grad
    return root * scaled - value * root**3 * jnp.mean(scaled * value, axis=-1, keepdims=True)


def attend_kernel(q_ref, kt_ref, v_ref, bias_ref, mixed_ref, heads_ref, lse_ref):
    raw = jnp.dot(q_ref[...], kt_ref[...], preferred_element_type=F32)
    raw = raw * (SCALE * LOG2E) + bias_ref[...]
    top = jnp.max(raw, axis=-1, keepdims=True)
    weights = jnp.exp2(raw - top)
    total = jnp.sum(weights, axis=-1, keepdims=True)
    mixed = jnp.dot(half(weights), v_ref[...], preferred_element_type=F32) / total
    mixed_ref[...] = mixed
    heads_ref[...] = half(mixed)
    lse_ref[0] = top + jnp.log2(total)


def attend(query, keys_t, values, bias, rows=256):
    count, features = query.shape
    n = values.shape[0]
    part = pl.BlockSpec((rows, HD), lambda j, h: (j, h))
    return pl.pallas_call(
        attend_kernel,
        grid=(count // rows, features // HD),
        in_specs=[
            part,
            pl.BlockSpec((HD, n), lambda j, h: (0, 0)),
            pl.BlockSpec((n, HD), lambda j, h: (0, 0)),
            pl.BlockSpec((rows, n), lambda j, h: (j, 0)),
        ],
        out_specs=[part, part, pl.BlockSpec((1, rows, 1), lambda j, h: (h, j, 0))],
        out_shape=[
            jax.ShapeDtypeStruct((count, features), F32),
            jax.ShapeDtypeStruct((count, features), BF16),
            jax.ShapeDtypeStruct((features // HD, count, 1), F32),
        ],
        compiler_params=pltpu.CompilerParams(vmem_limit_bytes=VMEM),
    )(query, keys_t, values, bias)


def attend_back_kernel(
    q_ref, qt_ref, do_ref, dot_ref, lse_ref, delta_ref, k_ref, kt_ref, v_ref, bias_ref,
    dqt_ref, dk_ref, dv_ref, *, piece,
):
    @pl.when(pl.program_id(0) == 0)
    def _():
        dk_ref[...] = jnp.zeros_like(dk_ref)
        dv_ref[...] = jnp.zeros_like(dv_ref)

    q, qt, d_out, d_out_t = q_ref[...], qt_ref[...], do_ref[...], dot_ref[...]
    lse, delta = lse_ref[0], delta_ref[0]
    grad_qt = jnp.zeros(dqt_ref.shape, F32)
    for at in range(0, k_ref.shape[0], piece):
        part = pl.ds(at, piece)
        raw = jnp.dot(k_ref[part, :], qt, preferred_element_type=F32)
        probs = jnp.exp2(raw * (SCALE * LOG2E) + (bias_ref[part, :] - lse))
        d_probs = jnp.dot(v_ref[part, :], d_out_t, preferred_element_type=F32)
        dv_ref[part, :] += jnp.dot(half(probs), d_out, preferred_element_type=F32)
        d_scores = half(probs * (SCALE * (d_probs - delta)))
        dk_ref[part, :] += jnp.dot(d_scores, q, preferred_element_type=F32)
        grad_qt += jnp.dot(kt_ref[:, part], d_scores, preferred_element_type=F32)
    dqt_ref[...] = grad_qt


def attend_back(query, query_t, d_heads, d_heads_t, lse, delta, keys, keys_t, values, bias_t):
    count, features = query.shape
    n = keys.shape[0]
    row = pl.BlockSpec((count, HD), lambda h: (0, h))
    col = pl.BlockSpec((HD, count), lambda h: (h, 0))
    line = pl.BlockSpec((1, 1, count), lambda h: (h, 0, 0))
    whole = pl.BlockSpec((n, HD), lambda h: (0, 0))
    return pl.pallas_call(
        functools.partial(attend_back_kernel, piece=512),
        grid=(features // HD,),
        in_specs=[
            row, col, row, col, line, line, whole,
            pl.BlockSpec((HD, n), lambda h: (0, 0)), whole,
            pl.BlockSpec((n, count), lambda h: (0, 0)),
        ],
        out_specs=[col, whole, whole],
        out_shape=[
            jax.ShapeDtypeStruct((features, count), F32),
            jax.ShapeDtypeStruct((n, HD), F32),
            jax.ShapeDtypeStruct((n, HD), F32),
        ],
        compiler_params=pltpu.CompilerParams(vmem_limit_bytes=VMEM),
    )(query, query_t, d_heads, d_heads_t, lse, delta, keys, keys_t, values, bias_t)


def per_device(
    tokens, cotangent, seq_ids, block_ids, keep_layer, gain_attn, gain_ffn,
    w_query, w_key, w_value, w_out, w_gate, w_up, w_down,
):
    core, x_at, y_at = lax.axis_index("tp"), lax.axis_index("x"), lax.axis_index("yh")
    first = core == 0
    rows = tokens.shape[1] // 2
    width = tokens.shape[2]
    keep = keep_layer[0].astype(F32)

    own_tokens = lax.dynamic_slice_in_dim(tokens[0], core * rows, rows, axis=0)
    x_all = lax.all_gather(own_tokens, "x", axis=0, tiled=True)
    own_top = lax.dynamic_slice_in_dim(cotangent[0], core * rows, rows, axis=0)
    xval, grad_top = own_tokens.astype(F32), own_top.astype(F32)

    side = x_at // 2
    at = x_at % 2
    wq = half(lax.dynamic_slice_in_dim(w_query, at * 512, 512, axis=1))
    wk = half(lax.dynamic_slice_in_dim(w_key, at * HD, HD, axis=1))
    wv = half(lax.dynamic_slice_in_dim(w_value, at * HD, HD, axis=1))
    wo = half(lax.dynamic_slice_in_dim(w_out, at * 512, 512, axis=1))
    pack0 = jnp.concatenate([wq[:, :256], wk, wo[:, :256]], axis=1)
    pack1 = jnp.concatenate([wq[:, 256:], wv, wo[:, 256:]], axis=1)
    lent = lax.ppermute(
        jnp.where(first, pack1, pack0),
        ("x", "tp"),
        [(2 * i + i // 2, 2 * i + 1 - i // 2) for i in range(4)],
    )
    pack = jnp.where(core == side, jnp.where(first, pack0, pack1), lent)
    pack = gather_shard(pack)

    units = w_gate.shape[1] // 4
    tiles = units // HD * HD
    spare = units - tiles
    split = tiles + HD

    def hidden_units(weight):
        main = lax.dynamic_slice_in_dim(weight, x_at * tiles, tiles, axis=1)
        rest = lax.dynamic_slice_in_dim(weight[:, 4 * tiles :], x_at * spare, spare, axis=1)
        return jnp.concatenate([half(main), jnp.pad(half(rest), ((0, 0), (0, HD - spare)))], axis=1)

    own_down = lax.all_gather(after(hidden_units(w_down), x_all), SHARD, axis=0, tiled=True)
    own_gu = jnp.concatenate([hidden_units(w_gate), hidden_units(w_up)], axis=1)
    own_gu = lax.all_gather(after(own_gu, pack), SHARD, axis=0, tiled=True)

    def of_positions(line, y_index, core_index):
        grid = line.reshape(2, 4, 2, rows)
        picked = lax.dynamic_index_in_dim(grid, y_index, 0, keepdims=False)
        picked = lax.dynamic_index_in_dim(picked, core_index, 1, keepdims=False)
        double = jnp.concatenate([picked, picked], axis=0)
        return lax.dynamic_slice_in_dim(double, x_at, 4, axis=0).reshape(-1)

    corners = ((y_at, core), (y_at, 1 - core), (1 - y_at, core), (1 - y_at, 1 - core))
    seg_query = of_positions(seq_ids[0], y_at, core)
    blk_query = of_positions(block_ids[0], y_at, core)
    seg_keys = jnp.concatenate([of_positions(seq_ids[0], *corner) for corner in corners])
    blk_keys = jnp.concatenate([of_positions(block_ids[0], *corner) for corner in corners])
    allowed = (seg_query[:, None] == seg_keys[None, :]) & (blk_keys[None, :] <= blk_query[:, None])
    bias = jnp.where(allowed, 0.0, NEG).astype(F32)
    allowed = (seg_query[None, :] == seg_keys[:, None]) & (blk_keys[:, None] <= blk_query[None, :])
    bias_t = jnp.where(allowed, 0.0, NEG).astype(F32)
    position = of_positions(jnp.arange(seq_ids.shape[1], dtype=jnp.int32), y_at, core)
    freqs = 10000.0 ** (-(jnp.arange(HD // 2).astype(F32) * 2.0 / HD))
    angle = position.astype(F32)[:, None] * freqs[None, :]
    cosine = jnp.concatenate([jnp.cos(angle), jnp.cos(angle)], axis=-1)
    sine = jnp.concatenate([jnp.sin(angle), jnp.sin(angle)], axis=-1)

    count = x_all.shape[0]
    x_all = jnp.concatenate([x_all, x_all[: 3 * rows]], axis=0)
    x_all = lax.dynamic_slice_in_dim(x_all, x_at * rows, count, axis=0).astype(F32)
    top_chunks = gather_x(after(own_top, x_all))
    x_unit = x_all * norm_root(x_all)
    normed_attn = half(x_unit * gain_attn)
    root_attn = norm_root(xval)
    packs_qkv = pack[:, :384], swap_cores(pack[:, :384])
    packs_out = pack[:, 384:], swap_cores(pack[:, 384:])
    own_pre, other_pre = [mm(normed_attn, part) for part in packs_qkv]
    key_pre = jnp.where(first, own_pre[:, 256:], other_pre[:, 256:])
    value_pre = jnp.where(first, other_pre[:, 256:], own_pre[:, 256:])
    query = jnp.concatenate(
        [half(rotate(pre[:, s : s + HD], cosine, sine)) for pre in (own_pre, other_pre) for s in (0, HD)],
        axis=1,
    )
    keys_values = jnp.concatenate([half(rotate(key_pre, cosine, sine)), half(value_pre)], axis=1)
    two_kv = jnp.concatenate([keys_values, across_y(keys_values)], axis=0)
    other_kv = swap_cores(two_kv)
    all_kv = jnp.concatenate(
        [two_kv[:count], other_kv[:count], two_kv[count:], other_kv[count:]], axis=0
    )
    all_keys, all_values = all_kv[:, :HD], all_kv[:, HD:]
    d_ffn = half(keep * jnp.concatenate(top_chunks, axis=0).astype(F32))

    keys_t = all_keys.T
    heads_f, heads, lse = attend(query, keys_t, all_values, bias)

    def chunked(value):
        return [value[j * rows : (j + 1) * rows] for j in range(4)]

    heads = after(heads, d_ffn)
    attn_branch = mm_nt(heads[:, :256], packs_out[0]) + mm_nt(heads[:, 256:], packs_out[1])
    attn_branch = scatter_x(chunked(attn_branch))
    middle = xval + keep * attn_branch
    root_ffn = norm_root(middle)
    normed_ffn = jnp.concatenate(gather_x(half(middle * root_ffn * gain_ffn)), axis=0)

    own_gu, own_down = after(own_gu, normed_ffn), after(own_down, normed_ffn)
    full_gu = (own_gu, swap_cores(own_gu))
    full_down = (own_down, swap_cores(own_down))
    branch = 0.0
    d_normed = 0.0
    d_gus, hiddens = [], []
    for wgu, wd in zip(full_gu, full_down, strict=True):
        gate_up = mm(normed_ffn, wgu)
        gate, up = gate_up[:, :split], gate_up[:, split:]
        sig = jax.nn.sigmoid(gate)
        silu = gate * sig
        hidden = half(silu * up)
        d_hidden = mm(d_ffn, wd)
        d_gate = half(d_hidden * up * sig * (1.0 + gate * (1.0 - sig)))
        d_up = half(d_hidden * silu)
        d_gu = jnp.concatenate([d_gate, d_up], axis=1)
        d_normed = d_normed + mm_nt(d_gu, wgu)
        branch = branch + mm_nt(hidden, wd)
        d_gus.append(d_gu)
        hiddens.append(hidden)
    left_down = after(d_ffn, d_normed)
    grads_down = [mm_tn(left_down, hidden) for hidden in hiddens]
    d_normed_ffn = scatter_x(chunked(d_normed))
    left_gu = after(normed_ffn, d_normed_ffn)
    grads_gu = [mm_tn(left_gu, d_gu) for d_gu in d_gus]
    d_middle = grad_top + norm_backward(middle, root_ffn, gain_ffn, d_normed_ffn)
    gain_ffn_local = jnp.sum(d_normed_ffn * middle * root_ffn, axis=0)

    def both_cores(value):
        other = swap_cores(value)
        return jnp.concatenate(
            [jnp.where(first, value, other), jnp.where(first, other, value)], axis=0
        )

    def sum_cores(mine, theirs):
        return half(mine + swap_cores(half(theirs)).astype(F32))

    def reduce_rows(value):
        return lax.psum_scatter(value, SHARD, scatter_dimension=0, tiled=True)

    def columns(value):
        value = half(value.astype(F32) + across_y(value).astype(F32))
        return absolute(gather_x(value), x_at)

    def units_of(parts, start):
        main = [part[:, start : start + tiles].astype(F32) for part in parts]
        rest = [part[:, start + tiles : start + units].astype(F32) for part in parts]
        return jnp.concatenate(main + rest, axis=1)

    sum_down, sum_gu = sum_cores(*grads_down), sum_cores(*grads_gu)
    own_d_attn = half(keep * d_middle)
    own_d_attn = after(own_d_attn, sum_down)
    d_attn = jnp.concatenate(gather_x(own_d_attn), axis=0)
    rows_down = reduce_rows(sum_down)
    rows_gu = reduce_rows(sum_gu)
    d_attn = after(d_attn, rows_down, sum_gu)
    parts_down = columns(after(rows_down, d_attn))
    ffn_branch = scatter_x(chunked(after(branch, d_attn)))
    output = both_cores(half(middle + keep * ffn_branch))

    d_heads = jnp.concatenate([half(mm(d_attn, part)) for part in packs_out], axis=1)
    delta = jnp.sum((d_heads.astype(F32) * heads_f).reshape(count, 4, HD), axis=-1).T[:, None, :]
    grad_qt, key_part, value_part = attend_back(
        query, query.T, d_heads, d_heads.T, lse.reshape(4, 1, count), delta,
        all_keys, keys_t, all_values, bias_t,
    )
    grad_q = grad_qt.T
    kv_part = jnp.concatenate([key_part, value_part], axis=1)
    kv_mine = jnp.concatenate([kv_part[:count], kv_part[2 * count : 3 * count]], axis=0)
    kv_theirs = jnp.concatenate([kv_part[count : 2 * count], kv_part[3 * count :]], axis=0)
    kv_two = kv_mine + swap_cores(half(kv_theirs)).astype(F32)
    grad_kv = kv_two[:count] + across_y(half(kv_two[count:])).astype(F32)
    grad_kv = after(grad_kv, ffn_branch, *parts_down)
    d_q = [half(unrotate(grad_q[:, h * HD : (h + 1) * HD], cosine, sine)) for h in range(4)]
    d_key = half(unrotate(grad_kv[:, :HD], cosine, sine))
    d_value = half(grad_kv[:, HD:])
    d_own = jnp.concatenate([d_q[0], d_q[1], jnp.where(first, d_key, d_value)], axis=1)
    d_other = jnp.concatenate([d_q[2], d_q[3], jnp.where(first, d_value, d_key)], axis=1)
    d_normed_part = mm_nt(d_own, packs_qkv[0]) + mm_nt(d_other, packs_qkv[1])
    d_normed_attn = scatter_x(chunked(d_normed_part))
    grad_down = units_of(parts_down, 0)
    input_part = norm_backward(xval, root_attn, gain_attn, d_normed_attn)
    input_grad = both_cores(half(d_middle + input_part))
    gain_attn_local = jnp.sum(d_normed_part * x_unit, axis=0)
    gains = half(jnp.stack([gain_attn_local, gain_ffn_local])).T
    sum_qkv = sum_cores(mm_tn(normed_attn, d_own), mm_tn(normed_attn, d_other))
    sum_out = sum_cores(mm_tn(d_attn, heads[:, :256]), mm_tn(d_attn, heads[:, 256:]))
    sums = jnp.concatenate([sum_qkv, sum_out], axis=1)
    sums = jnp.concatenate([sums, jnp.pad(gains, ((0, 0), (0, HD - 2)))], axis=1)
    sixteenth = width // 16
    parts = lax.all_to_all(sums.reshape(16, sixteenth, -1), ("yl", "z", "yh"), 0, 0)
    total_rows = after(half(jnp.sum(parts.astype(F32), axis=0)), rows_gu)
    packs = lax.all_to_all(jnp.broadcast_to(total_rows[None], (8, *total_rows.shape)), ("yh", "x"), 0, 0)
    packs = packs.reshape(2, 4, sixteenth, -1).transpose(1, 0, 2, 3).reshape(4, 2 * sixteenth, -1)
    parts_gu = columns(after(rows_gu, total_rows))
    grad_gate, grad_up = units_of(parts_gu, 0), units_of(parts_gu, split)
    gains = jnp.sum(packs[:, :, 640:642].astype(F32), axis=0)
    gains = (gains + swap_cores(gains)).T
    packs = packs[:, :, :640]
    mine = lax.dynamic_slice_in_dim(packs, 2 * core, 2, axis=0)
    theirs = swap_cores(lax.dynamic_slice_in_dim(packs, 2 - 2 * core, 2, axis=0))
    out0 = jnp.where(first, mine, theirs).astype(F32)
    out1 = jnp.where(first, theirs, mine).astype(F32)
    grad_query = jnp.concatenate(
        [out0[0, :, :256], out1[0, :, :256], out0[1, :, :256], out1[1, :, :256]], axis=1
    )
    grad_key = jnp.concatenate([out0[0, :, 256:384], out0[1, :, 256:384]], axis=1)
    grad_value = jnp.concatenate([out1[0, :, 256:384], out1[1, :, 256:384]], axis=1)
    grad_out = jnp.concatenate(
        [out0[0, :, 384:], out1[0, :, 384:], out0[1, :, 384:], out1[1, :, 384:]], axis=1
    )
    return (
        output[None], input_grad[None], gains[0], gains[1],
        grad_query, grad_key, grad_value, grad_out, grad_gate, grad_up, grad_down,
    )


def solution(mesh):
    fine = Mesh(mesh.devices.reshape(2, 4, 2, 4, 2), ("yl", "z", "yh", "x", "tp"))
    shard, ctx = ("yl", "z"), ("yh", "x")
    acts, weight = P(shard, ctx, None), P(shard, "tp")
    return jax.shard_map(
        per_device,
        mesh=fine,
        in_specs=(acts, acts, P(shard, None), P(shard, None), P(shard), P(), P()) + (weight,) * 7,
        out_specs=(acts, acts, P(shard), P(shard)) + (weight,) * 7,
        check_vma=False,
    )
```

time: 734 us -> 579 us (0.79)
  the two profiles are of different devices: /device:TPU:97 before, /device:TPU:9 now
where the time goes in v2:
time: 579 us; the launch traced here: 569 us
  waiting for transfers between devices  213 us (37%)
  local copies, waits for them, and re-layouts  82.3 us (14%)
  matrix products  82 us (14%)
  other arithmetic  71.3 us (12%)
  starting transfers between devices  66.1 us (11%)
  between operations  28.6 us (5%)
  Pallas kernels  26.1 us (5%)
    ppermute x27, waiting for transfers between devices, shift_x(): return lax.ppermute(value, 'x', [(i, (i + hop) % 4) for i in range(4)])  132 us
    dot_general x8, matrix products, mm_nt(): lax.dot_general(left, right, (((1,), (1,)), ((), ())), preferred_element_...  32.1 us
    ppermute x27, starting transfers between devices, shift_x(): return lax.ppermute(value, 'x', [(i, (i + hop) % 4) for i in range(4)])  26.7 us
    dot_general x8, matrix products, mm(): return jnp.dot(left, right, preferred_element_type=F32)  26.4 us
    all_to_all x1, waiting for transfers between devices, gather_shard(): return lax.all_to_all(spread, SHARD, 0, 0).reshape(-1, value.shape[1])  26.1 us
    dot_general x8, matrix products, mm_tn(): lax.dot_general(left, right, (((0,), (0,)), ((), ())), preferred_element_...  23.5 us
    ppermute x4, waiting for transfers between devices, across_y(): return lax.ppermute(value, 'yh', SWAP)  21.4 us
    all_to_all x1, waiting for transfers between devices, per_device(): lax.all_to_all(sums.reshape(16, sixteenth, -1), ('yl', 'z', 'yh'), 0, 0)  17.7 us
  transfers between devices with their start and end apart: 54, of which 25 were waited for; matrix products, arithmetic and copies ran while one was open for 35% of the time, Pallas kernels for 5%

profile of v2, /device:TPU:9, one launch (start us, length us, event | category | flops | bytes accessed | tf_op | source)
XLA Modules:
  0.0 569.4 jit_solution(9448369002178771987)
XLA Ops:
  12.9 2.2 collective-permute-done
  16.9 6.2 %all-to-all-start = ((bf16[8,256,640]{2,1,0:T(8,128)(2,1)}), bf16[8,256,640]{2,1,0:T(8,128)(2,1)S(1)}, u32[]{:S(2)}, u32[]{:S(2)}) async-start(bf16[8,256,640]{2,1,0:T(8,128)(2,1)} %broadcast_in_dim.26), calls=%async_computation | async-start | bytes 5242880 | tf_op jit(solution)/shard_map/all_to_all | solution.py:72
  28.6 26.1 %all-to-all-done = bf16[8,256,640]{2,1,0:T(8,128)(2,1)S(1)} async-done(((bf16[8,256,640]{2,1,0:T(8,128)(2,1)}), bf16[8,256,640]{2,1,0:T(8,128)(2,1)S(1)}, u32[]{:S(2)}, u32[]{:S(2)}) %all-to-all-start) | async-done | bytes 2621472 | tf_op jit(solution)/shard_map/all_to_all | solution.py:72
  62.4 2.6 and_select_fusion.1.bias_ref
  76.0 2.8 collective-permute-start.4
  83.3 2.9 fusion.79
  87.8 2.7 fusion.82
  91.4 2.1 collective-permute-start.2
  93.5 7.5 %collective-permute-done.4 = bf16[128,2048]{1,0:T(8,128)(2,1)} collective-permute-done((bf16[128,2048]{1,0:T(8,128)(2,1)}, bf16[128,2048]{1,0:T(8,128)(2,1)}, u32[]{:S(2)}, u32[]{:S(2)}) %collective-permute-start.4) | collective-permute-done | bytes 524320 | tf_op jit(solution)/shard_map/ppermute | solution.py:53
  101.0 4.6 collective-permute-done.6
  105.6 2.0 multiply_convert_fusion
  111.9 11.2 %shard_map.221 = (f32[512,512]{1,0:T(8,128)S(1)}, bf16[512,512]{1,0:T(8,128)(2,1)S(1)}, f32[4,512,1]{2,1,0:T(8,128)S(1)}) custom-call(bf16[512,512]{1,0:T(8,128)(2,1)S(1)} %get-tuple-element.134.q_ref, bf16[128,2048]{1,0:T(8,128)(2,1)S(1)} %copy.108.kt_ref, bf16[2048,128]{1,0:T(8,128)(2,1)S(1)} %get-tuple-element.103.v_ref, ...), custom_call_target="tpu_custom_call" | custom-call | tf_op jit(solution)/shard_map/pallas_call | solution.py:112
  123.2 2.8 fusion.50
  130.6 10.8 %collective-permute-done.10 = bf16[128,2048]{1,0:T(8,128)(2,1)S(1)} collective-permute-done((bf16[128,2048]{1,0:T(8,128)(2,1)S(1)}, bf16[128,2048]{1,0:T(8,128)(2,1)S(1)}, u32[]{:S(2)}, u32[]{:S(2)}) %collective-permute-start.10) | collective-permute-done | bytes 524320 | tf_op jit(solution)/shard_map/ppermute | solution.py:53
  141.4 2.0 collective-permute-done.8
  143.4 12.3 %collective-permute-done.9 = bf16[128,2048]{1,0:T(8,128)(2,1)S(1)} collective-permute-done((bf16[128,2048]{1,0:T(8,128)(2,1)S(1)}, bf16[128,2048]{1,0:T(8,128)(2,1)S(1)}, u32[]{:S(2)}, u32[]{:S(2)}) %collective-permute-start.9) | collective-permute-done | bytes 524320 | tf_op jit(solution)/shard_map/ppermute | solution.py:53
  162.6 13.5 %all-gather.7.cloned.1.call-done = bf16[2048,768]{1,0:T(8,128)(2,1)} async-done(((bf16[256,768]{1,0:T(8,128)(2,1)}), bf16[2048,768]{1,0:T(8,128)(2,1)}) %all-gather.7.cloned.1.call-update) | async-done | bytes 3145744 | tf_op jit(solution)/shard_map/all_gather | solution.py:221
  177.4 3.5 collective-permute-start.15
  180.8 6.7 %collective-permute-done.13 = bf16[128,2048]{1,0:T(8,128)(2,1)} collective-permute-done((bf16[128,2048]{1,0:T(8,128)(2,1)}, bf16[128,2048]{1,0:T(8,128)(2,1)}, u32[]{:S(2)}, u32[]{:S(2)}) %collective-permute-start.13) | collective-permute-done | bytes 524320 | tf_op jit(solution)/shard_map/ppermute | solution.py:53
  187.5 6.1 %fusion.84 = f32[512,1536]{1,0:T(8,128)S(1)} fusion(bf16[2048,1536]{1,0:T(8,128)(2,1)} %constant_dynamic-update-slice_fusion.10, bf16[128,2048]{1,0:T(8,128)(2,1)} %collective-permute-done.13, bf16[128,2048]{1,0:T(8,128)(2,1)} %collective-permute-done.12, bf16[128,2048]{1,0:T(8,128)(2,1)} %collective-permute-done.11, bf16[128,2048]{1,0:T(8,128)(2,1)} %copy-done.26), kind=kOutput, calls=%fused_computation.317 | convolution fusion | flops 3229614080 | bytes 11534336 | tf_op jit(solution)/shard_map/dot_general | solution.py:27
  193.6 2.3 multiply_convert_fusion.5
  196.4 5.1 fusion.26
  201.5 6.0 %fusion.83 = f32[512,1536]{1,0:T(8,128)S(1)} fusion(bf16[2048,1536]{1,0:T(8,128)(2,1)} %collective-permute-done.14, bf16[128,2048]{1,0:T(8,128)(2,1)} %collective-permute-done.13, bf16[128,2048]{1,0:T(8,128)(2,1)} %collective-permute-done.12, bf16[128,2048]{1,0:T(8,128)(2,1)} %collective-permute-done.11, bf16[128,2048]{1,0:T(8,128)(2,1)S(1)} %copy-done.27), kind=kOutput, calls=%fused_computation.316 | convolution fusion | flops 3229614080 | bytes 11534336 | tf_op jit(solution)/shard_map/dot_general | solution.py:27
  207.5 2.3 multiply_convert_fusion.3
  209.8 7.4 %fusion.114 = (bf16[512,2048]{1,0:T(8,128)(2,1)S(1)}, f32[512,2048]{1,0:T(8,128)S(1)}) fusion(f32[512,2048]{1,0:T(8,128)} %fusion.26, bf16[2048,1536]{1,0:T(8,128)(2,1)} %collective-permute-done.14, bf16[512,768]{1,0:T(8,128)(2,1)S(1)} %get-tuple-element.43, bf16[512,768]{1,0:T(8,128)(2,1)S(1)} %get-tuple-element.42), kind=kOutput, calls=%fused_computation.342 | convolution fusion | flops 3226468352 | bytes 18350080 | tf_op jit(solution)/shard_map/dot_general | solution.py:31
  222.5 3.1 collective-permute-start.18
  227.1 9.0 %collective-permute-done.16 = bf16[128,2048]{1,0:T(8,128)(2,1)S(1)} collective-permute-done((bf16[128,2048]{1,0:T(8,128)(2,1)S(1)}, bf16[128,2048]{1,0:T(8,128)(2,1)S(1)}, u32[]{:S(2)}, u32[]{:S(2)}) %collective-permute-start.16) | collective-permute-done | bytes 524320 | tf_op jit(solution)/shard_map/ppermute | solution.py:53
  236.1 11.5 %collective-permute-done.17 = bf16[128,2048]{1,0:T(8,128)(2,1)S(1)} collective-permute-done((bf16[128,2048]{1,0:T(8,128)(2,1)S(1)}, bf16[128,2048]{1,0:T(8,128)(2,1)S(1)}, u32[]{:S(2)}, u32[]{:S(2)}) %collective-permute-start.17) | collective-permute-done | bytes 524320 | tf_op jit(solution)/shard_map/ppermute | solution.py:53
  250.4 5.7 convolution_convert_fusion
  256.6 3.7 add_convert_fusion.1
  260.9 3.4 and_select_fusion.bias_ref
  264.5 2.6 copy.109
  268.9 4.1 fusion.115
  278.9 3.9 convolution_add_fusion.3
  282.8 7.5 %collective-permute-done.25 = bf16[128,2048]{1,0:T(8,128)(2,1)S(1)} collective-permute-done((bf16[128,2048]{1,0:T(8,128)(2,1)S(1)}, bf16[128,2048]{1,0:T(8,128)(2,1)S(1)}, u32[]{:S(2)}, u32[]{:S(2)}) %collective-permute-start.25) | collective-permute-done | bytes 524320 | tf_op jit(solution)/shard_map/ppermute | solution.py:53
  292.1 11.7 %collective-permute-done.27 = bf16[128,2048]{1,0:T(8,128)(2,1)S(1)} collective-permute-done((bf16[128,2048]{1,0:T(8,128)(2,1)S(1)}, bf16[128,2048]{1,0:T(8,128)(2,1)S(1)}, u32[]{:S(2)}, u32[]{:S(2)}) %collective-permute-start.27) | collective-permute-done | bytes 524320 | tf_op jit(solution)/shard_map/ppermute | solution.py:53
  305.4 7.5 %add_convert_fusion = bf16[2048,1536]{1,0:T(8,128)(2,1)} fusion(bf16[2048,1536]{1,0:T(8,128)(2,1)} %collective-permute-done.20, bf16[512,2048]{1,0:T(8,128)(2,1)S(1)} %copy-done.35, bf16[512,768]{1,0:T(8,128)(2,1)S(1)} %copy-done.64, bf16[512,768]{1,0:T(8,128)(2,1)S(1)} %copy-done.62), kind=kOutput, calls=%fused_computation | convolution fusion | flops 3233808384 | bytes 16252928 | tf_op jit(solution)/shard_map/dot_general | solution.py:35
  322.9 2.5 convert.47
  328.2 2.7 collective-permute-start.23
  332.8 2.1 convolution_convert_fusion.4
  336.0 2.0 copy.111.do_ref
  339.1 14.9 %shard_map.222 = (f32[512,512]{1,0:T(8,128)S(1)}, f32[2048,128]{1,0:T(8,128)S(1)}, f32[2048,128]{1,0:T(8,128)}) custom-call(bf16[512,512]{1,0:T(8,128)(2,1)S(1)} %get-tuple-element.134.q_ref, bf16[512,512]{1,0:T(8,128)(2,1)S(1)} %copy.110.qt_ref, bf16[512,512]{1,0:T(8,128)(2,1)S(1)} %copy-done, bf16[512,512]{1,0:T(8,128)(2,1)S(1)} %get-tuple-element.131.dot_ref, ...), custom_call_target="tpu_custom_call" | custom-call | tf_op jit(solution)/shard_map/pallas_call | solution.py:162
  367.5 2.9 add_convert_fusion.4
  373.2 3.5 collective-permute-done.31
  378.4 8.7 %collective-permute-done.33 = bf16[256,768]{1,0:T(8,128)(2,1)S(1)} collective-permute-done((bf16[256,768]{1,0:T(8,128)(2,1)S(1)}, bf16[256,768]{1,0:T(8,128)(2,1)S(1)}, u32[]{:S(2)}, u32[]{:S(2)}) %collective-permute-start.33) | collective-permute-done | bytes 393248 | tf_op jit(solution)/shard_map/ppermute | solution.py:53
  398.9 5.6 multiply_reduce_fusion
  408.5 4.4 all-to-all-start.1
  413.0 2.5 fusion.90
  416.5 2.3 collective-permute-start.36
  431.1 3.3 concatenate.225
  434.3 3.3 concatenate.226
  437.6 4.8 collective-permute-done.35
  442.4 2.0 fusion.10
  444.5 2.7 fusion.14
  447.7 17.7 %all-to-all-done.1 = bf16[16,128,768]{1,2,0:T(8,128)(2,1)S(1)} async-done(((bf16[16,128,768]{1,2,0:T(8,128)(2,1)}), bf16[16,128,768]{1,2,0:T(8,128)(2,1)S(1)}, u32[]{:S(2)}, u32[]{:S(2)}) %all-to-all-start.1) | async-done | bytes 3145760 | tf_op jit(solution)/shard_map/all_to_all | solution.py:375
  473.6 5.0 all-to-all-start.2
  480.9 21.4 %collective-permute-done.42 = bf16[256,1536]{1,0:T(8,128)(2,1)} collective-permute-done((bf16[256,1536]{1,0:T(8,128)(2,1)}, bf16[256,1536]{1,0:T(8,128)(2,1)}, u32[]{:S(2)}, u32[]{:S(2)}) %collective-permute-start.42) | collective-permute-done | bytes 786464 | tf_op jit(solution)/shard_map/ppermute | solution.py:43
  502.3 2.2 add_convert_fusion.3
  507.8 5.2 collective-permute-start.40
  514.9 4.5 collective-permute-done.43
  521.0 21.7 %collective-permute-done.45 = bf16[256,1536]{1,0:T(8,128)(2,1)} collective-permute-done((bf16[256,1536]{1,0:T(8,128)(2,1)}, bf16[256,1536]{1,0:T(8,128)(2,1)}, u32[]{:S(2)}, u32[]{:S(2)}) %collective-permute-start.45) | collective-permute-done | bytes 786464 | tf_op jit(solution)/shard_map/ppermute | solution.py:53
  542.6 2.2 select_select_fusion
  549.0 2.4 concatenate.223
  553.2 2.3 concatenate.221
  (405 shorter events, 158.7 us)
Async XLA Ops:
  7.2 61.1 %all-gather.9.cloned.1.call-start = ((), (), s32[]{:S(2)}) async-start(), calls=%async_computation.9 | async-start | bytes 2621440 | tf_op jit(solution)/shard_map/all_gather | solution.py:191
  11.6 3.5 collective-permute-start
  16.9 37.8 %all-to-all-start = ((bf16[8,256,640]{2,1,0:T(8,128)(2,1)}), bf16[8,256,640]{2,1,0:T(8,128)(2,1)S(1)}, u32[]{:S(2)}, u32[]{:S(2)}) async-start(bf16[8,256,640]{2,1,0:T(8,128)(2,1)} %broadcast_in_dim.26), calls=%async_computation | async-start | bytes 5242880 | tf_op jit(solution)/shard_map/all_to_all | solution.py:72
  23.2 135.5 %all-gather.5.cloned.1.call-start = ((), (), s32[]{:S(2)}) async-start(), calls=%async_computation.5 | async-start | bytes 7077888 | tf_op jit(solution)/shard_map/all_gather | solution.py:223
  26.1 31.3 %copy-start.52 = (s32[1,2048]{1,0:T(1,128)S(1)}, s32[1,2048]{1,0:T(1,128)}, u32[]{:S(2)}) copy-start(s32[1,2048]{1,0:T(1,128)} %param.16) | copy-start | bytes 24580
  26.1 31.3 %copy-start.53 = (s32[1,2048]{1,0:T(1,128)S(1)}, s32[1,2048]{1,0:T(1,128)}, u32[]{:S(2)}) copy-start(s32[1,2048]{1,0:T(1,128)} %param.17) | copy-start | bytes 24580
  54.7 28.6 %copy-start.10 = (bf16[8,256,640]{2,1,0:T(8,128)(2,1)}, bf16[8,256,640]{2,1,0:T(8,128)(2,1)S(1)}, u32[]{:S(2)}) copy-start(bf16[8,256,640]{2,1,0:T(8,128)(2,1)S(1)} %all-to-all-done) | copy-start | bytes 7864324
  56.6 119.5 %all-gather.7.cloned.1.call-start = ((), (), s32[]{:S(2)}) async-start(), calls=%async_computation.6 | async-start | bytes 3538944 | tf_op jit(solution)/shard_map/all_gather | solution.py:221
  62.4 47.5 %copy-start.17 = (f32[512,64]{1,0:T(8,128)}, f32[512,64]{1,0:T(8,128)S(1)}, u32[]{:S(2)}) copy-start(f32[512,64]{1,0:T(8,128)S(1)} %get-tuple-element.163) | copy-start | bytes 393220
  67.4 19.0 %collective-permute-start.1 = (bf16[2048,384]{1,0:T(8,128)(2,1)}, bf16[2048,384]{1,0:T(8,128)(2,1)}, u32[]{:S(2)}, u32[]{:S(2)}) collective-permute-start(bf16[2048,384]{1,0:T(8,128)(2,1)} %slice.625), channel_id=1, source_target_pairs={{0,1},{1,0},{2,3},{3,2},{4,5},{5,4},{6,7},{7,6},{8,9},{9,8},{10,11... | collective-permute-start | bytes 4718600 | tf_op jit(solution)/shard_map/ppermute | solution.py:39
  68.2 57.8 %collective-permute-start.7 = (bf16[2048,256]{1,0:T(8,128)(2,1)}, bf16[2048,256]{1,0:T(8,128)(2,1)}, u32[]{:S(2)}, u32[]{:S(2)}) collective-permute-start(bf16[2048,256]{1,0:T(8,128)(2,1)} %slice.650), channel_id=1, source_target_pairs={{0,1},{1,0},{2,3},{3,2},{4,5},{5,4},{6,7},{7,6},{8,9},{9,8},{10,11... | collective-permute-start | bytes 3145736 | tf_op jit(solution)/shard_map/ppermute | solution.py:39
  76.0 25.1 %collective-permute-start.4 = (bf16[128,2048]{1,0:T(8,128)(2,1)}, bf16[128,2048]{1,0:T(8,128)(2,1)}, u32[]{:S(2)}, u32[]{:S(2)}) collective-permute-start(bf16[128,2048]{1,0:T(8,128)(2,1)} %constant_dynamic-update-slice_fusion.13), channel_id=1, source_target_pairs={{0,6},{2,0},{4,2},{6,4},{1,7},{3,1},{5,3},{7,5},{8,14},{10,8},{12,... | collective-permute-start | bytes 1572872 | tf_op jit(solution)/shard_map/ppermute | solution.py:53
  78.8 22.3 %collective-permute-start.5 = (bf16[128,2048]{1,0:T(8,128)(2,1)}, bf16[128,2048]{1,0:T(8,128)(2,1)}, u32[]{:S(2)}, u32[]{:S(2)}) collective-permute-start(bf16[128,2048]{1,0:T(8,128)(2,1)} %constant_dynamic-update-slice_fusion.13), channel_id=1, source_target_pairs={{0,4},{2,6},{4,0},{6,2},{1,5},{3,7},{5,1},{7,3},{8,12},{10,14},{12... | collective-permute-start | bytes 1572872 | tf_op jit(solution)/shard_map/ppermute | solution.py:53
  79.0 26.6 %collective-permute-start.6 = (bf16[128,2048]{1,0:T(8,128)(2,1)}, bf16[128,2048]{1,0:T(8,128)(2,1)}, u32[]{:S(2)}, u32[]{:S(2)}) collective-permute-start(bf16[128,2048]{1,0:T(8,128)(2,1)} %constant_dynamic-update-slice_fusion.13), channel_id=1, source_target_pairs={{0,2},{2,4},{4,6},{6,0},{1,3},{3,5},{5,7},{7,1},{8,10},{10,12},{12... | collective-permute-start | bytes 1572872 | tf_op jit(solution)/shard_map/ppermute | solution.py:53
  82.5 231.6 %reduce-scatter.3.cloned.1.call-start = ((), (), s32[]{:S(2)}) async-start(), calls=%async_computation.7 | async-start | bytes 3538944 | tf_op jit(solution)/shard_map/reduce_scatter | solution.py:323
  91.4 17.5 %collective-permute-start.2 = (bf16[512,256]{1,0:T(8,128)(2,1)S(1)}, bf16[512,256]{1,0:T(8,128)(2,1)S(1)}, u32[]{:S(2)}, u32[]{:S(2)}) collective-permute-start(bf16[512,256]{1,0:T(8,128)(2,1)S(1)} %pad_maximum_fusion.21), channel_id=1, source_target_pairs={{0,8},{8,0},{1,9},{9,1},{2,10},{10,2},{3,11},{11,3},{4,12},{12,4},... | collective-permute-start | bytes 786440 | tf_op jit(solution)/shard_map/ppermute | solution.py:43
  109.0 2.3 collective-permute-start.3
  128.0 27.7 %copy-start.20 = (bf16[1,256,2048]{2,1,0:T(8,128)(2,1)S(1)}, bf16[1,256,2048]{2,1,0:T(8,128)(2,1)}, u32[]{:S(2)}) copy-start(bf16[1,256,2048]{2,1,0:T(8,128)(2,1)} %param.14) | copy-start | bytes 3145732
  128.2 13.2 %collective-permute-start.10 = (bf16[128,2048]{1,0:T(8,128)(2,1)S(1)}, bf16[128,2048]{1,0:T(8,128)(2,1)S(1)}, u32[]{:S(2)}, u32[]{:S(2)}) collective-permute-start(bf16[128,2048]{1,0:T(8,128)(2,1)S(1)} %get-tuple-element.66), channel_id=1, source_target_pairs={{0,6},{2,0},{4,2},{6,4},{1,7},{3,1},{5,3},{7,5},{8,14},{10,8},{12,... | collective-permute-start | bytes 1572872 | tf_op jit(solution)/shard_map/ppermute | solution.py:53
  129.1 14.4 %collective-permute-start.8 = (bf16[128,2048]{1,0:T(8,128)(2,1)S(1)}, bf16[128,2048]{1,0:T(8,128)(2,1)S(1)}, u32[]{:S(2)}, u32[]{:S(2)}) collective-permute-start(bf16[128,2048]{1,0:T(8,128)(2,1)S(1)} %get-tuple-element.65), channel_id=1, source_target_pairs={{0,4},{2,6},{4,0},{6,2},{1,5},{3,7},{5,1},{7,3},{8,12},{10,14},{12... | collective-permute-start | bytes 1572872 | tf_op jit(solution)/shard_map/ppermute | solution.py:53
  130.6 25.1 %collective-permute-start.9 = (bf16[128,2048]{1,0:T(8,128)(2,1)S(1)}, bf16[128,2048]{1,0:T(8,128)(2,1)S(1)}, u32[]{:S(2)}, u32[]{:S(2)}) collective-permute-start(bf16[128,2048]{1,0:T(8,128)(2,1)S(1)} %get-tuple-element.67), channel_id=1, source_target_pairs={{0,2},{2,4},{4,6},{6,0},{1,3},{3,5},{5,7},{7,1},{8,10},{10,12},{12... | collective-permute-start | bytes 1572872 | tf_op jit(solution)/shard_map/ppermute | solution.py:53
  156.3 91.4 %copy-start.7 = (f32[128,2048]{1,0:T(8,128)}, f32[128,2048]{1,0:T(8,128)S(1)}, u32[]{:S(2)}) copy-start(f32[128,2048]{1,0:T(8,128)S(1)} %get-tuple-element.39) | copy-start | bytes 3145732
  159.9 41.6 %collective-permute-start.14 = (bf16[2048,1536]{1,0:T(8,128)(2,1)}, bf16[2048,1536]{1,0:T(8,128)(2,1)}, u32[]{:S(2)}, u32[]{:S(2)}) collective-permute-start(bf16[2048,1536]{1,0:T(8,128)(2,1)} %constant_dynamic-update-slice_fusion.10), channel_id=1, source_target_pairs={{0,1},{1,0},{2,3},{3,2},{4,5},{5,4},{6,7},{7,6},{8,9},{9,8},{10,11... | collective-permute-start | bytes 18874376 | tf_op jit(solution)/shard_map/ppermute | solution.py:39
  160.3 20.6 %collective-permute-start.11 = (bf16[128,2048]{1,0:T(8,128)(2,1)}, bf16[128,2048]{1,0:T(8,128)(2,1)}, u32[]{:S(2)}, u32[]{:S(2)}) collective-permute-start(bf16[128,2048]{1,0:T(8,128)(2,1)} %copy-done.26), channel_id=1, source_target_pairs={{0,6},{2,0},{4,2},{6,4},{1,7},{3,1},{5,3},{7,5},{8,14},{10,8},{12,... | collective-permute-start | bytes 1572872 | tf_op jit(solution)/shard_map/ppermute | solution.py:53
  160.6 20.2 %collective-permute-start.12 = (bf16[128,2048]{1,0:T(8,128)(2,1)}, bf16[128,2048]{1,0:T(8,128)(2,1)}, u32[]{:S(2)}, u32[]{:S(2)}) collective-permute-start(bf16[128,2048]{1,0:T(8,128)(2,1)} %copy-done.26), channel_id=1, source_target_pairs={{0,4},{2,6},{4,0},{6,2},{1,5},{3,7},{5,1},{7,3},{8,12},{10,14},{12... | collective-permute-start | bytes 1572872 | tf_op jit(solution)/shard_map/ppermute | solution.py:53
  162.1 25.4 %collective-permute-start.13 = (bf16[128,2048]{1,0:T(8,128)(2,1)}, bf16[128,2048]{1,0:T(8,128)(2,1)}, u32[]{:S(2)}, u32[]{:S(2)}) collective-permute-start(bf16[128,2048]{1,0:T(8,128)(2,1)} %copy-done.26), channel_id=1, source_target_pairs={{0,2},{2,4},{4,6},{6,0},{1,3},{3,5},{5,7},{7,1},{8,10},{10,12},{12... | collective-permute-start | bytes 1572872 | tf_op jit(solution)/shard_map/ppermute | solution.py:53
  177.4 30.1 %collective-permute-start.15 = (bf16[2048,768]{1,0:T(8,128)(2,1)}, bf16[2048,768]{1,0:T(8,128)(2,1)S(1)}, u32[]{:S(2)}, u32[]{:S(2)}) collective-permute-start(bf16[2048,768]{1,0:T(8,128)(2,1)} %constant_dynamic-update-slice_fusion.8), channel_id=1, source_target_pairs={{0,1},{1,0},{2,3},{3,2},{4,5},{5,4},{6,7},{7,6},{8,9},{9,8},{10,11... | collective-permute-start | bytes 9437192 | tf_op jit(solution)/shard_map/ppermute | solution.py:39
  196.0 60.6 %copy-start.60 = (bf16[512,768]{1,0:T(8,128)(2,1)}, bf16[512,768]{1,0:T(8,128)(2,1)S(1)}, u32[]{:S(2)}) copy-start(bf16[512,768]{1,0:T(8,128)(2,1)S(1)} %get-tuple-element.53) | copy-start | bytes 2359300
  220.3 36.3 %collective-permute-start.19 = (bf16[2048,768]{1,0:T(8,128)(2,1)S(1)}, bf16[2048,768]{1,0:T(8,128)(2,1)S(1)}, u32[]{:S(2)}, u32[]{:S(2)}) collective-permute-start(bf16[2048,768]{1,0:T(8,128)(2,1)S(1)} %convolution_convert_fusion.1), channel_id=1, source_target_pairs={{0,1},{1,0},{2,3},{3,2},{4,5},{5,4},{6,7},{7,6},{8,9},{9,8},{10,11... | collective-permute-start | bytes 9437192 | tf_op jit(solution)/shard_map/ppermute | solution.py:39
  221.0 15.2 %collective-permute-start.16 = (bf16[128,2048]{1,0:T(8,128)(2,1)S(1)}, bf16[128,2048]{1,0:T(8,128)(2,1)S(1)}, u32[]{:S(2)}, u32[]{:S(2)}) collective-permute-start(bf16[128,2048]{1,0:T(8,128)(2,1)S(1)} %get-tuple-element.62), channel_id=1, source_target_pairs={{0,4},{2,6},{4,0},{6,2},{1,5},{3,7},{5,1},{7,3},{8,12},{10,14},{12... | collective-permute-start | bytes 1572872 | tf_op jit(solution)/shard_map/ppermute | solution.py:53
  222.5 25.2 %collective-permute-start.17 = (bf16[128,2048]{1,0:T(8,128)(2,1)S(1)}, bf16[128,2048]{1,0:T(8,128)(2,1)S(1)}, u32[]{:S(2)}, u32[]{:S(2)}) collective-permute-start(bf16[128,2048]{1,0:T(8,128)(2,1)S(1)} %get-tuple-element.64), channel_id=1, source_target_pairs={{0,2},{2,4},{4,6},{6,0},{1,3},{3,5},{5,7},{7,1},{8,10},{10,12},{12... | collective-permute-start | bytes 1572872 | tf_op jit(solution)/shard_map/ppermute | solution.py:53
  222.5 25.2 %collective-permute-start.18 = (bf16[128,2048]{1,0:T(8,128)(2,1)S(1)}, bf16[128,2048]{1,0:T(8,128)(2,1)S(1)}, u32[]{:S(2)}, u32[]{:S(2)}) collective-permute-start(bf16[128,2048]{1,0:T(8,128)(2,1)S(1)} %get-tuple-element.63), channel_id=1, source_target_pairs={{0,6},{2,0},{4,2},{6,4},{1,7},{3,1},{5,3},{7,5},{8,14},{10,8},{12,... | collective-permute-start | bytes 1572872 | tf_op jit(solution)/shard_map/ppermute | solution.py:53
  256.1 49.3 %collective-permute-start.20 = (bf16[2048,1536]{1,0:T(8,128)(2,1)}, bf16[2048,1536]{1,0:T(8,128)(2,1)}, u32[]{:S(2)}, u32[]{:S(2)}) collective-permute-start(bf16[2048,1536]{1,0:T(8,128)(2,1)} %convolution_convert_fusion), channel_id=1, source_target_pairs={{0,1},{1,0},{2,3},{3,2},{4,5},{5,4},{6,7},{7,6},{8,9},{9,8},{10,11... | collective-permute-start | bytes 18874376 | tf_op jit(solution)/shard_map/ppermute | solution.py:39
  260.3 205.6 %reduce-scatter.5.cloned.1.call-start = ((), (), s32[]{:S(2)}) async-start(), calls=%async_computation.8 | async-start | bytes 7077888 | tf_op jit(solution)/shard_map/reduce_scatter | solution.py:323
  276.5 13.7 %collective-permute-start.25 = (bf16[128,2048]{1,0:T(8,128)(2,1)S(1)}, bf16[128,2048]{1,0:T(8,128)(2,1)S(1)}, u32[]{:S(2)}, u32[]{:S(2)}) collective-permute-start(bf16[128,2048]{1,0:T(8,128)(2,1)S(1)} %constant_dynamic-update-slice_fusion.4), channel_id=1, source_target_pairs={{0,6},{2,0},{4,2},{6,4},{1,7},{3,1},{5,3},{7,5},{8,14},{10,8},{12,... | collective-permute-start | bytes 1572872 | tf_op jit(solution)/shard_map/ppermute | solution.py:53
  277.2 14.9 %collective-permute-start.26 = (bf16[128,2048]{1,0:T(8,128)(2,1)S(1)}, bf16[128,2048]{1,0:T(8,128)(2,1)S(1)}, u32[]{:S(2)}, u32[]{:S(2)}) collective-permute-start(bf16[128,2048]{1,0:T(8,128)(2,1)S(1)} %constant_dynamic-update-slice_fusion.4), channel_id=1, source_target_pairs={{0,4},{2,6},{4,0},{6,2},{1,5},{3,7},{5,1},{7,3},{8,12},{10,14},{12... | collective-permute-start | bytes 1572872 | tf_op jit(solution)/shard_map/ppermute | solution.py:53
  278.3 25.5 %collective-permute-start.27 = (bf16[128,2048]{1,0:T(8,128)(2,1)S(1)}, bf16[128,2048]{1,0:T(8,128)(2,1)S(1)}, u32[]{:S(2)}, u32[]{:S(2)}) collective-permute-start(bf16[128,2048]{1,0:T(8,128)(2,1)S(1)} %constant_dynamic-update-slice_fusion.4), channel_id=1, source_target_pairs={{0,2},{2,4},{4,6},{6,0},{1,3},{3,5},{5,7},{7,1},{8,10},{10,12},{12... | collective-permute-start | bytes 1572872 | tf_op jit(solution)/shard_map/ppermute | solution.py:53
  282.8 22.6 %copy-start.35 = (bf16[512,2048]{1,0:T(8,128)(2,1)S(1)}, bf16[512,2048]{1,0:T(8,128)(2,1)}, u32[]{:S(2)}) copy-start(bf16[512,2048]{1,0:T(8,128)(2,1)} %copy-done.34) | copy-start | bytes 6291460
  282.8 22.6 %copy-start.62 = (bf16[512,768]{1,0:T(8,128)(2,1)S(1)}, bf16[512,768]{1,0:T(8,128)(2,1)}, u32[]{:S(2)}) copy-start(bf16[512,768]{1,0:T(8,128)(2,1)} %copy-done.61) | copy-start | bytes 2359300
  319.7 44.4 %collective-permute-start.30 = (bf16[256,768]{1,0:T(8,128)(2,1)}, bf16[256,768]{1,0:T(8,128)(2,1)}, u32[]{:S(2)}, u32[]{:S(2)}) collective-permute-start(bf16[256,768]{1,0:T(8,128)(2,1)} %constant_dynamic-update-slice_fusion.2), channel_id=1, source_target_pairs={{0,8},{8,0},{1,9},{9,1},{2,10},{10,2},{3,11},{11,3},{4,12},{12,4},... | collective-permute-start | bytes 1179656 | tf_op jit(solution)/shard_map/ppermute | solution.py:43
  326.6 39.3 %collective-permute-start.21 = (bf16[128,2048]{1,0:T(8,128)(2,1)}, bf16[128,2048]{1,0:T(8,128)(2,1)}, u32[]{:S(2)}, u32[]{:S(2)}) collective-permute-start(bf16[128,2048]{1,0:T(8,128)(2,1)} %get-tuple-element.59), channel_id=1, source_target_pairs={{0,4},{2,6},{4,0},{6,2},{1,5},{3,7},{5,1},{7,3},{8,12},{10,14},{12... | collective-permute-start | bytes 1572872 | tf_op jit(solution)/shard_map/ppermute | solution.py:53
  328.2 37.8 %collective-permute-start.22 = (bf16[128,2048]{1,0:T(8,128)(2,1)}, bf16[128,2048]{1,0:T(8,128)(2,1)}, u32[]{:S(2)}, u32[]{:S(2)}) collective-permute-start(bf16[128,2048]{1,0:T(8,128)(2,1)} %get-tuple-element.61), channel_id=1, source_target_pairs={{0,2},{2,4},{4,6},{6,0},{1,3},{3,5},{5,7},{7,1},{8,10},{10,12},{12... | collective-permute-start | bytes 1572872 | tf_op jit(solution)/shard_map/ppermute | solution.py:53
  328.2 38.5 %collective-permute-start.23 = (bf16[128,2048]{1,0:T(8,128)(2,1)}, bf16[128,2048]{1,0:T(8,128)(2,1)}, u32[]{:S(2)}, u32[]{:S(2)}) collective-permute-start(bf16[128,2048]{1,0:T(8,128)(2,1)} %get-tuple-element.60), channel_id=1, source_target_pairs={{0,6},{2,0},{4,2},{6,4},{1,7},{3,1},{5,3},{7,5},{8,14},{10,8},{12,... | collective-permute-start | bytes 1572872 | tf_op jit(solution)/shard_map/ppermute | solution.py:53
  361.0 10.7 %collective-permute-start.28 = (bf16[1024,256]{1,0:T(8,128)(2,1)}, bf16[1024,256]{1,0:T(8,128)(2,1)S(1)}, u32[]{:S(2)}, u32[]{:S(2)}) collective-permute-start(bf16[1024,256]{1,0:T(8,128)(2,1)} %pad_maximum_fusion.14), channel_id=1, source_target_pairs={{0,1},{1,0},{2,3},{3,2},{4,5},{5,4},{6,7},{7,6},{8,9},{9,8},{10,11... | collective-permute-start | bytes 1572872 | tf_op jit(solution)/shard_map/ppermute | solution.py:39
  364.1 40.6 %collective-permute-start.39 = (bf16[2048,256]{0,1:T(8,128)(2,1)}, bf16[2048,256]{0,1:T(8,128)(2,1)S(1)}, u32[]{:S(2)}, u32[]{:S(2)}) collective-permute-start(bf16[2048,256]{0,1:T(8,128)(2,1)} %convolution_convert_fusion.3), channel_id=1, source_target_pairs={{0,1},{1,0},{2,3},{3,2},{4,5},{5,4},{6,7},{7,6},{8,9},{9,8},{10,11... | collective-permute-start | bytes 3145736 | tf_op jit(solution)/shard_map/ppermute | solution.py:39
  365.9 10.9 %collective-permute-start.31 = (bf16[256,768]{1,0:T(8,128)(2,1)S(1)}, bf16[256,768]{1,0:T(8,128)(2,1)S(1)}, u32[]{:S(2)}, u32[]{:S(2)}) collective-permute-start(bf16[256,768]{1,0:T(8,128)(2,1)S(1)} %add_convert_fusion.5), channel_id=1, source_target_pairs={{0,6},{2,0},{4,2},{6,4},{1,7},{3,1},{5,3},{7,5},{8,14},{10,8},{12,... | collective-permute-start | bytes 1179656 | tf_op jit(solution)/shard_map/ppermute | solution.py:53
  366.0 12.4 %collective-permute-start.32 = (bf16[256,768]{1,0:T(8,128)(2,1)S(1)}, bf16[256,768]{1,0:T(8,128)(2,1)S(1)}, u32[]{:S(2)}, u32[]{:S(2)}) collective-permute-start(bf16[256,768]{1,0:T(8,128)(2,1)S(1)} %add_convert_fusion.5), channel_id=1, source_target_pairs={{0,4},{2,6},{4,0},{6,2},{1,5},{3,7},{5,1},{7,3},{8,12},{10,14},{12... | collective-permute-start | bytes 1179656 | tf_op jit(solution)/shard_map/ppermute | solution.py:53
  366.7 20.5 %collective-permute-start.33 = (bf16[256,768]{1,0:T(8,128)(2,1)S(1)}, bf16[256,768]{1,0:T(8,128)(2,1)S(1)}, u32[]{:S(2)}, u32[]{:S(2)}) collective-permute-start(bf16[256,768]{1,0:T(8,128)(2,1)S(1)} %add_convert_fusion.5), channel_id=1, source_target_pairs={{0,2},{2,4},{4,6},{6,0},{1,3},{3,5},{5,7},{7,1},{8,10},{10,12},{12... | collective-permute-start | bytes 1179656 | tf_op jit(solution)/shard_map/ppermute | solution.py:53
  371.8 20.4 %collective-permute-start.29 = (bf16[512,256]{1,0:T(8,128)(2,1)S(1)}, bf16[512,256]{1,0:T(8,128)(2,1)S(1)}, u32[]{:S(2)}, u32[]{:S(2)}) collective-permute-start(bf16[512,256]{1,0:T(8,128)(2,1)S(1)} %slice.931), channel_id=1, source_target_pairs={{0,8},{8,0},{1,9},{9,1},{2,10},{10,2},{3,11},{11,3},{4,12},{12,4},... | collective-permute-start | bytes 786440 | tf_op jit(solution)/shard_map/ppermute | solution.py:43
  395.9 9.5 %collective-permute-start.38 = (bf16[2048,384]{0,1:T(8,128)(2,1)S(1)}, bf16[2048,384]{0,1:T(8,128)(2,1)S(1)}, u32[]{:S(2)}, u32[]{:S(2)}) collective-permute-start(bf16[2048,384]{0,1:T(8,128)(2,1)S(1)} %convolution_convert_fusion.2), channel_id=1, source_target_pairs={{0,1},{1,0},{2,3},{3,2},{4,5},{5,4},{6,7},{7,6},{8,9},{9,8},{10,11... | collective-permute-start | bytes 4718600 | tf_op jit(solution)/shard_map/ppermute | solution.py:39
  408.5 56.8 %all-to-all-start.1 = ((bf16[16,128,768]{1,2,0:T(8,128)(2,1)}), bf16[16,128,768]{1,2,0:T(8,128)(2,1)S(1)}, u32[]{:S(2)}, u32[]{:S(2)}) async-start(bf16[16,128,768]{1,2,0:T(8,128)(2,1)} %copy_bitcast_fusion), calls=%async_computation.2 | async-start | bytes 6291456 | tf_op jit(solution)/shard_map/all_to_all | solution.py:375
  415.5 22.1 %collective-permute-start.34 = (bf16[128,2048]{1,0:T(8,128)(2,1)}, bf16[128,2048]{1,0:T(8,128)(2,1)}, u32[]{:S(2)}, u32[]{:S(2)}) collective-permute-start(bf16[128,2048]{1,0:T(8,128)(2,1)} %get-tuple-element.54), channel_id=1, source_target_pairs={{0,4},{2,6},{4,0},{6,2},{1,5},{3,7},{5,1},{7,3},{8,12},{10,14},{12... | collective-permute-start | bytes 1572872 | tf_op jit(solution)/shard_map/ppermute | solution.py:53
  416.1 26.3 %collective-permute-start.35 = (bf16[128,2048]{1,0:T(8,128)(2,1)}, bf16[128,2048]{1,0:T(8,128)(2,1)}, u32[]{:S(2)}, u32[]{:S(2)}) collective-permute-start(bf16[128,2048]{1,0:T(8,128)(2,1)} %get-tuple-element.56), channel_id=1, source_target_pairs={{0,2},{2,4},{4,6},{6,0},{1,3},{3,5},{5,7},{7,1},{8,10},{10,12},{12... | collective-permute-start | bytes 1572872 | tf_op jit(solution)/shard_map/ppermute | solution.py:53
  416.5 25.9 %collective-permute-start.36 = (bf16[128,2048]{1,0:T(8,128)(2,1)}, bf16[128,2048]{1,0:T(8,128)(2,1)}, u32[]{:S(2)}, u32[]{:S(2)}) collective-permute-start(bf16[128,2048]{1,0:T(8,128)(2,1)} %get-tuple-element.55), channel_id=1, source_target_pairs={{0,6},{2,0},{4,2},{6,4},{1,7},{3,1},{5,3},{7,5},{8,14},{10,8},{12,... | collective-permute-start | bytes 1572872 | tf_op jit(solution)/shard_map/ppermute | solution.py:53
  418.8 51.5 %collective-permute-start.24 = (bf16[128,2048]{1,0:T(8,128)(2,1)}, bf16[128,2048]{1,0:T(8,128)(2,1)}, u32[]{:S(2)}, u32[]{:S(2)}) collective-permute-start(bf16[128,2048]{1,0:T(8,128)(2,1)} %get-tuple-element.33), channel_id=1, source_target_pairs={{0,1},{1,0},{2,3},{3,2},{4,5},{5,4},{6,7},{7,6},{8,9},{9,8},{10,11... | collective-permute-start | bytes 1572872 | tf_op jit(solution)/shard_map/ppermute | solution.py:39
  447.2 32.4 %collective-permute-start.37 = (bf16[128,2048]{1,0:T(8,128)(2,1)}, bf16[128,2048]{1,0:T(8,128)(2,1)}, u32[]{:S(2)}, u32[]{:S(2)}) collective-permute-start(bf16[128,2048]{1,0:T(8,128)(2,1)} %fusion.14), channel_id=1, source_target_pairs={{0,1},{1,0},{2,3},{3,2},{4,5},{5,4},{6,7},{7,6},{8,9},{9,8},{10,11... | collective-permute-start | bytes 1572872 | tf_op jit(solution)/shard_map/ppermute | solution.py:39
  470.3 32.0 %collective-permute-start.42 = (bf16[256,1536]{1,0:T(8,128)(2,1)}, bf16[256,1536]{1,0:T(8,128)(2,1)}, u32[]{:S(2)}, u32[]{:S(2)}) collective-permute-start(bf16[256,1536]{1,0:T(8,128)(2,1)} %constant_dynamic-update-slice_fusion), channel_id=1, source_target_pairs={{0,8},{8,0},{1,9},{9,1},{2,10},{10,2},{3,11},{11,3},{4,12},{12,4},... | collective-permute-start | bytes 2359304 | tf_op jit(solution)/shard_map/ppermute | solution.py:43
  473.6 33.9 %all-to-all-start.2 = ((bf16[8,128,768]{2,1,0:T(8,128)(2,1)}), bf16[8,128,768]{2,1,0:T(8,128)(2,1)S(1)}, u32[]{:S(2)}, u32[]{:S(2)}) async-start(bf16[8,128,768]{2,1,0:T(8,128)(2,1)} %broadcast_in_dim.60), calls=%async_computation.4 | async-start | bytes 3145728 | tf_op jit(solution)/shard_map/all_to_all | solution.py:377
  478.6 23.7 %copy-start.44 = (bf16[256,1536]{1,0:T(8,128)(2,1)S(1)}, bf16[256,1536]{1,0:T(8,128)(2,1)}, u32[]{:S(2)}) copy-start(bf16[256,1536]{1,0:T(8,128)(2,1)} %constant_dynamic-update-slice_fusion) | copy-start | bytes 2359300
  504.5 14.9 %collective-permute-start.43 = (bf16[256,1536]{1,0:T(8,128)(2,1)}, bf16[256,1536]{1,0:T(8,128)(2,1)}, u32[]{:S(2)}, u32[]{:S(2)}) collective-permute-start(bf16[256,1536]{1,0:T(8,128)(2,1)} %add_convert_fusion.3), channel_id=1, source_target_pairs={{0,6},{2,0},{4,2},{6,4},{1,7},{3,1},{5,3},{7,5},{8,14},{10,8},{12,... | collective-permute-start | bytes 2359304 | tf_op jit(solution)/shard_map/ppermute | solution.py:53
  504.5 16.5 %collective-permute-start.44 = (bf16[256,1536]{1,0:T(8,128)(2,1)}, bf16[256,1536]{1,0:T(8,128)(2,1)}, u32[]{:S(2)}, u32[]{:S(2)}) collective-permute-start(bf16[256,1536]{1,0:T(8,128)(2,1)} %add_convert_fusion.3), channel_id=1, source_target_pairs={{0,4},{2,6},{4,0},{6,2},{1,5},{3,7},{5,1},{7,3},{8,12},{10,14},{12... | collective-permute-start | bytes 2359304 | tf_op jit(solution)/shard_map/ppermute | solution.py:53
  505.6 37.0 %collective-permute-start.45 = (bf16[256,1536]{1,0:T(8,128)(2,1)}, bf16[256,1536]{1,0:T(8,128)(2,1)}, u32[]{:S(2)}, u32[]{:S(2)}) collective-permute-start(bf16[256,1536]{1,0:T(8,128)(2,1)} %add_convert_fusion.3), channel_id=1, source_target_pairs={{0,2},{2,4},{4,6},{6,0},{1,3},{3,5},{5,7},{7,1},{8,10},{10,12},{12... | collective-permute-start | bytes 2359304 | tf_op jit(solution)/shard_map/ppermute | solution.py:53
  507.8 6.2 %collective-permute-start.40 = (f32[256,2]{1,0:T(8,128)S(1)}, f32[256,2]{1,0:T(8,128)S(1)}, u32[]{:S(2)}, u32[]{:S(2)}) collective-permute-start(f32[256,2]{1,0:T(8,128)S(1)} %convert_reduce_fusion), channel_id=1, source_target_pairs={{0,1},{1,0},{2,3},{3,2},{4,5},{5,4},{6,7},{7,6},{8,9},{9,8},{10,11... | collective-permute-start | bytes 6152 | tf_op jit(solution)/shard_map/ppermute | solution.py:39
  514.0 43.3 %collective-permute-start.41 = (bf16[2,256,640]{2,1,0:T(8,128)(2,1)}, bf16[2,256,640]{2,1,0:T(8,128)(2,1)}, u32[]{:S(2)}, u32[]{:S(2)}) collective-permute-start(bf16[2,256,640]{2,1,0:T(8,128)(2,1)} %constant_dynamic-slice_fusion), channel_id=1, source_target_pairs={{0,1},{1,0},{2,3},{3,2},{4,5},{5,4},{6,7},{7,6},{8,9},{9,8},{10,11... | collective-permute-start | bytes 1966088 | tf_op jit(solution)/shard_map/ppermute | solution.py:39
  (55 other events, 263.6 us)
Sparse Core Ops, SparseCore 0:
  10.2 33.0 all-gather.8
  56.7 77.5 all-gather.4
  135.9 40.1 all-gather.6
  260.4 39.7 reduce-scatter.2
  314.2 84.6 reduce-scatter.4

commit v3 on v2

v3 whole, which is shorter than its diff:
```python
import functools

import jax
import jax.numpy as jnp
from jax import lax
from jax.experimental import pallas as pl
from jax.experimental.pallas import tpu as pltpu
from jax.sharding import Mesh, PartitionSpec as P

HD = 128
EPS = 1e-05
NEG = -1e30
F32 = jnp.float32
BF16 = jnp.bfloat16
SHARD = ("yl", "z")
SCALE = HD ** (-0.5)
LOG2E = 1.4426950408889634
VMEM = 48 * 2**20
SWAP = ((0, 1), (1, 0))


def half(value):
    return value.astype(BF16)


def mm(left, right):
    return jnp.dot(left, right, preferred_element_type=F32)


def mm_nt(left, right):
    return lax.dot_general(left, right, (((1,), (1,)), ((), ())), preferred_element_type=F32)


def mm_tn(left, right):
    return lax.dot_general(left, right, (((0,), (0,)), ((), ())), preferred_element_type=F32)


def swap_cores(value, name="swap"):
    with jax.named_scope(name):
        return lax.ppermute(value, "tp", SWAP)


def across_y(value):
    return lax.ppermute(value, "yh", SWAP)


def after(value, *others):
    zero = sum((other[:1, :1] * 0).astype(value.dtype) for other in others)
    tile = value[:16, :HD] + zero
    return lax.dynamic_update_slice(value, tile, (0, 0))


def shift_x(value, hop):
    return lax.ppermute(value, "x", [(i, (i + hop) % 4) for i in range(4)])


def chunk(value, index):
    rows = value.shape[0] // 4
    return lax.dynamic_slice_in_dim(value, index % 4 * rows, rows, axis=0)


def gather_x(value, name):
    x_at = lax.axis_index("x")
    with jax.named_scope(name):
        moved = {hop: shift_x(value, -hop) for hop in (2, 1, 3)}
    chunks = [value, moved[1], moved[2], moved[3]]
    return [lax.select_n((i - x_at) % 4, *chunks) for i in range(4)]


def scatter_x(value, name):
    x_at = lax.axis_index("x")
    with jax.named_scope(name):
        moved = [shift_x(half(chunk(value, x_at + hop)), hop) for hop in (2, 1, 3)]
    return chunk(value, x_at) + sum(part.astype(F32) for part in moved)


def gather_x_async(value, name):
    with jax.named_scope(name):
        return lax.all_gather(value, "x", axis=0, tiled=True)


def scatter_x_async(value, name):
    with jax.named_scope(name):
        return lax.psum_scatter(half(value), "x", scatter_dimension=0, tiled=True).astype(F32)


def gather_shard(value):
    spread = jnp.broadcast_to(value[None], (8, *value.shape))
    return lax.all_to_all(spread, SHARD, 0, 0).reshape(-1, value.shape[1])


def rotate(value, cosine, sine):
    turned = jnp.concatenate([-value[..., HD // 2 :], value[..., : HD // 2]], axis=-1)
    return value * cosine + turned * sine


def unrotate(grad, cosine, sine):
    scaled = grad * sine
    return grad * cosine + jnp.concatenate(
        [scaled[..., HD // 2 :], -scaled[..., : HD // 2]], axis=-1
    )


def norm_root(value):
    return lax.rsqrt(jnp.mean(value * value, axis=-1, keepdims=True) + EPS)


def norm_backward(value, root, gain, grad):
    scaled = gain * grad
    return root * scaled - value * root**3 * jnp.mean(scaled * value, axis=-1, keepdims=True)


def attend_kernel(q_ref, kt_ref, v_ref, rows_ref, cols_ref, mixed_ref, heads_ref, lse_ref, bias_ref):
    @pl.when(pl.program_id(1) == 0)
    def _():
        seg, blk = rows_ref[:, :1], rows_ref[:, 1:2]
        visible = (seg == cols_ref[:1, :]) & (cols_ref[1:2, :] <= blk)
        bias_ref[...] = jnp.where(visible, 0.0, NEG)

    raw = mm(q_ref[...], kt_ref[...])
    raw = raw * (SCALE * LOG2E) + bias_ref[...]
    top = jnp.max(raw, axis=-1, keepdims=True)
    weights = jnp.exp2(raw - top)
    total = jnp.sum(weights, axis=-1, keepdims=True)
    mixed = mm(half(weights), v_ref[...]) / total
    mixed_ref[...] = mixed
    heads_ref[...] = half(mixed)
    lse = jnp.broadcast_to(top + jnp.log2(total), mixed.shape)
    lse_ref[0] = lse.T[:8, :]


def attend(query, keys_t, values, query_tags, key_tags_t, rows=256):
    count, features = query.shape
    n = values.shape[0]
    part = pl.BlockSpec((rows, HD), lambda j, h: (j, h))
    return pl.pallas_call(
        attend_kernel,
        grid=(count // rows, features // HD),
        in_specs=[
            part,
            pl.BlockSpec((HD, n), lambda j, h: (0, 0)),
            pl.BlockSpec((n, HD), lambda j, h: (0, 0)),
            pl.BlockSpec((rows, 2), lambda j, h: (j, 0)),
            pl.BlockSpec((2, n), lambda j, h: (0, 0)),
        ],
        out_specs=[part, part, pl.BlockSpec((1, 8, rows), lambda j, h: (h, 0, j))],
        out_shape=[
            jax.ShapeDtypeStruct((count, features), F32),
            jax.ShapeDtypeStruct((count, features), BF16),
            jax.ShapeDtypeStruct((features // HD, 8, count), F32),
        ],
        scratch_shapes=[pltpu.VMEM((rows, n), F32)],
        compiler_params=pltpu.CompilerParams(vmem_limit_bytes=VMEM),
    )(query, keys_t, values, query_tags, key_tags_t)


def attend_back_kernel(
    q_ref, do_ref, mixed_ref, lse_ref, k_ref, kt_ref, v_ref, rows_ref, cols_ref, cos_ref, sin_ref,
    dq_ref, dk_ref, dv_ref, bias_ref, *, piece,
):
    @pl.when(pl.program_id(0) == 0)
    def _():
        dk_ref[...] = jnp.zeros_like(dk_ref)
        dv_ref[...] = jnp.zeros_like(dv_ref)
        seg, blk = rows_ref[:, :1], rows_ref[:, 1:2]
        visible = (seg == cols_ref[:1, :]) & (blk <= cols_ref[1:2, :])
        bias_ref[...] = jnp.where(visible, 0.0, NEG)

    q, d_out = q_ref[...], do_ref[...]
    wide = d_out.astype(F32)
    d_out_t = half(wide.T)
    qt = half(q.astype(F32).T)
    delta = jnp.sum((wide * mixed_ref[...]).T, axis=0, keepdims=True)
    lse = lse_ref[0, :1, :]
    grad_qt = jnp.zeros(qt.shape, F32)
    for at in range(0, k_ref.shape[0], piece):
        part = pl.ds(at, piece)
        raw = mm(k_ref[part, :], qt)
        probs = jnp.exp2(raw * (SCALE * LOG2E) + (bias_ref[part, :] - lse))
        d_probs = mm(v_ref[part, :], d_out_t)
        dv_ref[part, :] += mm(half(probs), d_out)
        d_scores = half(probs * (SCALE * (d_probs - delta)))
        dk_ref[part, :] += mm(d_scores, q)
        grad_qt += mm(kt_ref[:, part], d_scores)
    grad_q = grad_qt.T
    scaled = grad_q * sin_ref[...]
    lane = lax.broadcasted_iota(jnp.int32, scaled.shape, 1)
    turned = pltpu.roll(scaled, HD // 2, 1)
    dq_ref[...] = half(grad_q * cos_ref[...] + jnp.where(lane < HD // 2, turned, -turned))


def attend_back(query, d_heads, mixed, lse, keys, keys_t, values, key_tags, query_tags_t, cosine, sine):
    count, features = query.shape
    n = keys.shape[0]
    row = pl.BlockSpec((count, HD), lambda h: (0, h))

    def whole(*shape):
        return pl.BlockSpec(shape, lambda h: (0, 0))

    return pl.pallas_call(
        functools.partial(attend_back_kernel, piece=min(512, n)),
        grid=(features // HD,),
        in_specs=[
            row, row, row, pl.BlockSpec((1, 8, count), lambda h: (h, 0, 0)), whole(n, HD),
            whole(HD, n), whole(n, HD), whole(n, 2), whole(2, count), whole(count, HD), whole(count, HD),
        ],
        out_specs=[row, whole(n, HD), whole(n, HD)],
        out_shape=[
            jax.ShapeDtypeStruct((count, features), BF16),
            jax.ShapeDtypeStruct((n, HD), F32),
            jax.ShapeDtypeStruct((n, HD), F32),
        ],
        scratch_shapes=[pltpu.VMEM((n, count), F32)],
        compiler_params=pltpu.CompilerParams(vmem_limit_bytes=VMEM),
    )(query, d_heads, mixed, lse, keys, keys_t, values, key_tags, query_tags_t, cosine, sine)


def spread_kernel(parts_ref, *out_refs, tiles, spare):
    split = tiles + HD
    for place, out_ref in enumerate(out_refs):
        at = place * split
        for i in range(4):
            out_ref[:, i * tiles : (i + 1) * tiles] = parts_ref[i, :, at : at + tiles].astype(F32)
        rest = [parts_ref[i, :, at + tiles : at + split].astype(F32) for i in range(4)]
        for i in (0, 2):
            start = 4 * tiles + i * spare
            out_ref[:, start : start + HD] = rest[i] + pltpu.roll(rest[i + 1], spare, 1)


def spread(parts, tiles, spare, rows=64):
    _, count, columns = parts.shape
    outs = columns // (tiles + HD)
    units = 4 * (tiles + spare)
    return pl.pallas_call(
        functools.partial(spread_kernel, tiles=tiles, spare=spare),
        grid=(count // rows,),
        in_specs=[pl.BlockSpec((4, rows, columns), lambda j: (0, j, 0))],
        out_specs=[pl.BlockSpec((rows, units), lambda j: (j, 0))] * outs,
        out_shape=[jax.ShapeDtypeStruct((count, units), F32)] * outs,
        compiler_params=pltpu.CompilerParams(vmem_limit_bytes=VMEM),
    )(parts)


def per_device(
    tokens, cotangent, seq_ids, block_ids, keep_layer, gain_attn, gain_ffn,
    w_query, w_key, w_value, w_out, w_gate, w_up, w_down,
):
    core, x_at, y_at = lax.axis_index("tp"), lax.axis_index("x"), lax.axis_index("yh")
    first = core == 0
    rows = tokens.shape[1] // 2
    width = tokens.shape[2]
    keep = keep_layer[0].astype(F32)

    own_tokens = lax.dynamic_slice_in_dim(tokens[0], core * rows, rows, axis=0)
    own_top = lax.dynamic_slice_in_dim(cotangent[0], core * rows, rows, axis=0)
    x_top = gather_x_async(jnp.concatenate([own_tokens, own_top], axis=0), "token_gather")
    x_top = x_top.reshape(4, 2, rows, width)
    x_all, top_all = x_top[:, 0].reshape(-1, width), x_top[:, 1].reshape(-1, width)
    xval, grad_top = own_tokens.astype(F32), own_top.astype(F32)

    side = x_at // 2
    at = x_at % 2
    wq = half(lax.dynamic_slice_in_dim(w_query, at * 512, 512, axis=1))
    wk = half(lax.dynamic_slice_in_dim(w_key, at * HD, HD, axis=1))
    wv = half(lax.dynamic_slice_in_dim(w_value, at * HD, HD, axis=1))
    wo = half(lax.dynamic_slice_in_dim(w_out, at * 512, 512, axis=1))
    pack0 = jnp.concatenate([wq[:, :256], wk, wo[:, :256]], axis=1)
    pack1 = jnp.concatenate([wq[:, 256:], wv, wo[:, 256:]], axis=1)
    lent = lax.ppermute(
        jnp.where(first, pack1, pack0),
        ("x", "tp"),
        [(2 * i + i // 2, 2 * i + 1 - i // 2) for i in range(4)],
    )
    pack = jnp.where(core == side, jnp.where(first, pack0, pack1), lent)
    pack = gather_shard(pack)

    units = w_gate.shape[1] // 4
    tiles = units // HD * HD
    spare = units - tiles
    split = tiles + HD

    def hidden_units(weight):
        main = lax.dynamic_slice_in_dim(weight, x_at * tiles, tiles, axis=1)
        rest = lax.dynamic_slice_in_dim(weight[:, 4 * tiles :], x_at * spare, spare, axis=1)
        return jnp.concatenate([half(main), jnp.pad(half(rest), ((0, 0), (0, HD - spare)))], axis=1)

    own_ffn = jnp.concatenate([hidden_units(w) for w in (w_gate, w_up, w_down)], axis=1)
    with jax.named_scope("unit_gather"):
        own_ffn = lax.all_gather(after(own_ffn, pack), SHARD, axis=0, tiled=True)

    def of_positions(line, y_index, core_index):
        grid = line.reshape(2, 4, 2, rows)
        picked = lax.dynamic_index_in_dim(grid, y_index, 0, keepdims=False)
        picked = lax.dynamic_index_in_dim(picked, core_index, 1, keepdims=False)
        return picked.reshape(-1)

    corners = ((y_at, core), (y_at, 1 - core), (1 - y_at, core), (1 - y_at, 1 - core))
    lines = (seq_ids[0], block_ids[0])
    query_tags_t = jnp.stack([of_positions(line, y_at, core) for line in lines])
    key_tags_t = jnp.stack(
        [jnp.concatenate([of_positions(line, *corner) for corner in corners]) for line in lines]
    )
    query_tags, key_tags = query_tags_t.T, key_tags_t.T
    position = of_positions(jnp.arange(seq_ids.shape[1], dtype=jnp.int32), y_at, core)
    freqs = 10000.0 ** (-(jnp.arange(HD // 2).astype(F32) * 2.0 / HD))
    angle = position.astype(F32)[:, None] * freqs[None, :]
    cosine = jnp.concatenate([jnp.cos(angle), jnp.cos(angle)], axis=-1)
    sine = jnp.concatenate([jnp.sin(angle), jnp.sin(angle)], axis=-1)

    count = x_all.shape[0]
    x_all = x_all.astype(F32)
    x_unit = x_all * norm_root(x_all)
    normed_attn = half(x_unit * gain_attn)
    root_attn = norm_root(xval)
    packs_qkv = pack[:, :384], swap_cores(pack[:, :384])
    packs_out = pack[:, 384:], swap_cores(pack[:, 384:])
    own_pre, other_pre = [mm(normed_attn, part) for part in packs_qkv]
    key_pre = jnp.where(first, own_pre[:, 256:], other_pre[:, 256:])
    value_pre = jnp.where(first, other_pre[:, 256:], own_pre[:, 256:])
    query = jnp.concatenate(
        [half(rotate(pre[:, s : s + HD], cosine, sine)) for pre in (own_pre, other_pre) for s in (0, HD)],
        axis=1,
    )
    keys_values = jnp.concatenate([half(rotate(key_pre, cosine, sine)), half(value_pre)], axis=1)
    two_kv = jnp.concatenate([keys_values, across_y(keys_values)], axis=0)
    other_kv = swap_cores(two_kv)
    all_kv = jnp.concatenate(
        [two_kv[:count], other_kv[:count], two_kv[count:], other_kv[count:]], axis=0
    )
    all_keys, all_values = all_kv[:, :HD], all_kv[:, HD:]
    d_ffn = half(keep * top_all.astype(F32))

    keys_t = all_keys.T
    heads_f, heads, lse = attend(query, keys_t, all_values, query_tags, key_tags_t)

    attn_branch = mm_nt(heads[:, :256], packs_out[0]) + mm_nt(heads[:, 256:], packs_out[1])
    attn_branch = scatter_x(attn_branch, "attn_scatter")
    middle = xval + keep * attn_branch
    root_ffn = norm_root(middle)
    normed_ffn = jnp.concatenate(gather_x(half(middle * root_ffn * gain_ffn), "ffn_gather"), axis=0)

    own_ffn = after(own_ffn, normed_ffn)
    other_ffn = swap_cores(own_ffn)
    full_gu = (own_ffn[:, : 2 * split], other_ffn[:, : 2 * split])
    full_down = (own_ffn[:, 2 * split :], other_ffn[:, 2 * split :])
    branch = 0.0
    d_normed = 0.0
    d_gus, hiddens = [], []
    for wgu, wd in zip(full_gu, full_down, strict=True):
        gate_up = mm(after(normed_ffn, *hiddens[-1:]), wgu)
        gate, up = gate_up[:, :split], gate_up[:, split:]
        sig = jax.nn.sigmoid(gate)
        silu = gate * sig
        hidden = half(silu * up)
        d_hidden = mm(d_ffn, wd)
        d_gate = half(d_hidden * up * sig * (1.0 + gate * (1.0 - sig)))
        d_up = half(d_hidden * silu)
        d_gu = jnp.concatenate([d_gate, d_up], axis=1)
        d_normed = d_normed + mm_nt(d_gu, wgu)
        branch = branch + mm_nt(hidden, wd)
        d_gus.append(d_gu)
        hiddens.append(hidden)
    grads_down = [mm_tn(d_ffn, hidden) for hidden in hiddens]
    d_normed_ffn = scatter_x(d_normed, "d_ffn_scatter")
    left_gu = after(normed_ffn, d_normed_ffn)
    grads_gu = [mm_tn(left_gu, d_gu) for d_gu in d_gus]
    d_middle = grad_top + norm_backward(middle, root_ffn, gain_ffn, d_normed_ffn)
    gain_ffn_local = jnp.sum(d_normed_ffn * middle * root_ffn, axis=0)

    def both_cores(value):
        other = swap_cores(value)
        return jnp.concatenate(
            [jnp.where(first, value, other), jnp.where(first, other, value)], axis=0
        )

    def sum_cores(mine, theirs):
        return half(mine + swap_cores(half(theirs)).astype(F32))

    def reduce_rows(value, name):
        with jax.named_scope(name + "_rows"):
            parts = lax.all_to_all(value.reshape(16, width // 16, -1), ("yl", "z", "yh"), 0, 0)
        return half(jnp.sum(parts.astype(F32), axis=0))

    def columns(value, name):
        spread = jnp.broadcast_to(value[None], (8, *value.shape))
        with jax.named_scope(name + "_columns"):
            parts = lax.all_to_all(spread, ("yh", "x"), 0, 0)
        return parts.reshape(2, 4, *value.shape)

    def rows_of(parts, x_index):
        return parts[:, x_index].reshape(-1, parts.shape[-1])

    def samples(value, name):
        with jax.named_scope(name + "_rows"):
            return lax.psum_scatter(value, SHARD, scatter_dimension=0, tiled=True)

    def halves(value, name):
        with jax.named_scope(name + "_y"):
            return half(value.astype(F32) + across_y(value).astype(F32))

    sum_down, sum_gu = sum_cores(*grads_down), sum_cores(*grads_gu)
    rows_down = samples(sum_down, "down")
    d_attn = gather_x_async(after(half(keep * d_middle), rows_down), "d_attn_gather")
    rows_gu = samples(after(sum_gu, d_attn), "gate_up")
    d_attn = after(d_attn, branch)
    unit_down = halves(after(rows_down, d_attn), "down")
    ffn_branch = scatter_x(after(branch, d_attn), "branch_scatter")
    output = both_cores(half(middle + keep * ffn_branch))

    d_heads = jnp.concatenate([half(mm(d_attn, part)) for part in packs_out], axis=1)
    d_query, key_part, value_part = attend_back(
        query, d_heads, heads_f, lse, all_keys, keys_t, all_values, key_tags, query_tags_t, cosine, sine
    )
    kv_part = jnp.concatenate([key_part, value_part], axis=1)
    kv_mine = jnp.concatenate([kv_part[:count], kv_part[2 * count : 3 * count]], axis=0)
    kv_theirs = jnp.concatenate([kv_part[count : 2 * count], kv_part[3 * count :]], axis=0)
    kv_two = kv_mine + swap_cores(half(kv_theirs)).astype(F32)
    grad_kv = kv_two[:count] + across_y(half(kv_two[count:])).astype(F32)
    grad_kv = after(grad_kv, ffn_branch, unit_down)
    d_key = half(unrotate(grad_kv[:, :HD], cosine, sine))
    d_value = half(grad_kv[:, HD:])
    d_own = jnp.concatenate([d_query[:, :256], jnp.where(first, d_key, d_value)], axis=1)
    d_other = jnp.concatenate([d_query[:, 256:], jnp.where(first, d_value, d_key)], axis=1)
    d_normed_part = mm_nt(d_own, packs_qkv[0]) + mm_nt(d_other, packs_qkv[1])
    d_normed_attn = scatter_x_async(d_normed_part, "d_attn_scatter")
    input_part = norm_backward(xval, root_attn, gain_attn, d_normed_attn)
    input_grad = both_cores(half(d_middle + input_part))
    gain_attn_local = jnp.sum(d_normed_part * x_unit, axis=0)
    gains = half(jnp.stack([gain_attn_local, gain_ffn_local])).T
    sum_qkv = sum_cores(mm_tn(normed_attn, d_own), mm_tn(normed_attn, d_other))
    sum_out = sum_cores(mm_tn(d_attn, heads[:, :256]), mm_tn(d_attn, heads[:, 256:]))
    sums = jnp.concatenate([sum_qkv, sum_out], axis=1)
    sums = jnp.concatenate([sums, jnp.pad(gains, ((0, 0), (0, HD - 2)))], axis=1)
    total_rows = after(reduce_rows(sums, "attn"), rows_gu)
    packs = columns(total_rows, "attn")
    unit_rows = jnp.concatenate([halves(rows_gu, "gate_up"), unit_down], axis=1)
    with jax.named_scope("unit_columns"):
        parts = lax.all_gather(unit_rows, "x", axis=0, tiled=False)
    grad_gate, grad_up, grad_down = spread(parts, tiles, spare)
    packs = jnp.stack([rows_of(packs, i) for i in range(4)])
    gains = jnp.sum(packs[:, :, 640:642].astype(F32), axis=0)
    gains = (gains + swap_cores(gains)).T
    packs = packs[:, :, :640]
    mine = lax.dynamic_slice_in_dim(packs, 2 * core, 2, axis=0)
    theirs = swap_cores(lax.dynamic_slice_in_dim(packs, 2 - 2 * core, 2, axis=0))
    out0 = jnp.where(first, mine, theirs).astype(F32)
    out1 = jnp.where(first, theirs, mine).astype(F32)
    grad_query = jnp.concatenate(
        [out0[0, :, :256], out1[0, :, :256], out0[1, :, :256], out1[1, :, :256]], axis=1
    )
    grad_key = jnp.concatenate([out0[0, :, 256:384], out0[1, :, 256:384]], axis=1)
    grad_value = jnp.concatenate([out1[0, :, 256:384], out1[1, :, 256:384]], axis=1)
    grad_out = jnp.concatenate(
        [out0[0, :, 384:], out1[0, :, 384:], out0[1, :, 384:], out1[1, :, 384:]], axis=1
    )
    return (
        output[None], input_grad[None], gains[0], gains[1],
        grad_query, grad_key, grad_value, grad_out, grad_gate, grad_up, grad_down,
    )


def solution(mesh):
    fine = Mesh(mesh.devices.reshape(2, 4, 2, 4, 2), ("yl", "z", "yh", "x", "tp"))
    shard, ctx = ("yl", "z"), ("yh", "x")
    acts, weight = P(shard, ctx, None), P(shard, "tp")
    return jax.shard_map(
        per_device,
        mesh=fine,
        in_specs=(acts, acts, P(shard, None), P(shard, None), P(shard), P(), P()) + (weight,) * 7,
        out_specs=(acts, acts, P(shard), P(shard)) + (weight,) * 7,
        check_vma=False,
    )
```

time: 579 us -> 514 us (0.89)
  the two profiles are of different devices: /device:TPU:9 before, /device:TPU:97 now
where the time goes in v3:
time: 514 us; the launch traced here: 507 us
  waiting for transfers between devices  215 us (42%)
  matrix products  81 us (16%)
  starting transfers between devices  60 us (12%)
  local copies, waits for them, and re-layouts  51.8 us (10%)
  other arithmetic  45.6 us (9%)
  Pallas kernels  29.8 us (6%)
  between operations  23.6 us (5%)
    ppermute x12, waiting for transfers between devices, shift_x(): return lax.ppermute(value, 'x', [(i, (i + hop) % 4) for i in range(4)])  71.2 us
    ppermute x4, waiting for transfers between devices, across_y(): return lax.ppermute(value, 'yh', SWAP)  41.4 us
    all_to_all x1, waiting for transfers between devices, reduce_rows(): lax.all_to_all(value.reshape(16, width // 16, -1), ('yl', 'z', 'yh'), 0, 0)  37.5 us
    dot_general x8, matrix products, mm_nt(): lax.dot_general(left, right, (((1,), (1,)), ((), ())), preferred_element_...  30.5 us
    dot_general x8, matrix products, mm_tn(): lax.dot_general(left, right, (((0,), (0,)), ((), ())), preferred_element_...  28.1 us
    unnamed x106, local copies, waits for them, and re-layouts  23.6 us
    dot_general x8, matrix products, mm(): return jnp.dot(left, right, preferred_element_type=F32)  22.3 us
    all_to_all x1, waiting for transfers between devices, gather_shard(): return lax.all_to_all(spread, SHARD, 0, 0).reshape(-1, value.shape[1])  19.6 us
  transfers between devices with their start and end apart: 40, of which 24 were waited for; matrix products, arithmetic and copies ran while one was open for 28% of the time, Pallas kernels for 5%

profile of v3, /device:TPU:97, one launch (start us, length us, event | category | flops | bytes accessed | tf_op | source)
XLA Modules:
  0.0 506.7 jit_solution(17977979392594214030)
XLA Ops:
  14.3 2.2 collective-permute-done
  18.3 5.0 all-to-all-start
  26.3 1.9 constant_dynamic-update-slice_fusion
  34.1 19.6 %all-to-all-done = bf16[8,256,640]{2,1,0:T(8,128)(2,1)S(1)} async-done(((bf16[8,256,640]{2,1,0:T(8,128)(2,1)}), bf16[8,256,640]{2,1,0:T(8,128)(2,1)S(1)}, u32[]{:S(2)}, u32[]{:S(2)}) %all-to-all-start) | async-done | bytes 2621472 | tf_op jit(solution)/shard_map/all_to_all | solution.py:89
  60.2 2.1 multiply_reduce_fusion.1
  62.3 2.1 multiply_convert_fusion.1
  66.0 2.7 fusion.80
  70.2 2.8 collective-permute-start.2
  73.3 2.3 slice.424
  76.5 9.0 %collective-permute-done.2 = bf16[512,256]{1,0:T(8,128)(2,1)S(1)} collective-permute-done((bf16[512,256]{1,0:T(8,128)(2,1)S(1)}, bf16[512,256]{1,0:T(8,128)(2,1)S(1)}, u32[]{:S(2)}, u32[]{:S(2)}) %collective-permute-start.2) | collective-permute-done | bytes 262176 | tf_op jit(solution)/shard_map/ppermute | solution.py:44
  89.2 10.1 %shard_map.221 = (f32[512,512]{1,0:T(8,128)S(1)}, bf16[512,512]{1,0:T(8,128)(2,1)S(1)}, f32[4,8,512]{2,1,0:T(8,128)S(1)}) custom-call(bf16[512,512]{1,0:T(8,128)(2,1)S(1)} %pad_maximum_fusion.17.q_ref, bf16[128,2048]{1,0:T(8,128)(2,1)S(1)} %copy.94.kt_ref, bf16[2048,128]{1,0:T(8,128)(2,1)S(1)} %get-tuple-element.99.v_ref, s32[512,2]{1,0:T(8,128)S(1)} %copy.95.rows_ref, ...), custom_call_target="tpu_custom_call" | custom-call | tf_op jit(solution)/shard_map/pallas_call | solution.py:136
  99.3 2.3 fusion.49
  101.6 2.1 convolution_add_fusion.1
  103.7 2.0 copy-done.8
  110.7 9.7 %collective-permute-done.7 = bf16[128,2048]{1,0:T(8,128)(2,1)} collective-permute-done((bf16[128,2048]{1,0:T(8,128)(2,1)}, bf16[128,2048]{1,0:T(8,128)(2,1)}, u32[]{:S(2)}, u32[]{:S(2)}) %collective-permute-start.7) | collective-permute-done | bytes 524320 | tf_op jit(solution)/shard_map/attn_scatter/ppermute | solution.py:54
  120.4 3.0 collective-permute-done.6
  123.4 9.6 %collective-permute-done.5 = bf16[128,2048]{1,0:T(8,128)(2,1)} collective-permute-done((bf16[128,2048]{1,0:T(8,128)(2,1)}, bf16[128,2048]{1,0:T(8,128)(2,1)}, u32[]{:S(2)}, u32[]{:S(2)}) %collective-permute-start.5) | collective-permute-done | bytes 524320 | tf_op jit(solution)/shard_map/attn_scatter/ppermute | solution.py:54
  133.0 2.4 multiply_reduce_fusion.4
  138.9 2.3 collective-permute-start.8
  141.2 9.2 %collective-permute-done.9 = bf16[128,2048]{1,0:T(8,128)(2,1)} collective-permute-done((bf16[128,2048]{1,0:T(8,128)(2,1)}, bf16[128,2048]{1,0:T(8,128)(2,1)}, u32[]{:S(2)}, u32[]{:S(2)}) %collective-permute-start.9) | collective-permute-done | bytes 524320 | tf_op jit(solution)/shard_map/ffn_gather/ppermute | solution.py:54
  150.4 13.8 %collective-permute-done.10 = bf16[128,2048]{1,0:T(8,128)(2,1)} collective-permute-done((bf16[128,2048]{1,0:T(8,128)(2,1)}, bf16[128,2048]{1,0:T(8,128)(2,1)}, u32[]{:S(2)}, u32[]{:S(2)}) %collective-permute-start.10) | collective-permute-done | bytes 524320 | tf_op jit(solution)/shard_map/ffn_gather/ppermute | solution.py:54
  164.3 3.1 select_select_fusion.3
  171.8 2.0 multiply_convert_fusion
  175.7 2.6 copy-done.40
  178.3 3.4 fusion.7
  181.7 3.4 multiply_convert_fusion.5
  186.4 3.4 fusion.3
  190.1 3.4 multiply_convert_fusion.3
  195.9 5.1 %fusion.5 = f32[512,2048]{1,0:T(8,128)} fusion(bf16[2048,2304]{1,0:T(8,128)(2,1)S(1)} %copy-done.40, bf16[512,768]{1,0:T(8,128)(2,1)S(1)} %copy-done.48, bf16[512,768]{1,0:T(8,128)(2,1)S(1)} %copy-done.47), kind=kOutput, calls=%fused_computation.9 | convolution fusion | flops 3224371200 | bytes 12058624 | tf_op jit(solution)/shard_map/dot_general | solution.py:31
  201.3 3.6 add_convert_fusion.1
  205.0 7.9 %fusion.11 = f32[512,2048]{1,0:T(8,128)S(1)} fusion(f32[512,2048]{1,0:T(8,128)} %fusion.5, bf16[2048,2304]{1,0:T(8,128)(2,1)} %copy-done.41, bf16[512,768]{1,0:T(8,128)(2,1)} %get-tuple-element.49, bf16[512,768]{1,0:T(8,128)(2,1)} %get-tuple-element.48), kind=kOutput, calls=%fused_computation.25 | convolution fusion | flops 3225419776 | bytes 16252928 | tf_op jit(solution)/shard_map/dot_general | solution.py:31
  215.9 10.6 %collective-permute-done.14 = bf16[128,2048]{1,0:T(8,128)(2,1)S(1)} collective-permute-done((bf16[128,2048]{1,0:T(8,128)(2,1)S(1)}, bf16[128,2048]{1,0:T(8,128)(2,1)S(1)}, u32[]{:S(2)}, u32[]{:S(2)}) %collective-permute-start.14) | collective-permute-done | bytes 524320 | tf_op jit(solution)/shard_map/d_ffn_scatter/ppermute | solution.py:54
  226.5 2.9 collective-permute-done.13
  229.4 9.3 %collective-permute-done.12 = bf16[128,2048]{1,0:T(8,128)(2,1)S(1)} collective-permute-done((bf16[128,2048]{1,0:T(8,128)(2,1)S(1)}, bf16[128,2048]{1,0:T(8,128)(2,1)S(1)}, u32[]{:S(2)}, u32[]{:S(2)}) %collective-permute-start.12) | collective-permute-done | bytes 524320 | tf_op jit(solution)/shard_map/d_ffn_scatter/ppermute | solution.py:54
  241.2 5.7 %convolution_convert_fusion = bf16[2048,1536]{1,0:T(8,128)(2,1)} fusion(bf16[512,2048]{1,0:T(8,128)(2,1)S(1)} %constant_dynamic-update-slice_fusion.4, bf16[512,768]{1,0:T(8,128)(2,1)S(1)} %copy-done.46, bf16[512,768]{1,0:T(8,128)(2,1)S(1)} %copy-done.45), kind=kOutput, calls=%fused_computation.1 | convolution fusion | flops 3227516928 | bytes 9961472 | tf_op jit(solution)/shard_map/dot_general | solution.py:35
  246.9 2.3 collective-permute-start.26
  254.2 5.1 %collective-permute-done.26 = bf16[2048,1536]{1,0:T(8,128)(2,1)} collective-permute-done((bf16[2048,1536]{1,0:T(8,128)(2,1)}, bf16[2048,1536]{1,0:T(8,128)(2,1)}, u32[]{:S(2)}, u32[]{:S(2)}) %collective-permute-start.26) | collective-permute-done | bytes 6291488 | tf_op jit(solution)/shard_map/swap/ppermute | solution.py:40
  259.3 10.1 %add_convert_fusion = bf16[2048,1536]{1,0:T(8,128)(2,1)} fusion(bf16[2048,1536]{1,0:T(8,128)(2,1)} %collective-permute-done.26, bf16[512,2048]{1,0:T(8,128)(2,1)} %copy-done.17, bf16[512,768]{1,0:T(8,128)(2,1)} %get-tuple-element.51, bf16[512,768]{1,0:T(8,128)(2,1)} %get-tuple-element.50), kind=kOutput, calls=%fused_computation | convolution fusion | flops 3233808384 | bytes 16252928 | tf_op jit(solution)/shard_map/dot_general | solution.py:35
  269.4 15.0 %all-gather.10.cloned.1.call-done = bf16[512,2048]{1,0:T(8,128)(2,1)} async-done(((bf16[128,2048]{1,0:T(8,128)(2,1)}), bf16[512,2048]{1,0:T(8,128)(2,1)}) %all-gather.10.cloned.1.call-update) | async-done | bytes 2097168 | tf_op jit(solution)/shard_map/d_attn_gather/all_gather | solution.py:79
  289.0 4.0 fusion.19
  293.0 3.7 convolution_add_fusion.2
  296.8 2.0 copy-done.24
  302.4 2.8 convolution_convert_fusion.5
  305.2 2.0 convolution_convert_fusion.4
  307.2 15.9 %shard_map.222 = (bf16[512,512]{1,0:T(8,128)(2,1)S(1)}, f32[2048,128]{1,0:T(8,128)S(1)}, f32[2048,128]{1,0:T(8,128)S(1)}) custom-call(bf16[512,512]{1,0:T(8,128)(2,1)S(1)} %pad_maximum_fusion.17.q_ref, bf16[512,512]{1,0:T(8,128)(2,1)S(1)} %pad_maximum_fusion.19.do_ref, f32[512,512]{1,0:T(8,128)} %copy-done.1, f32[4,8,512]{2,1,0:T(8,128)S(1)} %get-tuple-element.22.lse_ref, ...), custom_call_target="tpu_custom_call" | custom-call | tf_op jit(solution)/shard_map/pallas_call | solution.py:200
  324.7 2.8 collective-permute-start.22
  330.8 15.2 %collective-permute-done.22 = bf16[256,768]{1,0:T(8,128)(2,1)S(1)} collective-permute-done((bf16[256,768]{1,0:T(8,128)(2,1)S(1)}, bf16[256,768]{1,0:T(8,128)(2,1)S(1)}, u32[]{:S(2)}, u32[]{:S(2)}) %collective-permute-start.22) | collective-permute-done | bytes 393248 | tf_op jit(solution)/shard_map/down_y/ppermute | solution.py:44
  347.4 2.8 collective-permute-start.21
  350.2 3.1 collective-permute-done.16
  355.6 7.2 %collective-permute-done.21 = bf16[512,256]{1,0:T(8,128)(2,1)S(1)} collective-permute-done((bf16[512,256]{1,0:T(8,128)(2,1)S(1)}, bf16[512,256]{1,0:T(8,128)(2,1)S(1)}, u32[]{:S(2)}, u32[]{:S(2)}) %collective-permute-start.21) | collective-permute-done | bytes 262176 | tf_op jit(solution)/shard_map/ppermute | solution.py:44
  366.9 4.1 multiply_reduce_fusion
  372.6 2.2 convolution_convert_fusion.2
  377.3 3.6 collective-permute-done.25
  382.7 2.2 add_convert_fusion.2
  384.9 2.7 collective-permute-start.29
  387.5 3.3 copy_bitcast_fusion
  390.8 4.5 all-to-all-start.1
  395.4 10.1 %collective-permute-done.29 = bf16[256,1536]{1,0:T(8,128)(2,1)} collective-permute-done((bf16[256,1536]{1,0:T(8,128)(2,1)}, bf16[256,1536]{1,0:T(8,128)(2,1)}, u32[]{:S(2)}, u32[]{:S(2)}) %collective-permute-start.29) | collective-permute-done | bytes 786464 | tf_op jit(solution)/shard_map/gate_up_y/ppermute | solution.py:44
  408.2 2.1 collective-permute-start.19
  410.3 37.5 %all-to-all-done.1 = bf16[16,128,768]{1,2,0:T(8,128)(2,1)S(1)} async-done(((bf16[16,128,768]{1,2,0:T(8,128)(2,1)}), bf16[16,128,768]{1,2,0:T(8,128)(2,1)S(1)}, u32[]{:S(2)}, u32[]{:S(2)}) %all-to-all-start.1) | async-done | bytes 3145760 | tf_op jit(solution)/shard_map/attn_rows/all_to_all | solution.py:381
  452.0 10.7 %all-to-all-start.2 = ((bf16[8,128,768]{2,1,0:T(8,128)(2,1)}), bf16[8,128,768]{2,1,0:T(8,128)(2,1)S(1)}, u32[]{:S(2)}, u32[]{:S(2)}) async-start(bf16[8,128,768]{2,1,0:T(8,128)(2,1)} %broadcast_in_dim.11), calls=%async_computation.5 | async-start | bytes 3145728 | tf_op jit(solution)/shard_map/attn_columns/all_to_all | solution.py:387
  469.0 16.6 %all-to-all-done.2 = bf16[8,128,768]{2,1,0:T(8,128)(2,1)S(1)} async-done(((bf16[8,128,768]{2,1,0:T(8,128)(2,1)}), bf16[8,128,768]{2,1,0:T(8,128)(2,1)S(1)}, u32[]{:S(2)}, u32[]{:S(2)}) %all-to-all-start.2) | async-done | bytes 1572896 | tf_op jit(solution)/shard_map/attn_columns/all_to_all | solution.py:387
  493.5 2.3 copy-done
  495.9 3.8 shard_map.223
  (285 shorter events, 101.0 us)
Async XLA Ops:
  7.2 53.0 %all-gather.6.cloned.1.call-start = ((), (), s32[]{:S(2)}) async-start(), calls=%async_computation.6 | async-start | bytes 5242880 | tf_op jit(solution)/shard_map/token_gather/all_gather | solution.py:79
  13.0 3.5 collective-permute-start
  18.3 35.4 %all-to-all-start = ((bf16[8,256,640]{2,1,0:T(8,128)(2,1)}), bf16[8,256,640]{2,1,0:T(8,128)(2,1)S(1)}, u32[]{:S(2)}, u32[]{:S(2)}) async-start(bf16[8,256,640]{2,1,0:T(8,128)(2,1)} %broadcast_in_dim.8), calls=%async_computation | async-start | bytes 5242880 | tf_op jit(solution)/shard_map/all_to_all | solution.py:89
  23.3 146.1 %all-gather.8.cloned.1.call-start = ((), (), s32[]{:S(2)}) async-start(), calls=%async_computation.7 | async-start | bytes 10616832 | tf_op jit(solution)/shard_map/unit_gather/all_gather | solution.py:289
  26.3 29.3 %copy-start.36 = (s32[1,2048]{1,0:T(1,128)S(1)}, s32[1,2048]{1,0:T(1,128)}, u32[]{:S(2)}) copy-start(s32[1,2048]{1,0:T(1,128)} %param.17) | copy-start | bytes 24580
  26.3 29.3 %copy-start.37 = (s32[1,2048]{1,0:T(1,128)S(1)}, s32[1,2048]{1,0:T(1,128)}, u32[]{:S(2)}) copy-start(s32[1,2048]{1,0:T(1,128)} %param.16) | copy-start | bytes 24580
  53.7 10.8 %copy-start.5 = (bf16[8,256,640]{2,1,0:T(8,128)(2,1)}, bf16[8,256,640]{2,1,0:T(8,128)(2,1)S(1)}, u32[]{:S(2)}) copy-start(bf16[8,256,640]{2,1,0:T(8,128)(2,1)S(1)} %all-to-all-done) | copy-start | bytes 7864324
  55.5 195.3 %reduce-scatter.4.cloned.1.call-start = ((), (), s32[]{:S(2)}) async-start(), calls=%async_computation.8 | async-start | bytes 3538944 | tf_op jit(solution)/shard_map/down_rows/reduce_scatter | solution.py:395
  56.7 30.5 %copy-start.9 = (f32[512,64]{1,0:T(8,128)}, f32[512,64]{1,0:T(8,128)S(1)}, u32[]{:S(2)}) copy-start(f32[512,64]{1,0:T(8,128)S(1)} %get-tuple-element.136) | copy-start | bytes 393220
  56.7 30.5 %copy-start.11 = (f32[512,64]{1,0:T(8,128)}, f32[512,64]{1,0:T(8,128)S(1)}, u32[]{:S(2)}) copy-start(f32[512,64]{1,0:T(8,128)S(1)} %get-tuple-element.135) | copy-start | bytes 393220
  56.7 5.6 %copy-start.35 = (f32[2048]{0:T(1024)S(1)}, f32[2048]{0:T(1024)}, u32[]{:S(2)}) copy-start(f32[2048]{0:T(1024)} %param.19) | copy-start | bytes 24580
  58.1 7.9 %collective-permute-start.1 = (bf16[2048,384]{1,0:T(8,128)(2,1)}, bf16[2048,384]{1,0:T(8,128)(2,1)}, u32[]{:S(2)}, u32[]{:S(2)}) collective-permute-start(bf16[2048,384]{1,0:T(8,128)(2,1)} %slice.403), channel_id=1, source_target_pairs={{0,1},{1,0},{2,3},{3,2},{4,5},{5,4},{6,7},{7,6},{8,9},{9,8},{10,11... | collective-permute-start | bytes 4718600 | tf_op jit(solution)/shard_map/swap/ppermute | solution.py:40
  70.2 15.2 %collective-permute-start.2 = (bf16[512,256]{1,0:T(8,128)(2,1)S(1)}, bf16[512,256]{1,0:T(8,128)(2,1)S(1)}, u32[]{:S(2)}, u32[]{:S(2)}) collective-permute-start(bf16[512,256]{1,0:T(8,128)(2,1)S(1)} %pad_maximum_fusion.27), channel_id=1, source_target_pairs={{0,8},{8,0},{1,9},{9,1},{2,10},{10,2},{3,11},{11,3},{4,12},{12,4},... | collective-permute-start | bytes 786440 | tf_op jit(solution)/shard_map/ppermute | solution.py:44
  75.5 26.1 %collective-permute-start.4 = (bf16[2048,256]{1,0:T(8,128)(2,1)}, bf16[2048,256]{1,0:T(8,128)(2,1)}, u32[]{:S(2)}, u32[]{:S(2)}) collective-permute-start(bf16[2048,256]{1,0:T(8,128)(2,1)} %slice.424), channel_id=1, source_target_pairs={{0,1},{1,0},{2,3},{3,2},{4,5},{5,4},{6,7},{7,6},{8,9},{9,8},{10,11... | collective-permute-start | bytes 3145736 | tf_op jit(solution)/shard_map/swap/ppermute | solution.py:40
  85.5 3.0 collective-permute-start.3
  106.9 13.4 %collective-permute-start.7 = (bf16[128,2048]{1,0:T(8,128)(2,1)}, bf16[128,2048]{1,0:T(8,128)(2,1)}, u32[]{:S(2)}, u32[]{:S(2)}) collective-permute-start(bf16[128,2048]{1,0:T(8,128)(2,1)} %get-tuple-element.61), channel_id=1, source_target_pairs={{0,6},{2,0},{4,2},{6,4},{1,7},{3,1},{5,3},{7,5},{8,14},{10,8},{12,... | collective-permute-start | bytes 1572872 | tf_op jit(solution)/shard_map/attn_scatter/ppermute | solution.py:54
  108.2 15.2 %collective-permute-start.6 = (bf16[128,2048]{1,0:T(8,128)(2,1)}, bf16[128,2048]{1,0:T(8,128)(2,1)}, u32[]{:S(2)}, u32[]{:S(2)}) collective-permute-start(bf16[128,2048]{1,0:T(8,128)(2,1)} %get-tuple-element.62), channel_id=1, source_target_pairs={{0,2},{2,4},{4,6},{6,0},{1,3},{3,5},{5,7},{7,1},{8,10},{10,12},{12... | collective-permute-start | bytes 1572872 | tf_op jit(solution)/shard_map/attn_scatter/ppermute | solution.py:54
  108.4 24.6 %collective-permute-start.5 = (bf16[128,2048]{1,0:T(8,128)(2,1)}, bf16[128,2048]{1,0:T(8,128)(2,1)}, u32[]{:S(2)}, u32[]{:S(2)}) collective-permute-start(bf16[128,2048]{1,0:T(8,128)(2,1)} %get-tuple-element.60), channel_id=1, source_target_pairs={{0,4},{2,6},{4,0},{6,2},{1,5},{3,7},{5,1},{7,3},{8,12},{10,14},{12... | collective-permute-start | bytes 1572872 | tf_op jit(solution)/shard_map/attn_scatter/ppermute | solution.py:54
  133.0 3.4 copy-start.34
  137.3 13.1 %collective-permute-start.9 = (bf16[128,2048]{1,0:T(8,128)(2,1)}, bf16[128,2048]{1,0:T(8,128)(2,1)}, u32[]{:S(2)}, u32[]{:S(2)}) collective-permute-start(bf16[128,2048]{1,0:T(8,128)(2,1)} %multiply_convert_fusion.9), channel_id=1, source_target_pairs={{0,4},{2,6},{4,0},{6,2},{1,5},{3,7},{5,1},{7,3},{8,12},{10,14},{12... | collective-permute-start | bytes 1572872 | tf_op jit(solution)/shard_map/ffn_gather/ppermute | solution.py:54
  138.6 25.7 %collective-permute-start.10 = (bf16[128,2048]{1,0:T(8,128)(2,1)}, bf16[128,2048]{1,0:T(8,128)(2,1)}, u32[]{:S(2)}, u32[]{:S(2)}) collective-permute-start(bf16[128,2048]{1,0:T(8,128)(2,1)} %multiply_convert_fusion.9), channel_id=1, source_target_pairs={{0,2},{2,4},{4,6},{6,0},{1,3},{3,5},{5,7},{7,1},{8,10},{10,12},{12... | collective-permute-start | bytes 1572872 | tf_op jit(solution)/shard_map/ffn_gather/ppermute | solution.py:54
  138.9 25.3 %collective-permute-start.8 = (bf16[128,2048]{1,0:T(8,128)(2,1)}, bf16[128,2048]{1,0:T(8,128)(2,1)}, u32[]{:S(2)}, u32[]{:S(2)}) collective-permute-start(bf16[128,2048]{1,0:T(8,128)(2,1)} %multiply_convert_fusion.9), channel_id=1, source_target_pairs={{0,6},{2,0},{4,2},{6,4},{1,7},{3,1},{5,3},{7,5},{8,14},{10,8},{12,... | collective-permute-start | bytes 1572872 | tf_op jit(solution)/shard_map/ffn_gather/ppermute | solution.py:54
  170.7 15.7 %collective-permute-start.11 = (bf16[2048,2304]{1,0:T(8,128)(2,1)}, bf16[2048,2304]{1,0:T(8,128)(2,1)S(1)}, u32[]{:S(2)}, u32[]{:S(2)}) collective-permute-start(bf16[2048,2304]{1,0:T(8,128)(2,1)} %constant_dynamic-update-slice_fusion.11), channel_id=1, source_target_pairs={{0,1},{1,0},{2,3},{3,2},{4,5},{5,4},{6,7},{7,6},{8,9},{9,8},{10,11... | collective-permute-start | bytes 28311560 | tf_op jit(solution)/shard_map/swap/ppermute | solution.py:40
  173.9 4.4 copy-start.40
  185.1 16.1 %copy-start.42 = (bf16[512,768]{1,0:T(8,128)(2,1)}, bf16[512,768]{1,0:T(8,128)(2,1)S(1)}, u32[]{:S(2)}) copy-start(bf16[512,768]{1,0:T(8,128)(2,1)S(1)} %get-tuple-element.64) | copy-start | bytes 2359300
  186.4 3.7 copy-start.41
  195.4 5.9 %collective-permute-start.15 = (bf16[2048,768]{1,0:T(8,128)(2,1)S(1)}, bf16[2048,768]{1,0:T(8,128)(2,1)S(1)}, u32[]{:S(2)}, u32[]{:S(2)}) collective-permute-start(bf16[2048,768]{1,0:T(8,128)(2,1)S(1)} %convolution_convert_fusion.1), channel_id=1, source_target_pairs={{0,1},{1,0},{2,3},{3,2},{4,5},{5,4},{6,7},{7,6},{8,9},{9,8},{10,11... | collective-permute-start | bytes 9437192 | tf_op jit(solution)/shard_map/swap/ppermute | solution.py:40
  204.9 79.5 %all-gather.10.cloned.1.call-start = ((), (), s32[]{:S(2)}) async-start(), calls=%async_computation.9 | async-start | bytes 2621440 | tf_op jit(solution)/shard_map/d_attn_gather/all_gather | solution.py:79
  212.9 25.8 %copy-start.3 = (f32[128,2048]{1,0:T(8,128)S(1)}, f32[128,2048]{1,0:T(8,128)}, u32[]{:S(2)}) copy-start(f32[128,2048]{1,0:T(8,128)} %copy-done.2) | copy-start | bytes 3145732
  213.1 13.4 %collective-permute-start.14 = (bf16[128,2048]{1,0:T(8,128)(2,1)S(1)}, bf16[128,2048]{1,0:T(8,128)(2,1)S(1)}, u32[]{:S(2)}, u32[]{:S(2)}) collective-permute-start(bf16[128,2048]{1,0:T(8,128)(2,1)S(1)} %get-tuple-element.58), channel_id=1, source_target_pairs={{0,6},{2,0},{4,2},{6,4},{1,7},{3,1},{5,3},{7,5},{8,14},{10,8},{12,... | collective-permute-start | bytes 1572872 | tf_op jit(solution)/shard_map/d_ffn_scatter/ppermute | solution.py:54
  214.2 15.2 %collective-permute-start.13 = (bf16[128,2048]{1,0:T(8,128)(2,1)S(1)}, bf16[128,2048]{1,0:T(8,128)(2,1)S(1)}, u32[]{:S(2)}, u32[]{:S(2)}) collective-permute-start(bf16[128,2048]{1,0:T(8,128)(2,1)S(1)} %get-tuple-element.59), channel_id=1, source_target_pairs={{0,2},{2,4},{4,6},{6,0},{1,3},{3,5},{5,7},{7,1},{8,10},{10,12},{12... | collective-permute-start | bytes 1572872 | tf_op jit(solution)/shard_map/d_ffn_scatter/ppermute | solution.py:54
  214.7 25.8 %copy-start.16 = (bf16[512,2048]{1,0:T(8,128)(2,1)S(1)}, bf16[512,2048]{1,0:T(8,128)(2,1)}, u32[]{:S(2)}) copy-start(bf16[512,2048]{1,0:T(8,128)(2,1)} %copy.132) | copy-start | bytes 6291460
  214.7 26.5 %copy-start.45 = (bf16[512,768]{1,0:T(8,128)(2,1)S(1)}, bf16[512,768]{1,0:T(8,128)(2,1)}, u32[]{:S(2)}) copy-start(bf16[512,768]{1,0:T(8,128)(2,1)} %get-tuple-element.48) | copy-start | bytes 2359300
  214.7 26.5 %copy-start.46 = (bf16[512,768]{1,0:T(8,128)(2,1)S(1)}, bf16[512,768]{1,0:T(8,128)(2,1)}, u32[]{:S(2)}) copy-start(bf16[512,768]{1,0:T(8,128)(2,1)} %get-tuple-element.49) | copy-start | bytes 2359300
  214.7 24.0 %collective-permute-start.12 = (bf16[128,2048]{1,0:T(8,128)(2,1)S(1)}, bf16[128,2048]{1,0:T(8,128)(2,1)S(1)}, u32[]{:S(2)}, u32[]{:S(2)}) collective-permute-start(bf16[128,2048]{1,0:T(8,128)(2,1)S(1)} %get-tuple-element.57), channel_id=1, source_target_pairs={{0,4},{2,6},{4,0},{6,2},{1,5},{3,7},{5,1},{7,3},{8,12},{10,14},{12... | collective-permute-start | bytes 1572872 | tf_op jit(solution)/shard_map/d_ffn_scatter/ppermute | solution.py:54
  241.2 5.7 %copy-start.17 = (bf16[512,2048]{1,0:T(8,128)(2,1)}, bf16[512,2048]{1,0:T(8,128)(2,1)S(1)}, u32[]{:S(2)}) copy-start(bf16[512,2048]{1,0:T(8,128)(2,1)S(1)} %constant_dynamic-update-slice_fusion.4) | copy-start | bytes 6291460
  241.2 8.0 %copy-start.26 = (bf16[1,256,2048]{2,1,0:T(8,128)(2,1)S(1)}, bf16[1,256,2048]{2,1,0:T(8,128)(2,1)}, u32[]{:S(2)}) copy-start(bf16[1,256,2048]{2,1,0:T(8,128)(2,1)} %param.15) | copy-start | bytes 3145732
  246.9 12.4 %collective-permute-start.26 = (bf16[2048,1536]{1,0:T(8,128)(2,1)}, bf16[2048,1536]{1,0:T(8,128)(2,1)}, u32[]{:S(2)}, u32[]{:S(2)}) collective-permute-start(bf16[2048,1536]{1,0:T(8,128)(2,1)} %convolution_convert_fusion), channel_id=1, source_target_pairs={{0,1},{1,0},{2,3},{3,2},{4,5},{5,4},{6,7},{7,6},{8,9},{9,8},{10,11... | collective-permute-start | bytes 18874376 | tf_op jit(solution)/shard_map/swap/ppermute | solution.py:40
  254.0 130.9 %reduce-scatter.8.cloned.1.call-start = ((), (), s32[]{:S(2)}) async-start(), calls=%async_computation.11 | async-start | bytes 7077888 | tf_op jit(solution)/shard_map/gate_up_rows/reduce_scatter | solution.py:395
  287.6 177.3 %reduce-scatter.6.cloned.1.call-start = ((), (), s32[]{:S(2)}) async-start(), calls=%async_computation.10 | async-start | bytes 2621440 | tf_op jit(solution)/shard_map/d_attn_scatter/reduce_scatter | solution.py:84
  289.0 4.0 copy-start.44
  323.3 4.2 copy-start.25
  323.5 23.7 %collective-permute-start.20 = (bf16[1024,256]{1,0:T(8,128)(2,1)S(1)}, bf16[1024,256]{1,0:T(8,128)(2,1)S(1)}, u32[]{:S(2)}, u32[]{:S(2)}) collective-permute-start(bf16[1024,256]{1,0:T(8,128)(2,1)S(1)} %pad_maximum_fusion.20), channel_id=1, source_target_pairs={{0,1},{1,0},{2,3},{3,2},{4,5},{5,4},{6,7},{7,6},{8,9},{9,8},{10,11... | collective-permute-start | bytes 1572872 | tf_op jit(solution)/shard_map/swap/ppermute | solution.py:40
  324.7 21.2 %collective-permute-start.22 = (bf16[256,768]{1,0:T(8,128)(2,1)S(1)}, bf16[256,768]{1,0:T(8,128)(2,1)S(1)}, u32[]{:S(2)}, u32[]{:S(2)}) collective-permute-start(bf16[256,768]{1,0:T(8,128)(2,1)S(1)} %constant_dynamic-update-slice_fusion.6), channel_id=1, source_target_pairs={{0,8},{8,0},{1,9},{9,1},{2,10},{10,2},{3,11},{11,3},{4,12},{12,4},... | collective-permute-start | bytes 1179656 | tf_op jit(solution)/shard_map/down_y/ppermute | solution.py:44
  327.8 22.4 %collective-permute-start.18 = (bf16[128,2048]{1,0:T(8,128)(2,1)S(1)}, bf16[128,2048]{1,0:T(8,128)(2,1)S(1)}, u32[]{:S(2)}, u32[]{:S(2)}) collective-permute-start(bf16[128,2048]{1,0:T(8,128)(2,1)S(1)} %get-tuple-element.55), channel_id=1, source_target_pairs={{0,6},{2,0},{4,2},{6,4},{1,7},{3,1},{5,3},{7,5},{8,14},{10,8},{12,... | collective-permute-start | bytes 1572872 | tf_op jit(solution)/shard_map/branch_scatter/ppermute | solution.py:54
  328.4 21.8 %collective-permute-start.17 = (bf16[128,2048]{1,0:T(8,128)(2,1)S(1)}, bf16[128,2048]{1,0:T(8,128)(2,1)S(1)}, u32[]{:S(2)}, u32[]{:S(2)}) collective-permute-start(bf16[128,2048]{1,0:T(8,128)(2,1)S(1)} %get-tuple-element.56), channel_id=1, source_target_pairs={{0,2},{2,4},{4,6},{6,0},{1,3},{3,5},{5,7},{7,1},{8,10},{10,12},{12... | collective-permute-start | bytes 1572872 | tf_op jit(solution)/shard_map/branch_scatter/ppermute | solution.py:54
  329.4 23.9 %collective-permute-start.16 = (bf16[128,2048]{1,0:T(8,128)(2,1)S(1)}, bf16[128,2048]{1,0:T(8,128)(2,1)S(1)}, u32[]{:S(2)}, u32[]{:S(2)}) collective-permute-start(bf16[128,2048]{1,0:T(8,128)(2,1)S(1)} %get-tuple-element.54), channel_id=1, source_target_pairs={{0,4},{2,6},{4,0},{6,2},{1,5},{3,7},{5,1},{7,3},{8,12},{10,14},{12... | collective-permute-start | bytes 1572872 | tf_op jit(solution)/shard_map/branch_scatter/ppermute | solution.py:54
  330.7 35.2 %copy-start.29 = (bf16[512,256]{1,0:T(8,128)(2,1)}, bf16[512,256]{1,0:T(8,128)(2,1)S(1)}, u32[]{:S(2)}) copy-start(bf16[512,256]{1,0:T(8,128)(2,1)S(1)} %get-tuple-element.111) | copy-start | bytes 786436
  330.8 22.5 %copy-start.4 = (f32[128,2048]{1,0:T(8,128)S(1)}, f32[128,2048]{1,0:T(8,128)}, u32[]{:S(2)}) copy-start(f32[128,2048]{1,0:T(8,128)} %copy-done.2) | copy-start | bytes 3145732
  347.4 15.5 %copy-start.10 = (f32[512,64]{1,0:T(8,128)S(1)}, f32[512,64]{1,0:T(8,128)}, u32[]{:S(2)}) copy-start(f32[512,64]{1,0:T(8,128)} %copy-done.9) | copy-start | bytes 393220
  347.4 15.4 %collective-permute-start.21 = (bf16[512,256]{1,0:T(8,128)(2,1)S(1)}, bf16[512,256]{1,0:T(8,128)(2,1)S(1)}, u32[]{:S(2)}, u32[]{:S(2)}) collective-permute-start(bf16[512,256]{1,0:T(8,128)(2,1)S(1)} %slice.623), channel_id=1, source_target_pairs={{0,8},{8,0},{1,9},{9,1},{2,10},{10,2},{3,11},{11,3},{4,12},{12,4},... | collective-permute-start | bytes 786440 | tf_op jit(solution)/shard_map/ppermute | solution.py:44
  354.5 8.7 %copy-start.12 = (f32[512,64]{1,0:T(8,128)S(1)}, f32[512,64]{1,0:T(8,128)}, u32[]{:S(2)}) copy-start(f32[512,64]{1,0:T(8,128)} %copy-done.11) | copy-start | bytes 393220
  372.6 3.8 copy-start.39
  374.8 7.8 %collective-permute-start.24 = (bf16[2048,384]{0,1:T(8,128)(2,1)S(1)}, bf16[2048,384]{0,1:T(8,128)(2,1)S(1)}, u32[]{:S(2)}, u32[]{:S(2)}) collective-permute-start(bf16[2048,384]{0,1:T(8,128)(2,1)S(1)} %convolution_convert_fusion.2), channel_id=1, source_target_pairs={{0,1},{1,0},{2,3},{3,2},{4,5},{5,4},{6,7},{7,6},{8,9},{9,8},{10,11... | collective-permute-start | bytes 4718600 | tf_op jit(solution)/shard_map/swap/ppermute | solution.py:40
  377.2 3.8 collective-permute-start.25
  384.9 20.6 %collective-permute-start.29 = (bf16[256,1536]{1,0:T(8,128)(2,1)}, bf16[256,1536]{1,0:T(8,128)(2,1)}, u32[]{:S(2)}, u32[]{:S(2)}) collective-permute-start(bf16[256,1536]{1,0:T(8,128)(2,1)} %reduce-scatter.8.cloned.1.call-done), channel_id=1, source_target_pairs={{0,8},{8,0},{1,9},{9,1},{2,10},{10,2},{3,11},{11,3},{4,12},{12,4},... | collective-permute-start | bytes 2359304 | tf_op jit(solution)/shard_map/gate_up_y/ppermute | solution.py:44
  390.8 56.9 %all-to-all-start.1 = ((bf16[16,128,768]{1,2,0:T(8,128)(2,1)}), bf16[16,128,768]{1,2,0:T(8,128)(2,1)S(1)}, u32[]{:S(2)}, u32[]{:S(2)}) async-start(bf16[16,128,768]{1,2,0:T(8,128)(2,1)} %copy_bitcast_fusion), calls=%async_computation.3 | async-start | bytes 6291456 | tf_op jit(solution)/shard_map/attn_rows/all_to_all | solution.py:381
  395.4 98.2 %all-gather.12.cloned.1.call-start = ((), (), s32[]{:S(2)}) async-start(), calls=%async_computation.12 | async-start | bytes 5898240 | tf_op jit(solution)/shard_map/unit_columns/all_gather | solution.py:438
  408.2 54.4 %collective-permute-start.19 = (bf16[128,2048]{1,0:T(8,128)(2,1)}, bf16[128,2048]{1,0:T(8,128)(2,1)}, u32[]{:S(2)}, u32[]{:S(2)}) collective-permute-start(bf16[128,2048]{1,0:T(8,128)(2,1)} %get-tuple-element.39), channel_id=1, source_target_pairs={{0,1},{1,0},{2,3},{3,2},{4,5},{5,4},{6,7},{7,6},{8,9},{9,8},{10,11... | collective-permute-start | bytes 1572872 | tf_op jit(solution)/shard_map/swap/ppermute | solution.py:40
  450.7 11.9 %copy-start.20 = (bf16[128,2048]{1,0:T(8,128)(2,1)S(1)}, bf16[128,2048]{1,0:T(8,128)(2,1)}, u32[]{:S(2)}) copy-start(bf16[128,2048]{1,0:T(8,128)(2,1)} %get-tuple-element.39) | copy-start | bytes 1572868
  452.0 33.6 %all-to-all-start.2 = ((bf16[8,128,768]{2,1,0:T(8,128)(2,1)}), bf16[8,128,768]{2,1,0:T(8,128)(2,1)S(1)}, u32[]{:S(2)}, u32[]{:S(2)}) async-start(bf16[8,128,768]{2,1,0:T(8,128)(2,1)} %broadcast_in_dim.11), calls=%async_computation.5 | async-start | bytes 3145728 | tf_op jit(solution)/shard_map/attn_columns/all_to_all | solution.py:387
  468.1 18.7 %collective-permute-start.23 = (bf16[128,2048]{1,0:T(8,128)(2,1)S(1)}, bf16[128,2048]{1,0:T(8,128)(2,1)S(1)}, u32[]{:S(2)}, u32[]{:S(2)}) collective-permute-start(bf16[128,2048]{1,0:T(8,128)(2,1)S(1)} %fusion.27), channel_id=1, source_target_pairs={{0,1},{1,0},{2,3},{3,2},{4,5},{5,4},{6,7},{7,6},{8,9},{9,8},{10,11... | collective-permute-start | bytes 1572872 | tf_op jit(solution)/shard_map/swap/ppermute | solution.py:40
  485.9 3.6 collective-permute-start.28
  486.9 1.8 collective-permute-start.27
  (25 other events, 53.7 us)
Sparse Core Ops, SparseCore 0:
  10.6 49.5 all-gather.5
  61.8 105.2 all-gather.7
  205.0 40.6 reduce-scatter.3
  254.1 30.2 all-gather.9
  287.7 84.5 reduce-scatter.7
  375.2 30.6 reduce-scatter.5
  408.3 53.5 all-gather.11

commit v4 on v3

--- a/solution.py
+++ b/solution.py
@@ -70,8 +70,8 @@
 def scatter_x(value, name):
     x_at = lax.axis_index("x")
     with jax.named_scope(name):
-        moved = [shift_x(half(chunk(value, x_at + hop)), hop) for hop in (2, 1, 3)]
-    return chunk(value, x_at) + sum(part.astype(F32) for part in moved)
+        moved = [shift_x(chunk(value, x_at + hop), hop) for hop in (2, 1, 3)]
+    return sum((part.astype(F32) for part in moved), chunk(value, x_at).astype(F32))
 
 
 def gather_x_async(value, name):
@@ -151,6 +151,9 @@
         ],
         scratch_shapes=[pltpu.VMEM((rows, n), F32)],
         compiler_params=pltpu.CompilerParams(vmem_limit_bytes=VMEM),
+        cost_estimate=pl.CostEstimate(
+            flops=8 * count * features * n, transcendentals=count * features // HD * n, bytes_accessed=2**22
+        ),
     )(query, keys_t, values, query_tags, key_tags_t)
 
 
@@ -212,7 +215,45 @@
         ],
         scratch_shapes=[pltpu.VMEM((n, count), F32)],
         compiler_params=pltpu.CompilerParams(vmem_limit_bytes=VMEM),
+        cost_estimate=pl.CostEstimate(
+            flops=20 * count * features * n, transcendentals=count * features // HD * n, bytes_accessed=2**23
+        ),
     )(query, d_heads, mixed, lse, keys, keys_t, values, key_tags, query_tags_t, cosine, sine)
+
+
+def place_heads_kernel(core_ref, mine_ref, theirs_ref, q_ref, k_ref, v_ref, o_ref):
+    def place(first_ref, second_ref):
+        for y in range(2):
+            rows = pl.ds(y * first_ref.shape[2], first_ref.shape[2])
+            for x in range(2):
+                for i, ref in enumerate((first_ref, second_ref)):
+                    lane = x * 512 + i * 256
+                    q_ref[rows, lane : lane + 256] = ref[y, x, :, :256].astype(F32)
+                    o_ref[rows, lane : lane + 256] = ref[y, x, :, 384:].astype(F32)
+                k_ref[rows, x * HD : (x + 1) * HD] = first_ref[y, x, :, 256:384].astype(F32)
+                v_ref[rows, x * HD : (x + 1) * HD] = second_ref[y, x, :, 256:384].astype(F32)
+
+    @pl.when(core_ref[0] == 0)
+    def _():
+        place(mine_ref, theirs_ref)
+
+    @pl.when(core_ref[0] != 0)
+    def _():
+        place(theirs_ref, mine_ref)
+
+
+def place_heads(core, mine, theirs):
+    rows = 2 * mine.shape[2]
+    return pl.pallas_call(
+        place_heads_kernel,
+        in_specs=[
+            pl.BlockSpec(memory_space=pltpu.SMEM),
+            pl.BlockSpec(memory_space=pltpu.VMEM),
+            pl.BlockSpec(memory_space=pltpu.VMEM),
+        ],
+        out_shape=[jax.ShapeDtypeStruct((rows, columns), F32) for columns in (1024, 256, 256, 1024)],
+        compiler_params=pltpu.CompilerParams(vmem_limit_bytes=VMEM),
+    )(core.reshape(1).astype(jnp.int32), mine, theirs)
 
 
 def spread_kernel(parts_ref, *out_refs, tiles, spare):
@@ -334,7 +375,7 @@
     heads_f, heads, lse = attend(query, keys_t, all_values, query_tags, key_tags_t)
 
     attn_branch = mm_nt(heads[:, :256], packs_out[0]) + mm_nt(heads[:, 256:], packs_out[1])
-    attn_branch = scatter_x(attn_branch, "attn_scatter")
+    attn_branch = scatter_x(half(attn_branch), "attn_scatter")
     middle = xval + keep * attn_branch
     root_ffn = norm_root(middle)
     normed_ffn = jnp.concatenate(gather_x(half(middle * root_ffn * gain_ffn), "ffn_gather"), axis=0)
@@ -361,7 +402,7 @@
         d_gus.append(d_gu)
         hiddens.append(hidden)
     grads_down = [mm_tn(d_ffn, hidden) for hidden in hiddens]
-    d_normed_ffn = scatter_x(d_normed, "d_ffn_scatter")
+    d_normed_ffn = scatter_x(half(d_normed), "d_ffn_scatter")
     left_gu = after(normed_ffn, d_normed_ffn)
     grads_gu = [mm_tn(left_gu, d_gu) for d_gu in d_gus]
     d_middle = grad_top + norm_backward(middle, root_ffn, gain_ffn, d_normed_ffn)
@@ -394,29 +435,28 @@
         with jax.named_scope(name + "_rows"):
             return lax.psum_scatter(value, SHARD, scatter_dimension=0, tiled=True)
 
-    def halves(value, name):
+    def halves(value, name, *others):
         with jax.named_scope(name + "_y"):
-            return half(value.astype(F32) + across_y(value).astype(F32))
+            came = after(across_y(value), *others) if others else across_y(value)
+            return half(value.astype(F32) + came.astype(F32))
 
     sum_down, sum_gu = sum_cores(*grads_down), sum_cores(*grads_gu)
     rows_down = samples(sum_down, "down")
     d_attn = gather_x_async(after(half(keep * d_middle), rows_down), "d_attn_gather")
-    rows_gu = samples(after(sum_gu, d_attn), "gate_up")
-    d_attn = after(d_attn, branch)
-    unit_down = halves(after(rows_down, d_attn), "down")
-    ffn_branch = scatter_x(after(branch, d_attn), "branch_scatter")
+    unit_down = halves(rows_down, "down")
+    ffn_branch = scatter_x(after(half(branch), d_attn), "branch_scatter")
+    rows_gu = samples(after(sum_gu, d_attn, unit_down), "gate_up")
     output = both_cores(half(middle + keep * ffn_branch))
 
     d_heads = jnp.concatenate([half(mm(d_attn, part)) for part in packs_out], axis=1)
     d_query, key_part, value_part = attend_back(
         query, d_heads, heads_f, lse, all_keys, keys_t, all_values, key_tags, query_tags_t, cosine, sine
     )
-    kv_part = jnp.concatenate([key_part, value_part], axis=1)
+    kv_part = after(jnp.concatenate([key_part, value_part], axis=1), ffn_branch)
     kv_mine = jnp.concatenate([kv_part[:count], kv_part[2 * count : 3 * count]], axis=0)
     kv_theirs = jnp.concatenate([kv_part[count : 2 * count], kv_part[3 * count :]], axis=0)
     kv_two = kv_mine + swap_cores(half(kv_theirs)).astype(F32)
     grad_kv = kv_two[:count] + across_y(half(kv_two[count:])).astype(F32)
-    grad_kv = after(grad_kv, ffn_branch, unit_down)
     d_key = half(unrotate(grad_kv[:, :HD], cosine, sine))
     d_value = half(grad_kv[:, HD:])
     d_own = jnp.concatenate([d_query[:, :256], jnp.where(first, d_key, d_value)], axis=1)
@@ -433,26 +473,17 @@
     sums = jnp.concatenate([sums, jnp.pad(gains, ((0, 0), (0, HD - 2)))], axis=1)
     total_rows = after(reduce_rows(sums, "attn"), rows_gu)
     packs = columns(total_rows, "attn")
-    unit_rows = jnp.concatenate([halves(rows_gu, "gate_up"), unit_down], axis=1)
+    unit_rows = jnp.concatenate([halves(rows_gu, "gate_up", sum_qkv, sum_out), unit_down], axis=1)
     with jax.named_scope("unit_columns"):
         parts = lax.all_gather(unit_rows, "x", axis=0, tiled=False)
     grad_gate, grad_up, grad_down = spread(parts, tiles, spare)
-    packs = jnp.stack([rows_of(packs, i) for i in range(4)])
-    gains = jnp.sum(packs[:, :, 640:642].astype(F32), axis=0)
+    packs = after(packs.reshape(width // 2, -1), grad_gate).reshape(packs.shape)
+    gains = jnp.sum(packs[..., 640:642].astype(F32), axis=1).reshape(-1, 2)
     gains = (gains + swap_cores(gains)).T
-    packs = packs[:, :, :640]
-    mine = lax.dynamic_slice_in_dim(packs, 2 * core, 2, axis=0)
-    theirs = swap_cores(lax.dynamic_slice_in_dim(packs, 2 - 2 * core, 2, axis=0))
-    out0 = jnp.where(first, mine, theirs).astype(F32)
-    out1 = jnp.where(first, theirs, mine).astype(F32)
-    grad_query = jnp.concatenate(
-        [out0[0, :, :256], out1[0, :, :256], out0[1, :, :256], out1[1, :, :256]], axis=1
-    )
-    grad_key = jnp.concatenate([out0[0, :, 256:384], out0[1, :, 256:384]], axis=1)
-    grad_value = jnp.concatenate([out1[0, :, 256:384], out1[1, :, 256:384]], axis=1)
-    grad_out = jnp.concatenate(
-        [out0[0, :, 384:], out1[0, :, 384:], out0[1, :, 384:], out1[1, :, 384:]], axis=1
-    )
+    packs = packs[..., :640]
+    mine = lax.dynamic_slice_in_dim(packs, 2 * core, 2, axis=1)
+    theirs = swap_cores(lax.dynamic_slice_in_dim(packs, 2 - 2 * core, 2, axis=1))
+    grad_query, grad_key, grad_value, grad_out = place_heads(core, mine, theirs)
     return (
         output[None], input_grad[None], gains[0], gains[1],
         grad_query, grad_key, grad_value, grad_out, grad_gate, grad_up, grad_down,

time: 514 us -> 494 us (0.961)
  waiting for transfers between devices: 215 us -> 198 us
  other arithmetic: 45.6 us -> 37.8 us
    all_to_all x1, waiting for transfers between devices: 16.6 us -> 0.44 us  [columns(): parts = lax.all_to_all(spread, ('yh', 'x'), 0, 0)]
    ppermute x4, waiting for transfers between devices: 41.4 us -> 31.1 us  [across_y(): return lax.ppermute(value, 'yh', SWAP)]
    all_gather x1, waiting for transfers between devices: 0.01 us -> 9.52 us  [per_device(): parts = lax.all_gather(unit_rows, 'x', axis=0, tiled=False)]
    ppermute x13, waiting for transfers between devices: 10.5 us -> 5.22 us  [swap_cores(): return lax.ppermute(value, 'tp', SWAP)]
    reduce_scatter x2, waiting for transfers between devices: 0.01 us -> 5.16 us  [samples(): return lax.psum_scatter(value, SHARD, scatter_dimension=0, tiled=True)]
    unnamed x106 -> x115, local copies, waits for them, and re-layouts: 23.6 us -> 21.3 us
  transfers between devices with their start and end apart: 40 -> 40, of which waited for: 24 -> 24; matrix products, arithmetic and copies ran while one was open for 28% -> 28% of each run, Pallas kernels for 5% -> 6%
where the time goes in v4:
time: 494 us; the launch traced here: 484 us
  waiting for transfers between devices  198 us (40%)
  matrix products  81.5 us (16%)
  starting transfers between devices  60.7 us (12%)
  local copies, waits for them, and re-layouts  50.7 us (10%)
  other arithmetic  37.8 us (8%)
  Pallas kernels  31.5 us (6%)
  between operations  24.2 us (5%)
    ppermute x12, waiting for transfers between devices, shift_x(): return lax.ppermute(value, 'x', [(i, (i + hop) % 4) for i in range(4)])  71.4 us
    all_to_all x1, waiting for transfers between devices, reduce_rows(): lax.all_to_all(value.reshape(16, width // 16, -1), ('yl', 'z', 'yh'), 0, 0)  36.9 us
    ppermute x4, waiting for transfers between devices, across_y(): return lax.ppermute(value, 'yh', SWAP)  31.1 us
    dot_general x8, matrix products, mm_tn(): lax.dot_general(left, right, (((0,), (0,)), ((), ())), preferred_element_...  30.7 us
    dot_general x8, matrix products, mm_nt(): lax.dot_general(left, right, (((1,), (1,)), ((), ())), preferred_element_...  30.6 us
    unnamed x115, local copies, waits for them, and re-layouts  21.3 us
    dot_general x8, matrix products, mm(): return jnp.dot(left, right, preferred_element_type=F32)  20.2 us
    all_to_all x1, waiting for transfers between devices, gather_shard(): return lax.all_to_all(spread, SHARD, 0, 0).reshape(-1, value.shape[1])  19.6 us
  transfers between devices with their start and end apart: 40, of which 24 were waited for; matrix products, arithmetic and copies ran while one was open for 28% of the time, Pallas kernels for 6%

profile of v4, /device:TPU:97, one launch (start us, length us, event | category | flops | bytes accessed | tf_op | source)
XLA Modules:
  0.0 484.2 jit_solution(10225390043991749446)
XLA Ops:
  14.3 2.2 collective-permute-done
  18.3 5.0 %all-to-all-start = ((bf16[8,256,640]{2,1,0:T(8,128)(2,1)}), bf16[8,256,640]{2,1,0:T(8,128)(2,1)S(1)}, u32[]{:S(2)}, u32[]{:S(2)}) async-start(bf16[8,256,640]{2,1,0:T(8,128)(2,1)} %broadcast_in_dim.8), calls=%async_computation | async-start | bytes 5242880 | tf_op jit(solution)/shard_map/all_to_all | solution.py:89
  26.3 1.9 constant_dynamic-update-slice_fusion
  31.6 1.9 fusion.29
  34.1 19.6 %all-to-all-done = bf16[8,256,640]{2,1,0:T(8,128)(2,1)S(1)} async-done(((bf16[8,256,640]{2,1,0:T(8,128)(2,1)}), bf16[8,256,640]{2,1,0:T(8,128)(2,1)S(1)}, u32[]{:S(2)}, u32[]{:S(2)}) %all-to-all-start) | async-done | bytes 2621472 | tf_op jit(solution)/shard_map/all_to_all | solution.py:89
  60.2 2.1 multiply_reduce_fusion.1
  62.3 2.1 multiply_convert_fusion.1
  66.0 2.7 fusion.78
  70.2 2.8 collective-permute-start.2
  73.3 2.3 slice.363
  76.5 9.0 %collective-permute-done.2 = bf16[512,256]{1,0:T(8,128)(2,1)S(1)} collective-permute-done((bf16[512,256]{1,0:T(8,128)(2,1)S(1)}, bf16[512,256]{1,0:T(8,128)(2,1)S(1)}, u32[]{:S(2)}, u32[]{:S(2)}) %collective-permute-start.2) | collective-permute-done | bytes 262176 | tf_op jit(solution)/shard_map/ppermute | solution.py:44
  89.2 10.1 %shard_map.221 = (f32[512,512]{1,0:T(8,128)S(1)}, bf16[512,512]{1,0:T(8,128)(2,1)S(1)}, f32[4,8,512]{2,1,0:T(8,128)S(1)}) custom-call(bf16[512,512]{1,0:T(8,128)(2,1)S(1)} %pad_maximum_fusion.13.q_ref, bf16[128,2048]{1,0:T(8,128)(2,1)S(1)} %copy.96.kt_ref, bf16[2048,128]{1,0:T(8,128)(2,1)S(1)} %get-tuple-element.87.v_ref, s32[512,2]{1,0:T(8,128)S(1)} %copy.97.rows_ref, ...), custom_call_target="tpu_custom_call" | custom-call | flops 4294967296 | bytes 4194304 | tf_op jit(solution)/shard_map/pallas_call | solution.py:136
  99.3 2.3 fusion.47
  101.6 2.0 add_convert_fusion.4
  108.0 2.5 collective-permute-start.7
  111.2 10.0 %collective-permute-done.5 = bf16[128,2048]{1,0:T(8,128)(2,1)} collective-permute-done((bf16[128,2048]{1,0:T(8,128)(2,1)}, bf16[128,2048]{1,0:T(8,128)(2,1)}, u32[]{:S(2)}, u32[]{:S(2)}) %collective-permute-start.5) | collective-permute-done | bytes 524320 | tf_op jit(solution)/shard_map/attn_scatter/ppermute | solution.py:54
  121.2 11.9 %collective-permute-done.6 = bf16[128,2048]{1,0:T(8,128)(2,1)} collective-permute-done((bf16[128,2048]{1,0:T(8,128)(2,1)}, bf16[128,2048]{1,0:T(8,128)(2,1)}, u32[]{:S(2)}, u32[]{:S(2)}) %collective-permute-start.6) | collective-permute-done | bytes 524320 | tf_op jit(solution)/shard_map/attn_scatter/ppermute | solution.py:54
  133.1 2.3 multiply_reduce_fusion.4
  137.5 2.5 collective-permute-start.8
  140.0 12.0 %collective-permute-done.10 = bf16[128,2048]{1,0:T(8,128)(2,1)} collective-permute-done((bf16[128,2048]{1,0:T(8,128)(2,1)}, bf16[128,2048]{1,0:T(8,128)(2,1)}, u32[]{:S(2)}, u32[]{:S(2)}) %collective-permute-start.10) | collective-permute-done | bytes 524320 | tf_op jit(solution)/shard_map/ffn_gather/ppermute | solution.py:54
  152.1 10.8 %collective-permute-done.9 = bf16[128,2048]{1,0:T(8,128)(2,1)} collective-permute-done((bf16[128,2048]{1,0:T(8,128)(2,1)}, bf16[128,2048]{1,0:T(8,128)(2,1)}, u32[]{:S(2)}, u32[]{:S(2)}) %collective-permute-start.9) | collective-permute-done | bytes 524320 | tf_op jit(solution)/shard_map/ffn_gather/ppermute | solution.py:54
  162.9 3.1 select_select_fusion.3
  169.3 2.2 collective-permute-start.11
  171.5 2.0 multiply_convert_fusion
  175.4 2.6 copy-done.43
  178.0 3.4 fusion.7
  181.4 3.4 multiply_convert_fusion.5
  186.0 3.4 fusion.3
  189.8 3.4 multiply_convert_fusion.3
  195.6 5.1 %fusion.5 = f32[512,2048]{1,0:T(8,128)} fusion(bf16[2048,2304]{1,0:T(8,128)(2,1)S(1)} %copy-done.43, bf16[512,768]{1,0:T(8,128)(2,1)S(1)} %copy-done.53, bf16[512,768]{1,0:T(8,128)(2,1)S(1)} %copy-done.52), kind=kOutput, calls=%fused_computation.9 | convolution fusion | flops 3224371200 | bytes 12058624 | tf_op jit(solution)/shard_map/dot_general | solution.py:31
  200.9 3.6 add_convert_fusion.1
  204.6 7.9 %add_convert_fusion.2 = bf16[512,2048]{1,0:T(8,128)(2,1)S(1)} fusion(f32[512,2048]{1,0:T(8,128)} %fusion.5, bf16[2048,2304]{1,0:T(8,128)(2,1)} %copy-done.44, bf16[512,768]{1,0:T(8,128)(2,1)} %get-tuple-element.53, bf16[512,768]{1,0:T(8,128)(2,1)} %get-tuple-element.52), kind=kOutput, calls=%fused_computation.15 | convolution fusion | flops 3226468352 | bytes 14155776 | tf_op jit(solution)/shard_map/dot_general | solution.py:31
  213.7 2.3 collective-permute-start.13
  216.4 11.3 %collective-permute-done.12 = bf16[128,2048]{1,0:T(8,128)(2,1)S(1)} collective-permute-done((bf16[128,2048]{1,0:T(8,128)(2,1)S(1)}, bf16[128,2048]{1,0:T(8,128)(2,1)S(1)}, u32[]{:S(2)}, u32[]{:S(2)}) %collective-permute-start.12) | collective-permute-done | bytes 524320 | tf_op jit(solution)/shard_map/d_ffn_scatter/ppermute | solution.py:54
  227.6 11.8 %collective-permute-done.13 = bf16[128,2048]{1,0:T(8,128)(2,1)S(1)} collective-permute-done((bf16[128,2048]{1,0:T(8,128)(2,1)S(1)}, bf16[128,2048]{1,0:T(8,128)(2,1)S(1)}, u32[]{:S(2)}, u32[]{:S(2)}) %collective-permute-start.13) | collective-permute-done | bytes 524320 | tf_op jit(solution)/shard_map/d_ffn_scatter/ppermute | solution.py:54
  242.0 5.7 %convolution_convert_fusion = bf16[2048,1536]{1,0:T(8,128)(2,1)} fusion(bf16[512,2048]{1,0:T(8,128)(2,1)S(1)} %constant_dynamic-update-slice_fusion.5, bf16[512,768]{1,0:T(8,128)(2,1)S(1)} %copy-done.51, bf16[512,768]{1,0:T(8,128)(2,1)S(1)} %copy-done.50), kind=kOutput, calls=%fused_computation.1 | convolution fusion | flops 3227516928 | bytes 9961472 | tf_op jit(solution)/shard_map/dot_general | solution.py:35
  253.2 3.3 collective-permute-start.26
  256.5 2.1 collective-permute-done.25
  258.6 10.0 %add_convert_fusion = bf16[2048,1536]{1,0:T(8,128)(2,1)} fusion(bf16[2048,1536]{1,0:T(8,128)(2,1)} %collective-permute-done.25, bf16[512,2048]{1,0:T(8,128)(2,1)} %copy-done.18, bf16[512,768]{1,0:T(8,128)(2,1)} %get-tuple-element.55, bf16[512,768]{1,0:T(8,128)(2,1)} %get-tuple-element.54), kind=kOutput, calls=%fused_computation | convolution fusion | flops 3233808384 | bytes 16252928 | tf_op jit(solution)/shard_map/dot_general | solution.py:35
  270.5 15.0 %all-gather.10.cloned.1.call-done = bf16[512,2048]{1,0:T(8,128)(2,1)} async-done(((bf16[128,2048]{1,0:T(8,128)(2,1)}), bf16[512,2048]{1,0:T(8,128)(2,1)}) %all-gather.10.cloned.1.call-update) | async-done | bytes 2097168 | tf_op jit(solution)/shard_map/d_attn_gather/all_gather | solution.py:79
  290.1 4.0 fusion.17
  294.1 3.7 add_convert_fusion.3
  300.4 3.1 collective-permute-start.18
  303.4 1.9 convolution_convert_fusion.4
  306.1 15.9 %shard_map.222 = (bf16[512,512]{1,0:T(8,128)(2,1)S(1)}, f32[2048,128]{1,0:T(8,128)S(1)}, f32[2048,128]{1,0:T(8,128)S(1)}) custom-call(bf16[512,512]{1,0:T(8,128)(2,1)S(1)} %pad_maximum_fusion.13.q_ref, bf16[512,512]{1,0:T(8,128)(2,1)S(1)} %pad_maximum_fusion.15.do_ref, f32[512,512]{1,0:T(8,128)} %copy-done.1, f32[4,8,512]{2,1,0:T(8,128)S(1)} %get-tuple-element.26.lse_ref, ...), custom_call_target="tpu_custom_call" | custom-call | flops 10737418240 | bytes 8388608 | tf_op jit(solution)/shard_map/pallas_call | solution.py:203
  322.3 3.5 collective-permute-done.17
  330.6 2.8 collective-permute-start.21
  333.4 12.7 %collective-permute-done.21 = bf16[512,256]{1,0:T(8,128)(2,1)S(1)} collective-permute-done((bf16[512,256]{1,0:T(8,128)(2,1)S(1)}, bf16[512,256]{1,0:T(8,128)(2,1)S(1)}, u32[]{:S(2)}, u32[]{:S(2)}) %collective-permute-start.21) | collective-permute-done | bytes 262176 | tf_op jit(solution)/shard_map/ppermute | solution.py:44
  349.0 4.1 multiply_reduce_fusion
  354.7 2.4 convolution_convert_fusion.2
  359.9 5.2 %reduce-scatter.8.cloned.1.call-done = bf16[256,1536]{1,0:T(8,128)(2,1)} async-done(((bf16[2048,1536]{1,0:T(8,128)(2,1)}), bf16[256,1536]{1,0:T(8,128)(2,1)}) %reduce-scatter.8.cloned.1.call-update) | async-done | bytes 786448 | tf_op jit(solution)/shard_map/gate_up_rows/reduce_scatter | solution.py:436
  365.0 2.6 collective-permute-start.27
  367.7 2.6 add_convert_fusion.6
  371.3 2.8 add_convert_fusion.5
  376.0 9.5 %collective-permute-done.27 = bf16[256,1536]{1,0:T(8,128)(2,1)S(1)} collective-permute-done((bf16[256,1536]{1,0:T(8,128)(2,1)}, bf16[256,1536]{1,0:T(8,128)(2,1)S(1)}, u32[]{:S(2)}, u32[]{:S(2)}) %collective-permute-start.27) | collective-permute-done | bytes 786464 | tf_op jit(solution)/shard_map/gate_up_y/ppermute | solution.py:44
  387.8 1.9 fusion.9
  389.7 6.6 %all-to-all-start.1 = ((bf16[16,128,768]{2,1,0:T(8,128)(2,1)}), bf16[16,128,768]{2,1,0:T(8,128)(2,1)S(1)}, u32[]{:S(2)}, u32[]{:S(2)}) async-start(bf16[16,128,768]{2,1,0:T(8,128)(2,1)} %bitcast.120), calls=%async_computation.3 | async-start | bytes 6291456 | tf_op jit(solution)/shard_map/attn_rows/all_to_all | solution.py:422
  396.4 2.0 collective-permute-start.19
  400.1 36.9 %all-to-all-done.1 = bf16[16,128,768]{2,1,0:T(8,128)(2,1)S(1)} async-done(((bf16[16,128,768]{2,1,0:T(8,128)(2,1)}), bf16[16,128,768]{2,1,0:T(8,128)(2,1)S(1)}, u32[]{:S(2)}, u32[]{:S(2)}) %all-to-all-start.1) | async-done | bytes 3145760 | tf_op jit(solution)/shard_map/attn_rows/all_to_all | solution.py:422
  440.5 5.8 %all-to-all-start.2 = ((bf16[8,128,768]{2,1,0:T(8,128)(2,1)}), bf16[8,128,768]{2,1,0:T(8,128)(2,1)S(1)}, u32[]{:S(2)}, u32[]{:S(2)}) async-start(bf16[8,128,768]{2,1,0:T(8,128)(2,1)} %broadcast_in_dim.11), calls=%async_computation.5 | async-start | bytes 3145728 | tf_op jit(solution)/shard_map/attn_columns/all_to_all | solution.py:428
  448.1 3.1 collective-permute-start.22
  453.6 9.5 %all-gather.12.cloned.1.call-done = bf16[1024,2304]{1,0:T(8,128)(2,1)} async-done(((bf16[256,2304]{1,0:T(8,128)(2,1)}), bf16[1024,2304]{1,0:T(8,128)(2,1)}) %all-gather.12.cloned.1.call-update) | async-done | bytes 4718608 | tf_op jit(solution)/shard_map/unit_columns/all_gather | solution.py:478
  463.2 2.3 copy-done
  465.5 3.8 shard_map.223
  (286 shorter events, 91.5 us)
Async XLA Ops:
  7.2 53.0 %all-gather.6.cloned.1.call-start = ((), (), s32[]{:S(2)}) async-start(), calls=%async_computation.6 | async-start | bytes 5242880 | tf_op jit(solution)/shard_map/token_gather/all_gather | solution.py:79
  13.0 3.5 collective-permute-start
  18.3 35.4 %all-to-all-start = ((bf16[8,256,640]{2,1,0:T(8,128)(2,1)}), bf16[8,256,640]{2,1,0:T(8,128)(2,1)S(1)}, u32[]{:S(2)}, u32[]{:S(2)}) async-start(bf16[8,256,640]{2,1,0:T(8,128)(2,1)} %broadcast_in_dim.8), calls=%async_computation | async-start | bytes 5242880 | tf_op jit(solution)/shard_map/all_to_all | solution.py:89
  23.3 144.7 %all-gather.8.cloned.1.call-start = ((), (), s32[]{:S(2)}) async-start(), calls=%async_computation.7 | async-start | bytes 10616832 | tf_op jit(solution)/shard_map/unit_gather/all_gather | solution.py:330
  26.3 29.3 %copy-start.41 = (s32[1,2048]{1,0:T(1,128)S(1)}, s32[1,2048]{1,0:T(1,128)}, u32[]{:S(2)}) copy-start(s32[1,2048]{1,0:T(1,128)} %param.16) | copy-start | bytes 24580
  26.3 29.3 %copy-start.42 = (s32[1,2048]{1,0:T(1,128)S(1)}, s32[1,2048]{1,0:T(1,128)}, u32[]{:S(2)}) copy-start(s32[1,2048]{1,0:T(1,128)} %param.17) | copy-start | bytes 24580
  53.7 10.8 %copy-start.5 = (bf16[8,256,640]{2,1,0:T(8,128)(2,1)}, bf16[8,256,640]{2,1,0:T(8,128)(2,1)S(1)}, u32[]{:S(2)}) copy-start(bf16[8,256,640]{2,1,0:T(8,128)(2,1)S(1)} %all-to-all-done) | copy-start | bytes 7864324
  55.5 194.5 %reduce-scatter.4.cloned.1.call-start = ((), (), s32[]{:S(2)}) async-start(), calls=%async_computation.8 | async-start | bytes 3538944 | tf_op jit(solution)/shard_map/down_rows/reduce_scatter | solution.py:436
  56.7 30.5 %copy-start.9 = (f32[512,64]{1,0:T(8,128)}, f32[512,64]{1,0:T(8,128)S(1)}, u32[]{:S(2)}) copy-start(f32[512,64]{1,0:T(8,128)S(1)} %get-tuple-element.124) | copy-start | bytes 393220
  56.7 30.5 %copy-start.11 = (f32[512,64]{1,0:T(8,128)}, f32[512,64]{1,0:T(8,128)S(1)}, u32[]{:S(2)}) copy-start(f32[512,64]{1,0:T(8,128)S(1)} %get-tuple-element.123) | copy-start | bytes 393220
  56.7 5.6 %copy-start.39 = (f32[2048]{0:T(1024)S(1)}, f32[2048]{0:T(1024)}, u32[]{:S(2)}) copy-start(f32[2048]{0:T(1024)} %param.19) | copy-start | bytes 24580
  58.0 7.9 %collective-permute-start.1 = (bf16[2048,384]{1,0:T(8,128)(2,1)}, bf16[2048,384]{1,0:T(8,128)(2,1)}, u32[]{:S(2)}, u32[]{:S(2)}) collective-permute-start(bf16[2048,384]{1,0:T(8,128)(2,1)} %slice.342), channel_id=1, source_target_pairs={{0,1},{1,0},{2,3},{3,2},{4,5},{5,4},{6,7},{7,6},{8,9},{9,8},{10,11... | collective-permute-start | bytes 4718600 | tf_op jit(solution)/shard_map/swap/ppermute | solution.py:40
  70.2 15.2 %collective-permute-start.2 = (bf16[512,256]{1,0:T(8,128)(2,1)S(1)}, bf16[512,256]{1,0:T(8,128)(2,1)S(1)}, u32[]{:S(2)}, u32[]{:S(2)}) collective-permute-start(bf16[512,256]{1,0:T(8,128)(2,1)S(1)} %pad_maximum_fusion.23), channel_id=1, source_target_pairs={{0,8},{8,0},{1,9},{9,1},{2,10},{10,2},{3,11},{11,3},{4,12},{12,4},... | collective-permute-start | bytes 786440 | tf_op jit(solution)/shard_map/ppermute | solution.py:44
  75.5 26.1 %collective-permute-start.4 = (bf16[2048,256]{1,0:T(8,128)(2,1)}, bf16[2048,256]{1,0:T(8,128)(2,1)}, u32[]{:S(2)}, u32[]{:S(2)}) collective-permute-start(bf16[2048,256]{1,0:T(8,128)(2,1)} %slice.363), channel_id=1, source_target_pairs={{0,1},{1,0},{2,3},{3,2},{4,5},{5,4},{6,7},{7,6},{8,9},{9,8},{10,11... | collective-permute-start | bytes 3145736 | tf_op jit(solution)/shard_map/swap/ppermute | solution.py:40
  85.5 3.0 collective-permute-start.3
  106.2 30.2 %copy-start.38 = (f32[2048]{0:T(1024)S(1)}, f32[2048]{0:T(1024)}, u32[]{:S(2)}) copy-start(f32[2048]{0:T(1024)} %param.20) | copy-start | bytes 24580
  106.2 15.0 %collective-permute-start.5 = (bf16[128,2048]{1,0:T(8,128)(2,1)}, bf16[128,2048]{1,0:T(8,128)(2,1)}, u32[]{:S(2)}, u32[]{:S(2)}) collective-permute-start(bf16[128,2048]{1,0:T(8,128)(2,1)} %get-tuple-element.72), channel_id=1, source_target_pairs={{0,4},{2,6},{4,0},{6,2},{1,5},{3,7},{5,1},{7,3},{8,12},{10,14},{12... | collective-permute-start | bytes 1572872 | tf_op jit(solution)/shard_map/attn_scatter/ppermute | solution.py:54
  107.8 25.3 %collective-permute-start.6 = (bf16[128,2048]{1,0:T(8,128)(2,1)}, bf16[128,2048]{1,0:T(8,128)(2,1)}, u32[]{:S(2)}, u32[]{:S(2)}) collective-permute-start(bf16[128,2048]{1,0:T(8,128)(2,1)} %get-tuple-element.74), channel_id=1, source_target_pairs={{0,2},{2,4},{4,6},{6,0},{1,3},{3,5},{5,7},{7,1},{8,10},{10,12},{12... | collective-permute-start | bytes 1572872 | tf_op jit(solution)/shard_map/attn_scatter/ppermute | solution.py:54
  108.0 25.1 %collective-permute-start.7 = (bf16[128,2048]{1,0:T(8,128)(2,1)}, bf16[128,2048]{1,0:T(8,128)(2,1)}, u32[]{:S(2)}, u32[]{:S(2)}) collective-permute-start(bf16[128,2048]{1,0:T(8,128)(2,1)} %get-tuple-element.73), channel_id=1, source_target_pairs={{0,6},{2,0},{4,2},{6,4},{1,7},{3,1},{5,3},{7,5},{8,14},{10,8},{12,... | collective-permute-start | bytes 1572872 | tf_op jit(solution)/shard_map/attn_scatter/ppermute | solution.py:54
  137.3 14.7 %collective-permute-start.10 = (bf16[128,2048]{1,0:T(8,128)(2,1)}, bf16[128,2048]{1,0:T(8,128)(2,1)}, u32[]{:S(2)}, u32[]{:S(2)}) collective-permute-start(bf16[128,2048]{1,0:T(8,128)(2,1)} %multiply_convert_fusion.9), channel_id=1, source_target_pairs={{0,2},{2,4},{4,6},{6,0},{1,3},{3,5},{5,7},{7,1},{8,10},{10,12},{12... | collective-permute-start | bytes 1572872 | tf_op jit(solution)/shard_map/ffn_gather/ppermute | solution.py:54
  137.5 14.6 %collective-permute-start.8 = (bf16[128,2048]{1,0:T(8,128)(2,1)}, bf16[128,2048]{1,0:T(8,128)(2,1)}, u32[]{:S(2)}, u32[]{:S(2)}) collective-permute-start(bf16[128,2048]{1,0:T(8,128)(2,1)} %multiply_convert_fusion.9), channel_id=1, source_target_pairs={{0,6},{2,0},{4,2},{6,4},{1,7},{3,1},{5,3},{7,5},{8,14},{10,8},{12,... | collective-permute-start | bytes 1572872 | tf_op jit(solution)/shard_map/ffn_gather/ppermute | solution.py:54
  140.0 22.9 %collective-permute-start.9 = (bf16[128,2048]{1,0:T(8,128)(2,1)}, bf16[128,2048]{1,0:T(8,128)(2,1)}, u32[]{:S(2)}, u32[]{:S(2)}) collective-permute-start(bf16[128,2048]{1,0:T(8,128)(2,1)} %multiply_convert_fusion.9), channel_id=1, source_target_pairs={{0,4},{2,6},{4,0},{6,2},{1,5},{3,7},{5,1},{7,3},{8,12},{10,14},{12... | collective-permute-start | bytes 1572872 | tf_op jit(solution)/shard_map/ffn_gather/ppermute | solution.py:54
  169.3 16.7 %collective-permute-start.11 = (bf16[2048,2304]{1,0:T(8,128)(2,1)}, bf16[2048,2304]{1,0:T(8,128)(2,1)S(1)}, u32[]{:S(2)}, u32[]{:S(2)}) collective-permute-start(bf16[2048,2304]{1,0:T(8,128)(2,1)} %constant_dynamic-update-slice_fusion.10), channel_id=1, source_target_pairs={{0,1},{1,0},{2,3},{3,2},{4,5},{5,4},{6,7},{7,6},{8,9},{9,8},{10,11... | collective-permute-start | bytes 28311560 | tf_op jit(solution)/shard_map/swap/ppermute | solution.py:40
  184.8 16.1 %copy-start.47 = (bf16[512,768]{1,0:T(8,128)(2,1)}, bf16[512,768]{1,0:T(8,128)(2,1)S(1)}, u32[]{:S(2)}) copy-start(bf16[512,768]{1,0:T(8,128)(2,1)S(1)} %get-tuple-element.59) | copy-start | bytes 2359300
  195.0 5.9 %collective-permute-start.15 = (bf16[2048,768]{1,0:T(8,128)(2,1)S(1)}, bf16[2048,768]{1,0:T(8,128)(2,1)S(1)}, u32[]{:S(2)}, u32[]{:S(2)}) collective-permute-start(bf16[2048,768]{1,0:T(8,128)(2,1)S(1)} %convolution_convert_fusion.1), channel_id=1, source_target_pairs={{0,1},{1,0},{2,3},{3,2},{4,5},{5,4},{6,7},{7,6},{8,9},{9,8},{10,11... | collective-permute-start | bytes 9437192 | tf_op jit(solution)/shard_map/swap/ppermute | solution.py:40
  204.6 80.9 %all-gather.10.cloned.1.call-start = ((), (), s32[]{:S(2)}) async-start(), calls=%async_computation.9 | async-start | bytes 2621440 | tf_op jit(solution)/shard_map/d_attn_gather/all_gather | solution.py:79
  212.6 26.9 %copy-start.3 = (f32[128,2048]{1,0:T(8,128)S(1)}, f32[128,2048]{1,0:T(8,128)}, u32[]{:S(2)}) copy-start(f32[128,2048]{1,0:T(8,128)} %copy-done.2) | copy-start | bytes 3145732
  212.7 14.9 %collective-permute-start.12 = (bf16[128,2048]{1,0:T(8,128)(2,1)S(1)}, bf16[128,2048]{1,0:T(8,128)(2,1)S(1)}, u32[]{:S(2)}, u32[]{:S(2)}) collective-permute-start(bf16[128,2048]{1,0:T(8,128)(2,1)S(1)} %get-tuple-element.65), channel_id=1, source_target_pairs={{0,4},{2,6},{4,0},{6,2},{1,5},{3,7},{5,1},{7,3},{8,12},{10,14},{12... | collective-permute-start | bytes 1572872 | tf_op jit(solution)/shard_map/d_ffn_scatter/ppermute | solution.py:54
  213.7 25.8 %collective-permute-start.13 = (bf16[128,2048]{1,0:T(8,128)(2,1)S(1)}, bf16[128,2048]{1,0:T(8,128)(2,1)S(1)}, u32[]{:S(2)}, u32[]{:S(2)}) collective-permute-start(bf16[128,2048]{1,0:T(8,128)(2,1)S(1)} %get-tuple-element.67), channel_id=1, source_target_pairs={{0,2},{2,4},{4,6},{6,0},{1,3},{3,5},{5,7},{7,1},{8,10},{10,12},{12... | collective-permute-start | bytes 1572872 | tf_op jit(solution)/shard_map/d_ffn_scatter/ppermute | solution.py:54
  216.0 25.2 %copy-start.17 = (bf16[512,2048]{1,0:T(8,128)(2,1)S(1)}, bf16[512,2048]{1,0:T(8,128)(2,1)}, u32[]{:S(2)}) copy-start(bf16[512,2048]{1,0:T(8,128)(2,1)} %copy.128) | copy-start | bytes 6291460
  216.0 26.0 %copy-start.50 = (bf16[512,768]{1,0:T(8,128)(2,1)S(1)}, bf16[512,768]{1,0:T(8,128)(2,1)}, u32[]{:S(2)}) copy-start(bf16[512,768]{1,0:T(8,128)(2,1)} %get-tuple-element.52) | copy-start | bytes 2359300
  216.0 26.0 %copy-start.51 = (bf16[512,768]{1,0:T(8,128)(2,1)S(1)}, bf16[512,768]{1,0:T(8,128)(2,1)}, u32[]{:S(2)}) copy-start(bf16[512,768]{1,0:T(8,128)(2,1)} %get-tuple-element.53) | copy-start | bytes 2359300
  216.0 23.4 %collective-permute-start.14 = (bf16[128,2048]{1,0:T(8,128)(2,1)S(1)}, bf16[128,2048]{1,0:T(8,128)(2,1)S(1)}, u32[]{:S(2)}, u32[]{:S(2)}) collective-permute-start(bf16[128,2048]{1,0:T(8,128)(2,1)S(1)} %get-tuple-element.66), channel_id=1, source_target_pairs={{0,6},{2,0},{4,2},{6,4},{1,7},{3,1},{5,3},{7,5},{8,14},{10,8},{12,... | collective-permute-start | bytes 1572872 | tf_op jit(solution)/shard_map/d_ffn_scatter/ppermute | solution.py:54
  242.0 5.7 %copy-start.18 = (bf16[512,2048]{1,0:T(8,128)(2,1)}, bf16[512,2048]{1,0:T(8,128)(2,1)S(1)}, u32[]{:S(2)}) copy-start(bf16[512,2048]{1,0:T(8,128)(2,1)S(1)} %constant_dynamic-update-slice_fusion.5) | copy-start | bytes 6291460
  242.0 6.4 %copy-start.31 = (bf16[1,256,2048]{2,1,0:T(8,128)(2,1)S(1)}, bf16[1,256,2048]{2,1,0:T(8,128)(2,1)}, u32[]{:S(2)}) copy-start(bf16[1,256,2048]{2,1,0:T(8,128)(2,1)} %param.15) | copy-start | bytes 3145732
  247.7 10.8 %collective-permute-start.25 = (bf16[2048,1536]{1,0:T(8,128)(2,1)}, bf16[2048,1536]{1,0:T(8,128)(2,1)}, u32[]{:S(2)}, u32[]{:S(2)}) collective-permute-start(bf16[2048,1536]{1,0:T(8,128)(2,1)} %convolution_convert_fusion), channel_id=1, source_target_pairs={{0,1},{1,0},{2,3},{3,2},{4,5},{5,4},{6,7},{7,6},{8,9},{9,8},{10,11... | collective-permute-start | bytes 18874376 | tf_op jit(solution)/shard_map/swap/ppermute | solution.py:40
  253.1 111.9 %reduce-scatter.8.cloned.1.call-start = ((), (), s32[]{:S(2)}) async-start(), calls=%async_computation.11 | async-start | bytes 7077888 | tf_op jit(solution)/shard_map/gate_up_rows/reduce_scatter | solution.py:436
  253.2 15.3 %copy-start.37 = (bf16[256,768]{1,0:T(8,128)(2,1)S(1)}, bf16[256,768]{1,0:T(8,128)(2,1)}, u32[]{:S(2)}) copy-start(bf16[256,768]{1,0:T(8,128)(2,1)} %reduce-scatter.4.cloned.1.call-done) | copy-start | bytes 1179652
  253.2 15.3 %collective-permute-start.26 = (bf16[256,768]{1,0:T(8,128)(2,1)}, bf16[256,768]{1,0:T(8,128)(2,1)S(1)}, u32[]{:S(2)}, u32[]{:S(2)}) collective-permute-start(bf16[256,768]{1,0:T(8,128)(2,1)} %reduce-scatter.4.cloned.1.call-done), channel_id=1, source_target_pairs={{0,8},{8,0},{1,9},{9,1},{2,10},{10,2},{3,11},{11,3},{4,12},{12,4},... | collective-permute-start | bytes 1179656 | tf_op jit(solution)/shard_map/down_y/ppermute | solution.py:44
  288.7 109.8 %reduce-scatter.6.cloned.1.call-start = ((), (), s32[]{:S(2)}) async-start(), calls=%async_computation.10 | async-start | bytes 2621440 | tf_op jit(solution)/shard_map/d_attn_scatter/reduce_scatter | solution.py:84
  298.9 6.5 %copy-start.6 = (bf16[8,256,640]{2,1,0:T(8,128)(2,1)S(1)}, bf16[8,256,640]{2,1,0:T(8,128)(2,1)}, u32[]{:S(2)}) copy-start(bf16[8,256,640]{2,1,0:T(8,128)(2,1)} %copy-done.5) | copy-start | bytes 7864324
  298.9 23.3 %collective-permute-start.16 = (bf16[128,2048]{1,0:T(8,128)(2,1)}, bf16[128,2048]{1,0:T(8,128)(2,1)S(1)}, u32[]{:S(2)}, u32[]{:S(2)}) collective-permute-start(bf16[128,2048]{1,0:T(8,128)(2,1)} %get-tuple-element.62), channel_id=1, source_target_pairs={{0,4},{2,6},{4,0},{6,2},{1,5},{3,7},{5,1},{7,3},{8,12},{10,14},{12... | collective-permute-start | bytes 1572872 | tf_op jit(solution)/shard_map/branch_scatter/ppermute | solution.py:54
  300.4 25.4 %collective-permute-start.17 = (bf16[128,2048]{1,0:T(8,128)(2,1)S(1)}, bf16[128,2048]{1,0:T(8,128)(2,1)S(1)}, u32[]{:S(2)}, u32[]{:S(2)}) collective-permute-start(bf16[128,2048]{1,0:T(8,128)(2,1)S(1)} %get-tuple-element.64), channel_id=1, source_target_pairs={{0,2},{2,4},{4,6},{6,0},{1,3},{3,5},{5,7},{7,1},{8,10},{10,12},{12... | collective-permute-start | bytes 1572872 | tf_op jit(solution)/shard_map/branch_scatter/ppermute | solution.py:54
  300.4 25.4 %collective-permute-start.18 = (bf16[128,2048]{1,0:T(8,128)(2,1)S(1)}, bf16[128,2048]{1,0:T(8,128)(2,1)S(1)}, u32[]{:S(2)}, u32[]{:S(2)}) collective-permute-start(bf16[128,2048]{1,0:T(8,128)(2,1)S(1)} %get-tuple-element.63), channel_id=1, source_target_pairs={{0,6},{2,0},{4,2},{6,4},{1,7},{3,1},{5,3},{7,5},{8,14},{10,8},{12,... | collective-permute-start | bytes 1572872 | tf_op jit(solution)/shard_map/branch_scatter/ppermute | solution.py:54
  328.4 2.0 collective-permute-start.20
  330.5 15.7 %copy-start.10 = (f32[512,64]{1,0:T(8,128)S(1)}, f32[512,64]{1,0:T(8,128)}, u32[]{:S(2)}) copy-start(f32[512,64]{1,0:T(8,128)} %copy-done.9) | copy-start | bytes 393220
  330.6 15.6 %collective-permute-start.21 = (bf16[512,256]{1,0:T(8,128)(2,1)S(1)}, bf16[512,256]{1,0:T(8,128)(2,1)S(1)}, u32[]{:S(2)}, u32[]{:S(2)}) collective-permute-start(bf16[512,256]{1,0:T(8,128)(2,1)S(1)} %slice.536), channel_id=1, source_target_pairs={{0,8},{8,0},{1,9},{9,1},{2,10},{10,2},{3,11},{11,3},{4,12},{12,4},... | collective-permute-start | bytes 786440 | tf_op jit(solution)/shard_map/ppermute | solution.py:44
  333.4 13.1 %copy-start.12 = (f32[512,64]{1,0:T(8,128)S(1)}, f32[512,64]{1,0:T(8,128)}, u32[]{:S(2)}) copy-start(f32[512,64]{1,0:T(8,128)} %copy-done.11) | copy-start | bytes 393220
  353.1 110.0 %all-gather.12.cloned.1.call-start = ((), (), s32[]{:S(2)}) async-start(), calls=%async_computation.12 | async-start | bytes 5898240 | tf_op jit(solution)/shard_map/unit_columns/all_gather | solution.py:478
  357.1 14.2 %collective-permute-start.23 = (bf16[2048,384]{1,0:T(8,128)(2,1)}, bf16[2048,384]{1,0:T(8,128)(2,1)}, u32[]{:S(2)}, u32[]{:S(2)}) collective-permute-start(bf16[2048,384]{1,0:T(8,128)(2,1)} %convolution_convert_fusion.2), channel_id=1, source_target_pairs={{0,1},{1,0},{2,3},{3,2},{4,5},{5,4},{6,7},{7,6},{8,9},{9,8},{10,11... | collective-permute-start | bytes 4718600 | tf_op jit(solution)/shard_map/swap/ppermute | solution.py:40
  359.8 7.8 %collective-permute-start.24 = (bf16[2048,256]{1,0:T(8,128)(2,1)}, bf16[2048,256]{1,0:T(8,128)(2,1)}, u32[]{:S(2)}, u32[]{:S(2)}) collective-permute-start(bf16[2048,256]{1,0:T(8,128)(2,1)} %convolution_convert_fusion.3), channel_id=1, source_target_pairs={{0,1},{1,0},{2,3},{3,2},{4,5},{5,4},{6,7},{7,6},{8,9},{9,8},{10,11... | collective-permute-start | bytes 3145736 | tf_op jit(solution)/shard_map/swap/ppermute | solution.py:40
  365.0 20.4 %collective-permute-start.27 = (bf16[256,1536]{1,0:T(8,128)(2,1)}, bf16[256,1536]{1,0:T(8,128)(2,1)S(1)}, u32[]{:S(2)}, u32[]{:S(2)}) collective-permute-start(bf16[256,1536]{1,0:T(8,128)(2,1)} %reduce-scatter.8.cloned.1.call-done), channel_id=1, source_target_pairs={{0,8},{8,0},{1,9},{9,1},{2,10},{10,2},{3,11},{11,3},{4,12},{12,4},... | collective-permute-start | bytes 2359304 | tf_op jit(solution)/shard_map/gate_up_y/ppermute | solution.py:44
  371.3 14.2 %copy-start.34 = (bf16[256,1536]{1,0:T(8,128)(2,1)S(1)}, bf16[256,1536]{1,0:T(8,128)(2,1)}, u32[]{:S(2)}) copy-start(bf16[256,1536]{1,0:T(8,128)(2,1)} %reduce-scatter.8.cloned.1.call-done) | copy-start | bytes 2359300
  374.1 11.3 %copy-start.27 = (bf16[2048,384]{1,0:T(8,128)(2,1)}, bf16[2048,384]{1,0:T(8,128)(2,1)S(1)}, u32[]{:S(2)}) copy-start(bf16[2048,384]{1,0:T(8,128)(2,1)S(1)} %add_convert_fusion.5) | copy-start | bytes 4718596
  374.1 11.6 %copy-start.26 = (bf16[256,768]{1,0:T(8,128)(2,1)S(1)}, bf16[256,768]{1,0:T(8,128)(2,1)}, u32[]{:S(2)}) copy-start(bf16[256,768]{1,0:T(8,128)(2,1)} %copy-done.25) | copy-start | bytes 1179652
  389.7 8.8 %copy-start.40 = (f32[2048]{0:T(1024)S(1)}, f32[2048]{0:T(1024)}, u32[]{:S(2)}) copy-start(f32[2048]{0:T(1024)} %param.19) | copy-start | bytes 24580
  389.7 47.2 %all-to-all-start.1 = ((bf16[16,128,768]{2,1,0:T(8,128)(2,1)}), bf16[16,128,768]{2,1,0:T(8,128)(2,1)S(1)}, u32[]{:S(2)}, u32[]{:S(2)}) async-start(bf16[16,128,768]{2,1,0:T(8,128)(2,1)} %bitcast.120), calls=%async_computation.3 | async-start | bytes 6291456 | tf_op jit(solution)/shard_map/attn_rows/all_to_all | solution.py:422
  396.4 54.9 %collective-permute-start.19 = (bf16[128,2048]{1,0:T(8,128)(2,1)}, bf16[128,2048]{1,0:T(8,128)(2,1)}, u32[]{:S(2)}, u32[]{:S(2)}) collective-permute-start(bf16[128,2048]{1,0:T(8,128)(2,1)} %get-tuple-element.43), channel_id=1, source_target_pairs={{0,1},{1,0},{2,3},{3,2},{4,5},{5,4},{6,7},{7,6},{8,9},{9,8},{10,11... | collective-permute-start | bytes 1572872 | tf_op jit(solution)/shard_map/swap/ppermute | solution.py:40
  439.2 7.1 %copy-start.13 = (bf16[1,256,2048]{2,1,0:T(8,128)(2,1)S(1)}, bf16[1,256,2048]{2,1,0:T(8,128)(2,1)}, u32[]{:S(2)}) copy-start(bf16[1,256,2048]{2,1,0:T(8,128)(2,1)} %param.14) | copy-start | bytes 3145732
  439.3 7.1 %copy-start.21 = (bf16[128,2048]{1,0:T(8,128)(2,1)S(1)}, bf16[128,2048]{1,0:T(8,128)(2,1)}, u32[]{:S(2)}) copy-start(bf16[128,2048]{1,0:T(8,128)(2,1)} %reduce-scatter.6.cloned.1.call-done) | copy-start | bytes 1572868
  440.5 31.1 %all-to-all-start.2 = ((bf16[8,128,768]{2,1,0:T(8,128)(2,1)}), bf16[8,128,768]{2,1,0:T(8,128)(2,1)S(1)}, u32[]{:S(2)}, u32[]{:S(2)}) async-start(bf16[8,128,768]{2,1,0:T(8,128)(2,1)} %broadcast_in_dim.11), calls=%async_computation.5 | async-start | bytes 3145728 | tf_op jit(solution)/shard_map/attn_columns/all_to_all | solution.py:428
  448.1 5.4 %collective-permute-start.22 = (bf16[128,2048]{1,0:T(8,128)(2,1)S(1)}, bf16[128,2048]{1,0:T(8,128)(2,1)S(1)}, u32[]{:S(2)}, u32[]{:S(2)}) collective-permute-start(bf16[128,2048]{1,0:T(8,128)(2,1)S(1)} %fusion.25), channel_id=1, source_target_pairs={{0,1},{1,0},{2,3},{3,2},{4,5},{5,4},{6,7},{7,6},{8,9},{9,8},{10,11... | collective-permute-start | bytes 1572872 | tf_op jit(solution)/shard_map/swap/ppermute | solution.py:40
  471.9 3.6 collective-permute-start.29
  473.3 1.7 collective-permute-start.28
  (30 other events, 79.6 us)
Sparse Core Ops, SparseCore 0:
  10.6 49.5 all-gather.5
  61.8 105.2 all-gather.7
  204.7 41.6 reduce-scatter.3
  253.3 32.2 all-gather.9
  288.8 76.1 reduce-scatter.7
  367.8 30.6 reduce-scatter.5
  400.9 62.2 all-gather.11

commit v5 on v4

--- a/solution.py
+++ b/solution.py
@@ -419,7 +419,7 @@
 
     def reduce_rows(value, name):
         with jax.named_scope(name + "_rows"):
-            parts = lax.all_to_all(value.reshape(16, width // 16, -1), ("yl", "z", "yh"), 0, 0)
+            parts = lax.all_to_all(value.reshape(16, value.shape[0] // 16, -1), ("yl", "z", "yh"), 0, 0)
         return half(jnp.sum(parts.astype(F32), axis=0))
 
     def columns(value, name):
@@ -466,21 +466,24 @@
     input_part = norm_backward(xval, root_attn, gain_attn, d_normed_attn)
     input_grad = both_cores(half(d_middle + input_part))
     gain_attn_local = jnp.sum(d_normed_part * x_unit, axis=0)
-    gains = half(jnp.stack([gain_attn_local, gain_ffn_local])).T
+    gains = jnp.stack([half(gain_attn_local).reshape(16, -1), half(gain_ffn_local).reshape(16, -1)], axis=1)
+    gains = gains.reshape(16, 1, width // 8)
     sum_qkv = sum_cores(mm_tn(normed_attn, d_own), mm_tn(normed_attn, d_other))
     sum_out = sum_cores(mm_tn(d_attn, heads[:, :256]), mm_tn(d_attn, heads[:, 256:]))
     sums = jnp.concatenate([sum_qkv, sum_out], axis=1)
-    sums = jnp.concatenate([sums, jnp.pad(gains, ((0, 0), (0, HD - 2)))], axis=1)
+    lines = jnp.pad(gains, ((0, 0), (0, 15), (0, sums.shape[1] - width // 8)))
+    sums = jnp.concatenate([sums.reshape(16, width // 16, -1), lines], axis=1).reshape(-1, sums.shape[1])
     total_rows = after(reduce_rows(sums, "attn"), rows_gu)
     packs = columns(total_rows, "attn")
     unit_rows = jnp.concatenate([halves(rows_gu, "gate_up", sum_qkv, sum_out), unit_down], axis=1)
     with jax.named_scope("unit_columns"):
         parts = lax.all_gather(unit_rows, "x", axis=0, tiled=False)
     grad_gate, grad_up, grad_down = spread(parts, tiles, spare)
-    packs = after(packs.reshape(width // 2, -1), grad_gate).reshape(packs.shape)
-    gains = jnp.sum(packs[..., 640:642].astype(F32), axis=1).reshape(-1, 2)
-    gains = (gains + swap_cores(gains)).T
-    packs = packs[..., :640]
+    packs = after(packs.reshape(-1, packs.shape[-1]), grad_gate).reshape(packs.shape)
+    owned = width // 16
+    gains = jnp.sum(packs[:, :, owned, : 2 * owned].astype(F32), axis=1)
+    gains = (gains + swap_cores(gains)).reshape(2, 2, owned).transpose(1, 0, 2).reshape(2, -1)
+    packs = packs[:, :, :owned]
     mine = lax.dynamic_slice_in_dim(packs, 2 * core, 2, axis=1)
     theirs = swap_cores(lax.dynamic_slice_in_dim(packs, 2 - 2 * core, 2, axis=1))
     grad_query, grad_key, grad_value, grad_out = place_heads(core, mine, theirs)

time: 494 us -> 495 us (level)
    unnamed x115 -> x121, local copies, waits for them, and re-layouts: 21.3 us -> 21.6 us
  transfers between devices with their start and end apart: 40 -> 40, of which waited for: 24 -> 23; matrix products, arithmetic and copies ran while one was open for 28% -> 29% of each run, Pallas kernels for 6% -> 6%
where the time goes in v5:
time: 495 us; the launch traced here: 487 us
  waiting for transfers between devices  198 us (40%)
  matrix products  82.7 us (17%)
  starting transfers between devices  60 us (12%)
  local copies, waits for them, and re-layouts  50.6 us (10%)
  other arithmetic  40.2 us (8%)
  Pallas kernels  31.5 us (6%)
  between operations  24.3 us (5%)
    ppermute x12, waiting for transfers between devices, shift_x(): return lax.ppermute(value, 'x', [(i, (i + hop) % 4) for i in range(4)])  71.4 us
    all_to_all x1, waiting for transfers between devices, reduce_rows(): lax.all_to_all(value.reshape(16, value.shape[0] // 16, -1), ('yl', 'z', '...  32.3 us
    dot_general x8, matrix products, mm_tn(): lax.dot_general(left, right, (((0,), (0,)), ((), ())), preferred_element_...  32 us
    ppermute x4, waiting for transfers between devices, across_y(): return lax.ppermute(value, 'yh', SWAP)  31.1 us
    dot_general x8, matrix products, mm_nt(): lax.dot_general(left, right, (((1,), (1,)), ((), ())), preferred_element_...  30.4 us
    unnamed x121, local copies, waits for them, and re-layouts  21.6 us
    dot_general x8, matrix products, mm(): return jnp.dot(left, right, preferred_element_type=F32)  20.2 us
    all_to_all x1, waiting for transfers between devices, gather_shard(): return lax.all_to_all(spread, SHARD, 0, 0).reshape(-1, value.shape[1])  19.6 us
  transfers between devices with their start and end apart: 40, of which 23 were waited for; matrix products, arithmetic and copies ran while one was open for 29% of the time, Pallas kernels for 6%

profile of v5, /device:TPU:97, one launch (start us, length us, event | category | flops | bytes accessed | tf_op | source)
XLA Modules:
  0.0 487.0 jit_solution(5522640455587711682)
XLA Ops:
  14.3 2.2 collective-permute-done
  18.3 5.0 %all-to-all-start = ((bf16[8,256,640]{2,1,0:T(8,128)(2,1)}), bf16[8,256,640]{2,1,0:T(8,128)(2,1)S(1)}, u32[]{:S(2)}, u32[]{:S(2)}) async-start(bf16[8,256,640]{2,1,0:T(8,128)(2,1)} %broadcast_in_dim.8), calls=%async_computation | async-start | bytes 5242880 | tf_op jit(solution)/shard_map/all_to_all | solution.py:89
  34.1 19.6 %all-to-all-done = bf16[8,256,640]{2,1,0:T(8,128)(2,1)S(1)} async-done(((bf16[8,256,640]{2,1,0:T(8,128)(2,1)}), bf16[8,256,640]{2,1,0:T(8,128)(2,1)S(1)}, u32[]{:S(2)}, u32[]{:S(2)}) %all-to-all-start) | async-done | bytes 2621472 | tf_op jit(solution)/shard_map/all_to_all | solution.py:89
  60.2 2.1 multiply_reduce_fusion.1
  62.3 2.1 multiply_convert_fusion.1
  66.0 2.7 fusion.79
  70.2 2.8 collective-permute-start.2
  73.3 2.3 slice.365
  76.5 9.0 %collective-permute-done.2 = bf16[512,256]{1,0:T(8,128)(2,1)S(1)} collective-permute-done((bf16[512,256]{1,0:T(8,128)(2,1)S(1)}, bf16[512,256]{1,0:T(8,128)(2,1)S(1)}, u32[]{:S(2)}, u32[]{:S(2)}) %collective-permute-start.2) | collective-permute-done | bytes 262176 | tf_op jit(solution)/shard_map/ppermute | solution.py:44
  89.2 10.1 %shard_map.221 = (f32[512,512]{1,0:T(8,128)S(1)}, bf16[512,512]{1,0:T(8,128)(2,1)S(1)}, f32[4,8,512]{2,1,0:T(8,128)S(1)}) custom-call(bf16[512,512]{1,0:T(8,128)(2,1)S(1)} %pad_maximum_fusion.14.q_ref, bf16[128,2048]{1,0:T(8,128)(2,1)S(1)} %copy.96.kt_ref, bf16[2048,128]{1,0:T(8,128)(2,1)S(1)} %get-tuple-element.87.v_ref, s32[512,2]{1,0:T(8,128)S(1)} %copy.97.rows_ref, ...), custom_call_target="tpu_custom_call" | custom-call | flops 4294967296 | bytes 4194304 | tf_op jit(solution)/shard_map/pallas_call | solution.py:136
  99.3 2.3 fusion.47
  101.6 2.0 add_convert_fusion.4
  108.0 2.5 collective-permute-start.7
  111.2 10.0 %collective-permute-done.5 = bf16[128,2048]{1,0:T(8,128)(2,1)} collective-permute-done((bf16[128,2048]{1,0:T(8,128)(2,1)}, bf16[128,2048]{1,0:T(8,128)(2,1)}, u32[]{:S(2)}, u32[]{:S(2)}) %collective-permute-start.5) | collective-permute-done | bytes 524320 | tf_op jit(solution)/shard_map/attn_scatter/ppermute | solution.py:54
  121.2 11.9 %collective-permute-done.6 = bf16[128,2048]{1,0:T(8,128)(2,1)} collective-permute-done((bf16[128,2048]{1,0:T(8,128)(2,1)}, bf16[128,2048]{1,0:T(8,128)(2,1)}, u32[]{:S(2)}, u32[]{:S(2)}) %collective-permute-start.6) | collective-permute-done | bytes 524320 | tf_op jit(solution)/shard_map/attn_scatter/ppermute | solution.py:54
  133.1 2.3 multiply_reduce_fusion.4
  137.5 2.5 collective-permute-start.8
  140.0 12.0 %collective-permute-done.10 = bf16[128,2048]{1,0:T(8,128)(2,1)} collective-permute-done((bf16[128,2048]{1,0:T(8,128)(2,1)}, bf16[128,2048]{1,0:T(8,128)(2,1)}, u32[]{:S(2)}, u32[]{:S(2)}) %collective-permute-start.10) | collective-permute-done | bytes 524320 | tf_op jit(solution)/shard_map/ffn_gather/ppermute | solution.py:54
  152.0 10.8 %collective-permute-done.9 = bf16[128,2048]{1,0:T(8,128)(2,1)} collective-permute-done((bf16[128,2048]{1,0:T(8,128)(2,1)}, bf16[128,2048]{1,0:T(8,128)(2,1)}, u32[]{:S(2)}, u32[]{:S(2)}) %collective-permute-start.9) | collective-permute-done | bytes 524320 | tf_op jit(solution)/shard_map/ffn_gather/ppermute | solution.py:54
  162.9 3.1 select_select_fusion.3
  169.3 2.2 collective-permute-start.11
  171.5 2.0 multiply_convert_fusion
  175.3 2.6 copy-done.46
  177.9 3.4 fusion.7
  181.4 3.4 multiply_convert_fusion.5
  186.0 3.4 fusion.3
  189.7 3.4 multiply_convert_fusion.3
  195.6 5.0 %fusion.5 = f32[512,2048]{1,0:T(8,128)} fusion(bf16[2048,2304]{1,0:T(8,128)(2,1)S(1)} %copy-done.46, bf16[512,768]{1,0:T(8,128)(2,1)S(1)} %copy-done.56, bf16[512,768]{1,0:T(8,128)(2,1)S(1)} %copy-done.55), kind=kOutput, calls=%fused_computation.9 | convolution fusion | flops 3224371200 | bytes 12058624 | tf_op jit(solution)/shard_map/dot_general | solution.py:31
  200.9 3.6 add_convert_fusion.1
  204.6 7.9 %add_convert_fusion.2 = bf16[512,2048]{1,0:T(8,128)(2,1)S(1)} fusion(f32[512,2048]{1,0:T(8,128)} %fusion.5, bf16[2048,2304]{1,0:T(8,128)(2,1)} %copy-done.47, bf16[512,768]{1,0:T(8,128)(2,1)} %get-tuple-element.53, bf16[512,768]{1,0:T(8,128)(2,1)} %get-tuple-element.52), kind=kOutput, calls=%fused_computation.15 | convolution fusion | flops 3226468352 | bytes 14155776 | tf_op jit(solution)/shard_map/dot_general | solution.py:31
  213.7 2.3 collective-permute-start.13
  216.4 11.2 %collective-permute-done.12 = bf16[128,2048]{1,0:T(8,128)(2,1)S(1)} collective-permute-done((bf16[128,2048]{1,0:T(8,128)(2,1)S(1)}, bf16[128,2048]{1,0:T(8,128)(2,1)S(1)}, u32[]{:S(2)}, u32[]{:S(2)}) %collective-permute-start.12) | collective-permute-done | bytes 524320 | tf_op jit(solution)/shard_map/d_ffn_scatter/ppermute | solution.py:54
  227.6 11.8 %collective-permute-done.13 = bf16[128,2048]{1,0:T(8,128)(2,1)S(1)} collective-permute-done((bf16[128,2048]{1,0:T(8,128)(2,1)S(1)}, bf16[128,2048]{1,0:T(8,128)(2,1)S(1)}, u32[]{:S(2)}, u32[]{:S(2)}) %collective-permute-start.13) | collective-permute-done | bytes 524320 | tf_op jit(solution)/shard_map/d_ffn_scatter/ppermute | solution.py:54
  242.0 5.7 %convolution_convert_fusion = bf16[2048,1536]{1,0:T(8,128)(2,1)} fusion(bf16[512,2048]{1,0:T(8,128)(2,1)S(1)} %constant_dynamic-update-slice_fusion.5, bf16[512,768]{1,0:T(8,128)(2,1)S(1)} %copy-done.54, bf16[512,768]{1,0:T(8,128)(2,1)S(1)} %copy-done.53), kind=kOutput, calls=%fused_computation.1 | convolution fusion | flops 3227516928 | bytes 9961472 | tf_op jit(solution)/shard_map/dot_general | solution.py:35
  253.2 3.3 collective-permute-start.26
  256.5 2.1 collective-permute-done.25
  258.5 10.0 %add_convert_fusion = bf16[2048,1536]{1,0:T(8,128)(2,1)} fusion(bf16[2048,1536]{1,0:T(8,128)(2,1)} %collective-permute-done.25, bf16[512,2048]{1,0:T(8,128)(2,1)} %copy-done.17, bf16[512,768]{1,0:T(8,128)(2,1)} %get-tuple-element.55, bf16[512,768]{1,0:T(8,128)(2,1)} %get-tuple-element.54), kind=kOutput, calls=%fused_computation | convolution fusion | flops 3233808384 | bytes 16252928 | tf_op jit(solution)/shard_map/dot_general | solution.py:35
  270.5 15.0 %all-gather.10.cloned.1.call-done = bf16[512,2048]{1,0:T(8,128)(2,1)} async-done(((bf16[128,2048]{1,0:T(8,128)(2,1)}), bf16[512,2048]{1,0:T(8,128)(2,1)}) %all-gather.10.cloned.1.call-update) | async-done | bytes 2097168 | tf_op jit(solution)/shard_map/d_attn_gather/all_gather | solution.py:79
  290.1 4.0 fusion.17
  294.1 3.7 add_convert_fusion.3
  300.4 3.1 collective-permute-start.18
  303.4 1.9 convolution_convert_fusion.4
  306.2 15.9 %shard_map.222 = (bf16[512,512]{1,0:T(8,128)(2,1)S(1)}, f32[2048,128]{1,0:T(8,128)S(1)}, f32[2048,128]{1,0:T(8,128)S(1)}) custom-call(bf16[512,512]{1,0:T(8,128)(2,1)S(1)} %pad_maximum_fusion.14.q_ref, bf16[512,512]{1,0:T(8,128)(2,1)S(1)} %pad_maximum_fusion.16.do_ref, f32[512,512]{1,0:T(8,128)} %copy-done.1, f32[4,8,512]{2,1,0:T(8,128)S(1)} %get-tuple-element.26.lse_ref, ...), custom_call_target="tpu_custom_call" | custom-call | flops 10737418240 | bytes 8388608 | tf_op jit(solution)/shard_map/pallas_call | solution.py:203
  322.3 3.5 collective-permute-done.17
  329.8 2.8 collective-permute-start.21
  332.6 12.7 %collective-permute-done.21 = bf16[512,256]{1,0:T(8,128)(2,1)S(1)} collective-permute-done((bf16[512,256]{1,0:T(8,128)(2,1)S(1)}, bf16[512,256]{1,0:T(8,128)(2,1)S(1)}, u32[]{:S(2)}, u32[]{:S(2)}) %collective-permute-start.21) | collective-permute-done | bytes 262176 | tf_op jit(solution)/shard_map/ppermute | solution.py:44
  348.2 4.1 multiply_reduce_fusion
  354.0 3.6 convolution_convert_fusion.2
  360.4 4.6 reduce-scatter.8.cloned.1.call-done
  365.0 2.4 collective-permute-start.27
  367.5 2.6 add_convert_fusion.6
  371.1 2.9 add_convert_fusion.5
  375.8 9.4 %collective-permute-done.27 = bf16[256,1536]{1,0:T(8,128)(2,1)S(1)} collective-permute-done((bf16[256,1536]{1,0:T(8,128)(2,1)}, bf16[256,1536]{1,0:T(8,128)(2,1)S(1)}, u32[]{:S(2)}, u32[]{:S(2)}) %collective-permute-start.27) | collective-permute-done | bytes 786464 | tf_op jit(solution)/shard_map/gate_up_y/ppermute | solution.py:44
  387.9 1.9 fusion.11
  389.8 6.5 %all-to-all-start.1 = ((bf16[16,144,640]{2,1,0:T(8,128)(2,1)}), bf16[16,144,640]{2,1,0:T(8,128)(2,1)S(1)}, u32[]{:S(2)}, u32[]{:S(2)}) async-start(bf16[16,144,640]{2,1,0:T(8,128)(2,1)} %fusion.11), calls=%async_computation.3 | async-start | bytes 5898240 | tf_op jit(solution)/shard_map/attn_rows/all_to_all | solution.py:422
  396.3 1.9 collective-permute-start.19
  399.9 2.1 broadcast_select_fusion.3
  402.0 32.3 %all-to-all-done.1 = bf16[16,144,640]{2,1,0:T(8,128)(2,1)S(1)} async-done(((bf16[16,144,640]{2,1,0:T(8,128)(2,1)}), bf16[16,144,640]{2,1,0:T(8,128)(2,1)S(1)}, u32[]{:S(2)}, u32[]{:S(2)}) %all-to-all-start.1) | async-done | bytes 2949152 | tf_op jit(solution)/shard_map/attn_rows/all_to_all | solution.py:422
  437.8 5.7 %all-to-all-start.2 = ((bf16[8,144,640]{2,1,0:T(8,128)(2,1)}), bf16[8,144,640]{2,1,0:T(8,128)(2,1)S(1)}, u32[]{:S(2)}, u32[]{:S(2)}) async-start(bf16[8,144,640]{2,1,0:T(8,128)(2,1)} %broadcast_in_dim.11), calls=%async_computation.5 | async-start | bytes 2949120 | tf_op jit(solution)/shard_map/attn_columns/all_to_all | solution.py:428
  445.0 2.7 fusion.25
  447.7 2.9 collective-permute-start.22
  451.7 14.0 %all-gather.12.cloned.1.call-done = bf16[1024,2304]{1,0:T(8,128)(2,1)} async-done(((bf16[256,2304]{1,0:T(8,128)(2,1)}), bf16[1024,2304]{1,0:T(8,128)(2,1)}) %all-gather.12.cloned.1.call-update) | async-done | bytes 4718608 | tf_op jit(solution)/shard_map/unit_columns/all_gather | solution.py:480
  465.6 2.3 copy-done
  468.0 3.8 shard_map.223
  (292 shorter events, 93.6 us)
Async XLA Ops:
  7.2 53.0 %all-gather.6.cloned.1.call-start = ((), (), s32[]{:S(2)}) async-start(), calls=%async_computation.6 | async-start | bytes 5242880 | tf_op jit(solution)/shard_map/token_gather/all_gather | solution.py:79
  13.0 3.5 collective-permute-start
  18.3 35.4 %all-to-all-start = ((bf16[8,256,640]{2,1,0:T(8,128)(2,1)}), bf16[8,256,640]{2,1,0:T(8,128)(2,1)S(1)}, u32[]{:S(2)}, u32[]{:S(2)}) async-start(bf16[8,256,640]{2,1,0:T(8,128)(2,1)} %broadcast_in_dim.8), calls=%async_computation | async-start | bytes 5242880 | tf_op jit(solution)/shard_map/all_to_all | solution.py:89
  23.3 144.7 %all-gather.8.cloned.1.call-start = ((), (), s32[]{:S(2)}) async-start(), calls=%async_computation.7 | async-start | bytes 10616832 | tf_op jit(solution)/shard_map/unit_gather/all_gather | solution.py:330
  26.3 29.3 %copy-start.44 = (s32[1,2048]{1,0:T(1,128)S(1)}, s32[1,2048]{1,0:T(1,128)}, u32[]{:S(2)}) copy-start(s32[1,2048]{1,0:T(1,128)} %param.16) | copy-start | bytes 24580
  26.3 29.3 %copy-start.45 = (s32[1,2048]{1,0:T(1,128)S(1)}, s32[1,2048]{1,0:T(1,128)}, u32[]{:S(2)}) copy-start(s32[1,2048]{1,0:T(1,128)} %param.17) | copy-start | bytes 24580
  53.7 10.8 %copy-start.5 = (bf16[8,256,640]{2,1,0:T(8,128)(2,1)}, bf16[8,256,640]{2,1,0:T(8,128)(2,1)S(1)}, u32[]{:S(2)}) copy-start(bf16[8,256,640]{2,1,0:T(8,128)(2,1)S(1)} %all-to-all-done) | copy-start | bytes 7864324
  55.5 194.5 %reduce-scatter.4.cloned.1.call-start = ((), (), s32[]{:S(2)}) async-start(), calls=%async_computation.8 | async-start | bytes 3538944 | tf_op jit(solution)/shard_map/down_rows/reduce_scatter | solution.py:436
  56.7 30.5 %copy-start.9 = (f32[512,64]{1,0:T(8,128)}, f32[512,64]{1,0:T(8,128)S(1)}, u32[]{:S(2)}) copy-start(f32[512,64]{1,0:T(8,128)S(1)} %get-tuple-element.124) | copy-start | bytes 393220
  56.7 30.5 %copy-start.11 = (f32[512,64]{1,0:T(8,128)}, f32[512,64]{1,0:T(8,128)S(1)}, u32[]{:S(2)}) copy-start(f32[512,64]{1,0:T(8,128)S(1)} %get-tuple-element.123) | copy-start | bytes 393220
  58.0 7.9 %collective-permute-start.1 = (bf16[2048,384]{1,0:T(8,128)(2,1)}, bf16[2048,384]{1,0:T(8,128)(2,1)}, u32[]{:S(2)}, u32[]{:S(2)}) collective-permute-start(bf16[2048,384]{1,0:T(8,128)(2,1)} %slice.344), channel_id=1, source_target_pairs={{0,1},{1,0},{2,3},{3,2},{4,5},{5,4},{6,7},{7,6},{8,9},{9,8},{10,11... | collective-permute-start | bytes 4718600 | tf_op jit(solution)/shard_map/swap/ppermute | solution.py:40
  70.2 15.2 %collective-permute-start.2 = (bf16[512,256]{1,0:T(8,128)(2,1)S(1)}, bf16[512,256]{1,0:T(8,128)(2,1)S(1)}, u32[]{:S(2)}, u32[]{:S(2)}) collective-permute-start(bf16[512,256]{1,0:T(8,128)(2,1)S(1)} %pad_maximum_fusion.24), channel_id=1, source_target_pairs={{0,8},{8,0},{1,9},{9,1},{2,10},{10,2},{3,11},{11,3},{4,12},{12,4},... | collective-permute-start | bytes 786440 | tf_op jit(solution)/shard_map/ppermute | solution.py:44
  75.5 26.1 %collective-permute-start.4 = (bf16[2048,256]{1,0:T(8,128)(2,1)}, bf16[2048,256]{1,0:T(8,128)(2,1)}, u32[]{:S(2)}, u32[]{:S(2)}) collective-permute-start(bf16[2048,256]{1,0:T(8,128)(2,1)} %slice.365), channel_id=1, source_target_pairs={{0,1},{1,0},{2,3},{3,2},{4,5},{5,4},{6,7},{7,6},{8,9},{9,8},{10,11... | collective-permute-start | bytes 3145736 | tf_op jit(solution)/shard_map/swap/ppermute | solution.py:40
  85.5 3.0 collective-permute-start.3
  106.2 30.2 %copy-start.41 = (f32[2048]{0:T(1024)S(1)}, f32[2048]{0:T(1024)}, u32[]{:S(2)}) copy-start(f32[2048]{0:T(1024)} %param.20) | copy-start | bytes 24580
  106.2 15.0 %collective-permute-start.5 = (bf16[128,2048]{1,0:T(8,128)(2,1)}, bf16[128,2048]{1,0:T(8,128)(2,1)}, u32[]{:S(2)}, u32[]{:S(2)}) collective-permute-start(bf16[128,2048]{1,0:T(8,128)(2,1)} %get-tuple-element.72), channel_id=1, source_target_pairs={{0,4},{2,6},{4,0},{6,2},{1,5},{3,7},{5,1},{7,3},{8,12},{10,14},{12... | collective-permute-start | bytes 1572872 | tf_op jit(solution)/shard_map/attn_scatter/ppermute | solution.py:54
  107.8 25.3 %collective-permute-start.6 = (bf16[128,2048]{1,0:T(8,128)(2,1)}, bf16[128,2048]{1,0:T(8,128)(2,1)}, u32[]{:S(2)}, u32[]{:S(2)}) collective-permute-start(bf16[128,2048]{1,0:T(8,128)(2,1)} %get-tuple-element.74), channel_id=1, source_target_pairs={{0,2},{2,4},{4,6},{6,0},{1,3},{3,5},{5,7},{7,1},{8,10},{10,12},{12... | collective-permute-start | bytes 1572872 | tf_op jit(solution)/shard_map/attn_scatter/ppermute | solution.py:54
  108.0 25.1 %collective-permute-start.7 = (bf16[128,2048]{1,0:T(8,128)(2,1)}, bf16[128,2048]{1,0:T(8,128)(2,1)}, u32[]{:S(2)}, u32[]{:S(2)}) collective-permute-start(bf16[128,2048]{1,0:T(8,128)(2,1)} %get-tuple-element.73), channel_id=1, source_target_pairs={{0,6},{2,0},{4,2},{6,4},{1,7},{3,1},{5,3},{7,5},{8,14},{10,8},{12,... | collective-permute-start | bytes 1572872 | tf_op jit(solution)/shard_map/attn_scatter/ppermute | solution.py:54
  137.3 14.7 %collective-permute-start.10 = (bf16[128,2048]{1,0:T(8,128)(2,1)}, bf16[128,2048]{1,0:T(8,128)(2,1)}, u32[]{:S(2)}, u32[]{:S(2)}) collective-permute-start(bf16[128,2048]{1,0:T(8,128)(2,1)} %multiply_convert_fusion.9), channel_id=1, source_target_pairs={{0,2},{2,4},{4,6},{6,0},{1,3},{3,5},{5,7},{7,1},{8,10},{10,12},{12... | collective-permute-start | bytes 1572872 | tf_op jit(solution)/shard_map/ffn_gather/ppermute | solution.py:54
  137.5 14.5 %collective-permute-start.8 = (bf16[128,2048]{1,0:T(8,128)(2,1)}, bf16[128,2048]{1,0:T(8,128)(2,1)}, u32[]{:S(2)}, u32[]{:S(2)}) collective-permute-start(bf16[128,2048]{1,0:T(8,128)(2,1)} %multiply_convert_fusion.9), channel_id=1, source_target_pairs={{0,6},{2,0},{4,2},{6,4},{1,7},{3,1},{5,3},{7,5},{8,14},{10,8},{12,... | collective-permute-start | bytes 1572872 | tf_op jit(solution)/shard_map/ffn_gather/ppermute | solution.py:54
  140.0 22.9 %collective-permute-start.9 = (bf16[128,2048]{1,0:T(8,128)(2,1)}, bf16[128,2048]{1,0:T(8,128)(2,1)}, u32[]{:S(2)}, u32[]{:S(2)}) collective-permute-start(bf16[128,2048]{1,0:T(8,128)(2,1)} %multiply_convert_fusion.9), channel_id=1, source_target_pairs={{0,4},{2,6},{4,0},{6,2},{1,5},{3,7},{5,1},{7,3},{8,12},{10,14},{12... | collective-permute-start | bytes 1572872 | tf_op jit(solution)/shard_map/ffn_gather/ppermute | solution.py:54
  169.3 16.7 %collective-permute-start.11 = (bf16[2048,2304]{1,0:T(8,128)(2,1)}, bf16[2048,2304]{1,0:T(8,128)(2,1)S(1)}, u32[]{:S(2)}, u32[]{:S(2)}) collective-permute-start(bf16[2048,2304]{1,0:T(8,128)(2,1)} %constant_dynamic-update-slice_fusion.10), channel_id=1, source_target_pairs={{0,1},{1,0},{2,3},{3,2},{4,5},{5,4},{6,7},{7,6},{8,9},{9,8},{10,11... | collective-permute-start | bytes 28311560 | tf_op jit(solution)/shard_map/swap/ppermute | solution.py:40
  184.8 16.1 %copy-start.50 = (bf16[512,768]{1,0:T(8,128)(2,1)}, bf16[512,768]{1,0:T(8,128)(2,1)S(1)}, u32[]{:S(2)}) copy-start(bf16[512,768]{1,0:T(8,128)(2,1)S(1)} %get-tuple-element.59) | copy-start | bytes 2359300
  195.0 5.9 %collective-permute-start.15 = (bf16[2048,768]{1,0:T(8,128)(2,1)S(1)}, bf16[2048,768]{1,0:T(8,128)(2,1)S(1)}, u32[]{:S(2)}, u32[]{:S(2)}) collective-permute-start(bf16[2048,768]{1,0:T(8,128)(2,1)S(1)} %convolution_convert_fusion.1), channel_id=1, source_target_pairs={{0,1},{1,0},{2,3},{3,2},{4,5},{5,4},{6,7},{7,6},{8,9},{9,8},{10,11... | collective-permute-start | bytes 9437192 | tf_op jit(solution)/shard_map/swap/ppermute | solution.py:40
  204.6 81.0 %all-gather.10.cloned.1.call-start = ((), (), s32[]{:S(2)}) async-start(), calls=%async_computation.9 | async-start | bytes 2621440 | tf_op jit(solution)/shard_map/d_attn_gather/all_gather | solution.py:79
  212.6 26.9 %copy-start.3 = (f32[128,2048]{1,0:T(8,128)S(1)}, f32[128,2048]{1,0:T(8,128)}, u32[]{:S(2)}) copy-start(f32[128,2048]{1,0:T(8,128)} %copy-done.2) | copy-start | bytes 3145732
  212.7 14.9 %collective-permute-start.12 = (bf16[128,2048]{1,0:T(8,128)(2,1)S(1)}, bf16[128,2048]{1,0:T(8,128)(2,1)S(1)}, u32[]{:S(2)}, u32[]{:S(2)}) collective-permute-start(bf16[128,2048]{1,0:T(8,128)(2,1)S(1)} %get-tuple-element.65), channel_id=1, source_target_pairs={{0,4},{2,6},{4,0},{6,2},{1,5},{3,7},{5,1},{7,3},{8,12},{10,14},{12... | collective-permute-start | bytes 1572872 | tf_op jit(solution)/shard_map/d_ffn_scatter/ppermute | solution.py:54
  213.7 25.8 %collective-permute-start.13 = (bf16[128,2048]{1,0:T(8,128)(2,1)S(1)}, bf16[128,2048]{1,0:T(8,128)(2,1)S(1)}, u32[]{:S(2)}, u32[]{:S(2)}) collective-permute-start(bf16[128,2048]{1,0:T(8,128)(2,1)S(1)} %get-tuple-element.67), channel_id=1, source_target_pairs={{0,2},{2,4},{4,6},{6,0},{1,3},{3,5},{5,7},{7,1},{8,10},{10,12},{12... | collective-permute-start | bytes 1572872 | tf_op jit(solution)/shard_map/d_ffn_scatter/ppermute | solution.py:54
  216.0 25.2 %copy-start.16 = (bf16[512,2048]{1,0:T(8,128)(2,1)S(1)}, bf16[512,2048]{1,0:T(8,128)(2,1)}, u32[]{:S(2)}) copy-start(bf16[512,2048]{1,0:T(8,128)(2,1)} %copy.128) | copy-start | bytes 6291460
  216.0 26.0 %copy-start.53 = (bf16[512,768]{1,0:T(8,128)(2,1)S(1)}, bf16[512,768]{1,0:T(8,128)(2,1)}, u32[]{:S(2)}) copy-start(bf16[512,768]{1,0:T(8,128)(2,1)} %get-tuple-element.52) | copy-start | bytes 2359300
  216.0 26.0 %copy-start.54 = (bf16[512,768]{1,0:T(8,128)(2,1)S(1)}, bf16[512,768]{1,0:T(8,128)(2,1)}, u32[]{:S(2)}) copy-start(bf16[512,768]{1,0:T(8,128)(2,1)} %get-tuple-element.53) | copy-start | bytes 2359300
  216.0 23.4 %collective-permute-start.14 = (bf16[128,2048]{1,0:T(8,128)(2,1)S(1)}, bf16[128,2048]{1,0:T(8,128)(2,1)S(1)}, u32[]{:S(2)}, u32[]{:S(2)}) collective-permute-start(bf16[128,2048]{1,0:T(8,128)(2,1)S(1)} %get-tuple-element.66), channel_id=1, source_target_pairs={{0,6},{2,0},{4,2},{6,4},{1,7},{3,1},{5,3},{7,5},{8,14},{10,8},{12,... | collective-permute-start | bytes 1572872 | tf_op jit(solution)/shard_map/d_ffn_scatter/ppermute | solution.py:54
  242.0 6.4 %copy-start.31 = (bf16[1,256,2048]{2,1,0:T(8,128)(2,1)S(1)}, bf16[1,256,2048]{2,1,0:T(8,128)(2,1)}, u32[]{:S(2)}) copy-start(bf16[1,256,2048]{2,1,0:T(8,128)(2,1)} %param.15) | copy-start | bytes 3145732
  247.7 10.8 %collective-permute-start.25 = (bf16[2048,1536]{1,0:T(8,128)(2,1)}, bf16[2048,1536]{1,0:T(8,128)(2,1)}, u32[]{:S(2)}, u32[]{:S(2)}) collective-permute-start(bf16[2048,1536]{1,0:T(8,128)(2,1)} %convolution_convert_fusion), channel_id=1, source_target_pairs={{0,1},{1,0},{2,3},{3,2},{4,5},{5,4},{6,7},{7,6},{8,9},{9,8},{10,11... | collective-permute-start | bytes 18874376 | tf_op jit(solution)/shard_map/swap/ppermute | solution.py:40
  253.1 111.9 %reduce-scatter.8.cloned.1.call-start = ((), (), s32[]{:S(2)}) async-start(), calls=%async_computation.11 | async-start | bytes 7077888 | tf_op jit(solution)/shard_map/gate_up_rows/reduce_scatter | solution.py:436
  253.2 15.3 %copy-start.40 = (bf16[256,768]{1,0:T(8,128)(2,1)S(1)}, bf16[256,768]{1,0:T(8,128)(2,1)}, u32[]{:S(2)}) copy-start(bf16[256,768]{1,0:T(8,128)(2,1)} %reduce-scatter.4.cloned.1.call-done) | copy-start | bytes 1179652
  253.2 15.3 %collective-permute-start.26 = (bf16[256,768]{1,0:T(8,128)(2,1)}, bf16[256,768]{1,0:T(8,128)(2,1)S(1)}, u32[]{:S(2)}, u32[]{:S(2)}) collective-permute-start(bf16[256,768]{1,0:T(8,128)(2,1)} %reduce-scatter.4.cloned.1.call-done), channel_id=1, source_target_pairs={{0,8},{8,0},{1,9},{9,1},{2,10},{10,2},{3,11},{11,3},{4,12},{12,4},... | collective-permute-start | bytes 1179656 | tf_op jit(solution)/shard_map/down_y/ppermute | solution.py:44
  288.7 154.8 %reduce-scatter.6.cloned.1.call-start = ((), (), s32[]{:S(2)}) async-start(), calls=%async_computation.10 | async-start | bytes 2621440 | tf_op jit(solution)/shard_map/d_attn_scatter/reduce_scatter | solution.py:84
  298.9 6.5 %copy-start.6 = (bf16[8,256,640]{2,1,0:T(8,128)(2,1)S(1)}, bf16[8,256,640]{2,1,0:T(8,128)(2,1)}, u32[]{:S(2)}) copy-start(bf16[8,256,640]{2,1,0:T(8,128)(2,1)} %copy-done.5) | copy-start | bytes 7864324
  298.9 23.3 %collective-permute-start.16 = (bf16[128,2048]{1,0:T(8,128)(2,1)}, bf16[128,2048]{1,0:T(8,128)(2,1)S(1)}, u32[]{:S(2)}, u32[]{:S(2)}) collective-permute-start(bf16[128,2048]{1,0:T(8,128)(2,1)} %get-tuple-element.62), channel_id=1, source_target_pairs={{0,4},{2,6},{4,0},{6,2},{1,5},{3,7},{5,1},{7,3},{8,12},{10,14},{12... | collective-permute-start | bytes 1572872 | tf_op jit(solution)/shard_map/branch_scatter/ppermute | solution.py:54
  300.4 25.4 %collective-permute-start.17 = (bf16[128,2048]{1,0:T(8,128)(2,1)S(1)}, bf16[128,2048]{1,0:T(8,128)(2,1)S(1)}, u32[]{:S(2)}, u32[]{:S(2)}) collective-permute-start(bf16[128,2048]{1,0:T(8,128)(2,1)S(1)} %get-tuple-element.64), channel_id=1, source_target_pairs={{0,2},{2,4},{4,6},{6,0},{1,3},{3,5},{5,7},{7,1},{8,10},{10,12},{12... | collective-permute-start | bytes 1572872 | tf_op jit(solution)/shard_map/branch_scatter/ppermute | solution.py:54
  300.4 25.4 %collective-permute-start.18 = (bf16[128,2048]{1,0:T(8,128)(2,1)S(1)}, bf16[128,2048]{1,0:T(8,128)(2,1)S(1)}, u32[]{:S(2)}, u32[]{:S(2)}) collective-permute-start(bf16[128,2048]{1,0:T(8,128)(2,1)S(1)} %get-tuple-element.63), channel_id=1, source_target_pairs={{0,6},{2,0},{4,2},{6,4},{1,7},{3,1},{5,3},{7,5},{8,14},{10,8},{12,... | collective-permute-start | bytes 1572872 | tf_op jit(solution)/shard_map/branch_scatter/ppermute | solution.py:54
  327.6 2.0 collective-permute-start.20
  329.7 15.7 %copy-start.10 = (f32[512,64]{1,0:T(8,128)S(1)}, f32[512,64]{1,0:T(8,128)}, u32[]{:S(2)}) copy-start(f32[512,64]{1,0:T(8,128)} %copy-done.9) | copy-start | bytes 393220
  329.8 15.6 %collective-permute-start.21 = (bf16[512,256]{1,0:T(8,128)(2,1)S(1)}, bf16[512,256]{1,0:T(8,128)(2,1)S(1)}, u32[]{:S(2)}, u32[]{:S(2)}) collective-permute-start(bf16[512,256]{1,0:T(8,128)(2,1)S(1)} %slice.540), channel_id=1, source_target_pairs={{0,8},{8,0},{1,9},{9,1},{2,10},{10,2},{3,11},{11,3},{4,12},{12,4},... | collective-permute-start | bytes 786440 | tf_op jit(solution)/shard_map/ppermute | solution.py:44
  332.6 13.1 %copy-start.12 = (f32[512,64]{1,0:T(8,128)S(1)}, f32[512,64]{1,0:T(8,128)}, u32[]{:S(2)}) copy-start(f32[512,64]{1,0:T(8,128)} %copy-done.11) | copy-start | bytes 393220
  332.6 14.7 %copy-start.34 = (bf16[512,256]{1,0:T(8,128)(2,1)}, bf16[512,256]{1,0:T(8,128)(2,1)S(1)}, u32[]{:S(2)}) copy-start(bf16[512,256]{1,0:T(8,128)(2,1)S(1)} %get-tuple-element.99) | copy-start | bytes 786436
  352.4 113.2 %all-gather.12.cloned.1.call-start = ((), (), s32[]{:S(2)}) async-start(), calls=%async_computation.12 | async-start | bytes 5898240 | tf_op jit(solution)/shard_map/unit_columns/all_gather | solution.py:480
  357.6 13.5 %collective-permute-start.23 = (bf16[2048,384]{1,0:T(8,128)(2,1)}, bf16[2048,384]{1,0:T(8,128)(2,1)}, u32[]{:S(2)}, u32[]{:S(2)}) collective-permute-start(bf16[2048,384]{1,0:T(8,128)(2,1)} %convolution_convert_fusion.2), channel_id=1, source_target_pairs={{0,1},{1,0},{2,3},{3,2},{4,5},{5,4},{6,7},{7,6},{8,9},{9,8},{10,11... | collective-permute-start | bytes 4718600 | tf_op jit(solution)/shard_map/swap/ppermute | solution.py:40
  360.3 7.2 %collective-permute-start.24 = (bf16[2048,256]{1,0:T(8,128)(2,1)}, bf16[2048,256]{1,0:T(8,128)(2,1)}, u32[]{:S(2)}, u32[]{:S(2)}) collective-permute-start(bf16[2048,256]{1,0:T(8,128)(2,1)} %convolution_convert_fusion.3), channel_id=1, source_target_pairs={{0,1},{1,0},{2,3},{3,2},{4,5},{5,4},{6,7},{7,6},{8,9},{9,8},{10,11... | collective-permute-start | bytes 3145736 | tf_op jit(solution)/shard_map/swap/ppermute | solution.py:40
  365.0 20.2 %collective-permute-start.27 = (bf16[256,1536]{1,0:T(8,128)(2,1)}, bf16[256,1536]{1,0:T(8,128)(2,1)S(1)}, u32[]{:S(2)}, u32[]{:S(2)}) collective-permute-start(bf16[256,1536]{1,0:T(8,128)(2,1)} %reduce-scatter.8.cloned.1.call-done), channel_id=1, source_target_pairs={{0,8},{8,0},{1,9},{9,1},{2,10},{10,2},{3,11},{11,3},{4,12},{12,4},... | collective-permute-start | bytes 2359304 | tf_op jit(solution)/shard_map/gate_up_y/ppermute | solution.py:44
  371.1 14.2 %copy-start.35 = (bf16[256,1536]{1,0:T(8,128)(2,1)S(1)}, bf16[256,1536]{1,0:T(8,128)(2,1)}, u32[]{:S(2)}) copy-start(bf16[256,1536]{1,0:T(8,128)(2,1)} %reduce-scatter.8.cloned.1.call-done) | copy-start | bytes 2359300
  373.9 11.3 %copy-start.27 = (bf16[2048,384]{1,0:T(8,128)(2,1)}, bf16[2048,384]{1,0:T(8,128)(2,1)S(1)}, u32[]{:S(2)}) copy-start(bf16[2048,384]{1,0:T(8,128)(2,1)S(1)} %add_convert_fusion.5) | copy-start | bytes 4718596
  373.9 11.5 %copy-start.26 = (bf16[256,768]{1,0:T(8,128)(2,1)S(1)}, bf16[256,768]{1,0:T(8,128)(2,1)}, u32[]{:S(2)}) copy-start(bf16[256,768]{1,0:T(8,128)(2,1)} %copy-done.25) | copy-start | bytes 1179652
  389.8 44.5 %all-to-all-start.1 = ((bf16[16,144,640]{2,1,0:T(8,128)(2,1)}), bf16[16,144,640]{2,1,0:T(8,128)(2,1)S(1)}, u32[]{:S(2)}, u32[]{:S(2)}) async-start(bf16[16,144,640]{2,1,0:T(8,128)(2,1)} %fusion.11), calls=%async_computation.3 | async-start | bytes 5898240 | tf_op jit(solution)/shard_map/attn_rows/all_to_all | solution.py:422
  396.3 3.6 collective-permute-start.19
  436.5 7.0 %copy-start.13 = (bf16[1,256,2048]{2,1,0:T(8,128)(2,1)S(1)}, bf16[1,256,2048]{2,1,0:T(8,128)(2,1)}, u32[]{:S(2)}) copy-start(bf16[1,256,2048]{2,1,0:T(8,128)(2,1)} %param.14) | copy-start | bytes 3145732
  436.5 7.0 %copy-start.43 = (f32[2048]{0:T(1024)S(1)}, f32[2048]{0:T(1024)}, u32[]{:S(2)}) copy-start(f32[2048]{0:T(1024)} %param.19) | copy-start | bytes 24580
  437.8 35.8 %all-to-all-start.2 = ((bf16[8,144,640]{2,1,0:T(8,128)(2,1)}), bf16[8,144,640]{2,1,0:T(8,128)(2,1)S(1)}, u32[]{:S(2)}, u32[]{:S(2)}) async-start(bf16[8,144,640]{2,1,0:T(8,128)(2,1)} %broadcast_in_dim.11), calls=%async_computation.5 | async-start | bytes 2949120 | tf_op jit(solution)/shard_map/attn_columns/all_to_all | solution.py:428
  443.5 7.1 %copy-start.18 = (bf16[128,2048]{1,0:T(8,128)(2,1)S(1)}, bf16[128,2048]{1,0:T(8,128)(2,1)}, u32[]{:S(2)}) copy-start(bf16[128,2048]{1,0:T(8,128)(2,1)} %get-tuple-element.88) | copy-start | bytes 1572868
  443.5 7.0 %copy-start.19 = (bf16[128,2048]{1,0:T(8,128)(2,1)S(1)}, bf16[128,2048]{1,0:T(8,128)(2,1)}, u32[]{:S(2)}) copy-start(bf16[128,2048]{1,0:T(8,128)(2,1)} %get-tuple-element.89) | copy-start | bytes 1572868
  447.7 27.4 %collective-permute-start.22 = (bf16[128,2048]{1,0:T(8,128)(2,1)}, bf16[128,2048]{1,0:T(8,128)(2,1)}, u32[]{:S(2)}, u32[]{:S(2)}) collective-permute-start(bf16[128,2048]{1,0:T(8,128)(2,1)} %fusion.25), channel_id=1, source_target_pairs={{0,1},{1,0},{2,3},{3,2},{4,5},{5,4},{6,7},{7,6},{8,9},{9,8},{10,11... | collective-permute-start | bytes 1572872 | tf_op jit(solution)/shard_map/swap/ppermute | solution.py:40
  473.9 4.3 collective-permute-start.29
  476.4 1.2 collective-permute-start.28
  (33 other events, 89.7 us)
Sparse Core Ops, SparseCore 0:
  10.6 49.5 all-gather.5
  61.8 105.2 all-gather.7
  204.7 41.8 reduce-scatter.3
  253.3 32.2 all-gather.9
  288.8 76.1 reduce-scatter.7
  367.9 30.6 reduce-scatter.5
  400.9 64.6 all-gather.11
